TPU v7x, 32 devices: a whole 2x2x4 slice. The times are simulated.
32 devices in a mesh: dp: 16 (over z, y, x), rep: 2 (over core).
Axes of the slice: x: 2, y: 2, z: 4, core: 2. Of those that a mesh axis runs over, the one named last changes fastest.
Arguments:
- media_tokens: bfloat16 [256, 576, 1024], P(('dp', 'rep')), may hold values from -6 to 6
- patch_counts: int32 [256], P(('dp', 'rep')), may hold values from 256 to 576, as said below
- latents: bfloat16 [256, 64, 1024], P(('dp', 'rep')), may hold values from -6 to 6
- media_gain: bfloat16 [1024], P('dp'), may hold values from 0.3984375 to 1.59375
- media_bias: bfloat16 [1024], P('dp'), may hold values from -3 to 3
- latent_gain: bfloat16 [1024], P('dp'), may hold values from 0.3984375 to 1.59375
- latent_bias: bfloat16 [1024], P('dp'), may hold values from -3 to 3
- query_weight: bfloat16 [1024, 512], P('dp'), may hold values from -0.1875 to 0.1875
- keyval_weight: bfloat16 [1024, 1024], P('dp'), may hold values from -0.1875 to 0.1875
- outproj_weight: bfloat16 [512, 1024], P('dp'), may hold values from -1.5 to 1.5
- ff_gain: bfloat16 [1024], P('dp'), may hold values from 0.3984375 to 1.59375
- ff_bias: bfloat16 [1024], P('dp'), may hold values from -3 to 3
- ff_in_weight: bfloat16 [1024, 4096], P('dp'), may hold values from -0.1875 to 0.1875
- ff_out_weight: bfloat16 [4096, 1024], P('dp'), may hold values from -0.09375 to 0.09375
- cotangent: float32 [256, 64, 1024], P(('dp', 'rep')), may hold values from -6 to 6
Outputs:
- new_latents: float32 [256, 64, 1024], P(('dp', 'rep'))
- media_grad: float32 [256, 576, 1024], P(('dp', 'rep'))
- latent_grad: float32 [256, 64, 1024], P(('dp', 'rep'))
- grad_media_gain: float32 [1024], P('dp')
- grad_media_bias: float32 [1024], P('dp')
- grad_latent_gain: float32 [1024], P('dp')
- grad_latent_bias: float32 [1024], P('dp')
- grad_query: float32 [1024, 512], P('dp')
- grad_keyval: float32 [1024, 1024], P('dp')
- grad_outproj: float32 [512, 1024], P('dp')
- grad_ff_gain: float32 [1024], P('dp')
- grad_ff_bias: float32 [1024], P('dp')
- grad_ff_in: float32 [1024, 4096], P('dp')
- grad_ff_out: float32 [4096, 1024], P('dp')
Inputs may be any that keep to these rules, and one draw needn't show every extreme that they name: `patch_counts`: each entry is 256 or 576; some device holds only 576-patch images and some only 256-patch ones.
All inputs are finite; a program needn't handle non-finite values.
Results may differ from a plain program's by a relative error of at most 0.02.
Values may be sent and summed in bfloat16 or wider, within the bound.
No kernel may reach another device: no remote copies, remote signals or barrier semaphores. Data moves between devices by JAX's collectives and lax.ppermute only.
A program may use at most 256 MiB of HBM per device.

v0:
```python
import math

import jax
import jax.numpy as jnp
from jax import lax
from jax.sharding import PartitionSpec as P

HEADS = 8


EPS = 1e-05


def norm_apply(values, gain, bias):
    centre = jnp.mean(values, -1, keepdims=True)
    centred = values - centre
    inverse = lax.rsqrt(jnp.mean(centred * centred, -1, keepdims=True) + EPS)
    unit = centred * inverse
    return (unit * gain.astype(jnp.float32) + bias.astype(jnp.float32), unit, inverse)


def norm_grad(grad_normed, unit, inverse, gain):
    scaled = grad_normed * gain.astype(jnp.float32)
    return inverse * (
        scaled
        - jnp.mean(scaled, -1, keepdims=True)
        - unit * jnp.mean(scaled * unit, -1, keepdims=True)
    )


def row_total(values):
    return jnp.sum(values.reshape(-1, values.shape[-1]), axis=0)


def gelu_exact(values):
    return jax.nn.gelu(values, approximate=False)


def masked_scores(query_heads, key_heads, valid, scale):
    raw = (
        jnp.einsum("iqhe,ikhe->ihqk", query_heads, key_heads, preferred_element_type=jnp.float32)
        * scale
    )
    return jnp.where(valid[:, None, None, :], raw, jnp.float32(-1e30))


def shards(
    media_tokens,
    patch_counts,
    latents,
    media_gain,
    media_bias,
    latent_gain,
    latent_bias,
    query_weight,
    keyval_weight,
    outproj_weight,
    ff_gain,
    ff_bias,
    ff_in_weight,
    ff_out_weight,
    cotangent,
):
    f32 = jnp.float32
    bf16 = jnp.bfloat16
    whole = (
        lax.all_gather(media_gain, "dp", axis=0, tiled=True),
        lax.all_gather(media_bias, "dp", axis=0, tiled=True),
        lax.all_gather(latent_gain, "dp", axis=0, tiled=True),
        lax.all_gather(latent_bias, "dp", axis=0, tiled=True),
        lax.all_gather(query_weight, "dp", axis=0, tiled=True),
        lax.all_gather(keyval_weight, "dp", axis=0, tiled=True),
        lax.all_gather(outproj_weight, "dp", axis=0, tiled=True),
        lax.all_gather(ff_gain, "dp", axis=0, tiled=True),
        lax.all_gather(ff_bias, "dp", axis=0, tiled=True),
        lax.all_gather(ff_in_weight, "dp", axis=0, tiled=True),
        lax.all_gather(ff_out_weight, "dp", axis=0, tiled=True),
    )
    (
        gain_media,
        bias_media,
        gain_latent,
        bias_latent,
        w_query,
        w_keyval,
        w_outproj,
        gain_ff,
        bias_ff,
        w_ffin,
        w_ffout,
    ) = whole
    images, media_len, width = media_tokens.shape
    lat_len = latents.shape[1]
    keys_len = media_len + lat_len
    inner_width = w_query.shape[1]
    head_size = inner_width // HEADS
    scale = 1.0 / math.sqrt(head_size)
    media_f = media_tokens.astype(f32)
    latent_f = latents.astype(f32)
    media_normed, media_unit, media_inv = norm_apply(media_f, gain_media, bias_media)
    latent_normed, latent_unit, latent_inv = norm_apply(latent_f, gain_latent, bias_latent)
    media_low = media_normed.astype(bf16)
    latent_low = latent_normed.astype(bf16)
    queries = jnp.einsum("ild,de->ile", latent_low, w_query, preferred_element_type=f32).astype(
        bf16
    )
    key_input = jnp.concatenate([media_low, latent_low], axis=1)
    keyvals = jnp.einsum("ikd,de->ike", key_input, w_keyval, preferred_element_type=f32).astype(
        bf16
    )
    key_heads = keyvals[:, :, :inner_width].reshape(images, keys_len, HEADS, head_size)
    value_heads = keyvals[:, :, inner_width:].reshape(images, keys_len, HEADS, head_size)
    query_heads = queries.reshape(images, lat_len, HEADS, head_size)
    positions = jnp.arange(keys_len, dtype=jnp.int32)
    valid = (positions[None, :] < patch_counts[:, None]) | (positions[None, :] >= media_len)
    scores = masked_scores(query_heads, key_heads, valid, scale)
    top = jnp.max(scores, -1, keepdims=True)
    expd = jnp.exp(scores - top)
    total = jnp.sum(expd, -1, keepdims=True)
    probs = expd / total
    log_total = top + jnp.log(total)
    mixed = jnp.einsum(
        "ihqk,ikhe->iqhe", probs.astype(bf16), value_heads, preferred_element_type=f32
    )
    mixed = mixed.reshape(images, lat_len, inner_width).astype(bf16)
    branch = jnp.einsum("ile,ed->ild", mixed, w_outproj, preferred_element_type=f32)
    resid = latent_f + branch
    ff_normed, ff_unit, ff_inv = norm_apply(resid, gain_ff, bias_ff)
    ff_low = ff_normed.astype(bf16)
    pre_act = jnp.einsum("ild,df->ilf", ff_low, w_ffin, preferred_element_type=f32)
    activ, gelu_pull = jax.vjp(gelu_exact, pre_act)
    activ_low = activ.astype(bf16)
    new_latents = resid + jnp.einsum("ilf,fd->ild", activ_low, w_ffout, preferred_element_type=f32)
    again = (
        lax.all_gather(media_gain, "dp", axis=0, tiled=True),
        lax.all_gather(media_bias, "dp", axis=0, tiled=True),
        lax.all_gather(latent_gain, "dp", axis=0, tiled=True),
        lax.all_gather(latent_bias, "dp", axis=0, tiled=True),
        lax.all_gather(query_weight, "dp", axis=0, tiled=True),
        lax.all_gather(keyval_weight, "dp", axis=0, tiled=True),
        lax.all_gather(outproj_weight, "dp", axis=0, tiled=True),
        lax.all_gather(ff_gain, "dp", axis=0, tiled=True),
        lax.all_gather(ff_bias, "dp", axis=0, tiled=True),
        lax.all_gather(ff_in_weight, "dp", axis=0, tiled=True),
        lax.all_gather(ff_out_weight, "dp", axis=0, tiled=True),
    )
    (
        gain_media_b,
        bias_media_b,
        gain_latent_b,
        bias_latent_b,
        w_query_b,
        w_keyval_b,
        w_outproj_b,
        gain_ff_b,
        bias_ff_b,
        w_ffin_b,
        w_ffout_b,
    ) = again
    grad_out_low = cotangent.astype(bf16)
    grad_ffout = jnp.einsum("ilf,ild->fd", activ_low, grad_out_low, preferred_element_type=f32)
    grad_activ = jnp.einsum("ild,fd->ilf", grad_out_low, w_ffout_b, preferred_element_type=f32)
    (grad_pre,) = gelu_pull(grad_activ)
    grad_pre_low = grad_pre.astype(bf16)
    grad_ffin = jnp.einsum("ild,ilf->df", ff_low, grad_pre_low, preferred_element_type=f32)
    grad_ffnormed = jnp.einsum("ilf,df->ild", grad_pre_low, w_ffin_b, preferred_element_type=f32)
    grad_gain_ff = row_total(grad_ffnormed * ff_unit)
    grad_bias_ff = row_total(grad_ffnormed)
    grad_resid = cotangent + norm_grad(grad_ffnormed, ff_unit, ff_inv, gain_ff_b)
    grad_resid_low = grad_resid.astype(bf16)
    grad_outproj = jnp.einsum("ile,ild->ed", mixed, grad_resid_low, preferred_element_type=f32)
    grad_mixed = jnp.einsum(
        "ild,ed->ile", grad_resid_low, w_outproj_b, preferred_element_type=f32
    ).astype(bf16)
    grad_mixed_heads = grad_mixed.reshape(images, lat_len, HEADS, head_size)
    scores_again = masked_scores(query_heads, key_heads, valid, scale)
    probs_again = jnp.exp(scores_again - log_total)
    grad_probs = jnp.einsum(
        "iqhe,ikhe->ihqk", grad_mixed_heads, value_heads, preferred_element_type=f32
    )
    grad_scores = probs_again * (grad_probs - jnp.sum(probs_again * grad_probs, -1, keepdims=True))
    grad_scores_low = grad_scores.astype(bf16)
    grad_queries = (
        jnp.einsum("ihqk,ikhe->iqhe", grad_scores_low, key_heads, preferred_element_type=f32)
        * scale
    )
    grad_queries = grad_queries.reshape(images, lat_len, inner_width).astype(bf16)
    grad_keys = (
        jnp.einsum("ihqk,iqhe->ikhe", grad_scores_low, query_heads, preferred_element_type=f32)
        * scale
    )
    grad_values = jnp.einsum(
        "ihqk,iqhe->ikhe", probs_again.astype(bf16), grad_mixed_heads, preferred_element_type=f32
    )
    grad_keyvals = jnp.concatenate(
        [
            grad_keys.reshape(images, keys_len, inner_width),
            grad_values.reshape(images, keys_len, inner_width),
        ],
        axis=-1,
    ).astype(bf16)
    grad_qweight = jnp.einsum("ild,ile->de", latent_low, grad_queries, preferred_element_type=f32)
    grad_kvweight = jnp.einsum("ikd,ike->de", key_input, grad_keyvals, preferred_element_type=f32)
    grad_key_input = jnp.einsum("ike,de->ikd", grad_keyvals, w_keyval_b, preferred_element_type=f32)
    grad_latnormed = jnp.einsum("ile,de->ild", grad_queries, w_query_b, preferred_element_type=f32)
    grad_latnormed = grad_latnormed + grad_key_input[:, media_len:]
    grad_medianormed = grad_key_input[:, :media_len]
    media_grad = norm_grad(grad_medianormed, media_unit, media_inv, gain_media_b)
    latent_grad = grad_resid + norm_grad(grad_latnormed, latent_unit, latent_inv, gain_latent_b)
    grad_gain_media = row_total(grad_medianormed * media_unit)
    grad_bias_media = row_total(grad_medianormed)
    grad_gain_latent = row_total(grad_latnormed * latent_unit)
    grad_bias_latent = row_total(grad_latnormed)
    owned = (
        lax.psum_scatter(
            grad_gain_media.astype(jnp.bfloat16), "dp", scatter_dimension=0, tiled=True
        ).astype(jnp.float32),
        lax.psum_scatter(
            grad_bias_media.astype(jnp.bfloat16), "dp", scatter_dimension=0, tiled=True
        ).astype(jnp.float32),
        lax.psum_scatter(
            grad_gain_latent.astype(jnp.bfloat16), "dp", scatter_dimension=0, tiled=True
        ).astype(jnp.float32),
        lax.psum_scatter(
            grad_bias_latent.astype(jnp.bfloat16), "dp", scatter_dimension=0, tiled=True
        ).astype(jnp.float32),
        lax.psum_scatter(
            grad_qweight.astype(jnp.bfloat16), "dp", scatter_dimension=0, tiled=True
        ).astype(jnp.float32),
        lax.psum_scatter(
            grad_kvweight.astype(jnp.bfloat16), "dp", scatter_dimension=0, tiled=True
        ).astype(jnp.float32),
        lax.psum_scatter(
            grad_outproj.astype(jnp.bfloat16), "dp", scatter_dimension=0, tiled=True
        ).astype(jnp.float32),
        lax.psum_scatter(
            grad_gain_ff.astype(jnp.bfloat16), "dp", scatter_dimension=0, tiled=True
        ).astype(jnp.float32),
        lax.psum_scatter(
            grad_bias_ff.astype(jnp.bfloat16), "dp", scatter_dimension=0, tiled=True
        ).astype(jnp.float32),
        lax.psum_scatter(
            grad_ffin.astype(jnp.bfloat16), "dp", scatter_dimension=0, tiled=True
        ).astype(jnp.float32),
        lax.psum_scatter(
            grad_ffout.astype(jnp.bfloat16), "dp", scatter_dimension=0, tiled=True
        ).astype(jnp.float32),
    )
    summed = (
        lax.psum(owned[0].astype(jnp.bfloat16), "rep").astype(jnp.float32),
        lax.psum(owned[1].astype(jnp.bfloat16), "rep").astype(jnp.float32),
        lax.psum(owned[2].astype(jnp.bfloat16), "rep").astype(jnp.float32),
        lax.psum(owned[3].astype(jnp.bfloat16), "rep").astype(jnp.float32),
        lax.psum(owned[4].astype(jnp.bfloat16), "rep").astype(jnp.float32),
        lax.psum(owned[5].astype(jnp.bfloat16), "rep").astype(jnp.float32),
        lax.psum(owned[6].astype(jnp.bfloat16), "rep").astype(jnp.float32),
        lax.psum(owned[7].astype(jnp.bfloat16), "rep").astype(jnp.float32),
        lax.psum(owned[8].astype(jnp.bfloat16), "rep").astype(jnp.float32),
        lax.psum(owned[9].astype(jnp.bfloat16), "rep").astype(jnp.float32),
        lax.psum(owned[10].astype(jnp.bfloat16), "rep").astype(jnp.float32),
    )
    (
        sum_gain_media,
        sum_bias_media,
        sum_gain_latent,
        sum_bias_latent,
        sum_query,
        sum_keyval,
        sum_outproj,
        sum_gain_ff,
        sum_bias_ff,
        sum_ffin,
        sum_ffout,
    ) = summed
    return (
        new_latents,
        media_grad,
        latent_grad,
        sum_gain_media,
        sum_bias_media,
        sum_gain_latent,
        sum_bias_latent,
        sum_query,
        sum_keyval,
        sum_outproj,
        sum_gain_ff,
        sum_bias_ff,
        sum_ffin,
        sum_ffout,
    )


def solution(mesh):
    return jax.shard_map(
        shards,
        mesh=mesh,
        in_specs=(
            P(("dp", "rep"), None, None),
            P(("dp", "rep")),
            P(("dp", "rep"), None, None),
            P("dp"),
            P("dp"),
            P("dp"),
            P("dp"),
            P("dp", None),
            P("dp", None),
            P("dp", None),
            P("dp"),
            P("dp"),
            P("dp", None),
            P("dp", None),
            P(("dp", "rep"), None, None),
        ),
        out_specs=(
            P(("dp", "rep"), None, None),
            P(("dp", "rep"), None, None),
            P(("dp", "rep"), None, None),
            P("dp"),
            P("dp"),
            P("dp"),
            P("dp"),
            P("dp", None),
            P("dp", None),
            P("dp", None),
            P("dp"),
            P("dp"),
            P("dp", None),
            P("dp", None),
        ),
        check_vma=False,
    )
```

profile of v0, /device:TPU:0, one launch (start us, length us, event | category | flops | bytes accessed | tf_op | source)
XLA Modules:
  0.0 1149.2 jit_solution(8845610947740791758)
XLA Ops:
  10.6 1.3 fusion.84
  12.6 0.8 dynamic-update-slice.5
  17.7 78.7 %all-reduce.13 = (bf16[1024]{0:T(1024)(128)(2,1)S(1)}, bf16[1024]{0:T(1024)(128)(2,1)S(1)}, bf16[1024]{0:T(1024)(128)(2,1)S(1)}, bf16[1024]{0:T(1024)(128)(2,1)S...) all-reduce(bf16[1024]{0:T(1024)(128)(2,1)S(1)} %dynamic-update-slic, ...), channel_id=1, replica_groups=mesh['dp'=16,'rep'=2] {'dp'}, use_global_device_ids=true, to_apply=%add.3 | all-reduce | flops 6144 | bytes 24576
  96.4 1.6 convert_reduce_fusion.1
  98.0 2.0 fusion.57
  100.0 5.1 convert_reduce_fusion
  105.1 2.7 fusion.12
  108.5 6.1 fusion.7
  114.6 2.7 convolution_convert_fusion.1
  117.3 1.5 copy.75
  118.8 12.7 %all-gather.6.cloned.1.call-done = bf16[1024,1024]{1,0:T(8,128)(2,1)} async-done(((bf16[64,1024]{1,0:T(8,128)(2,1)}), bf16[1024,1024]{1,0:T(8,128)(2,1)}) %all-gather.6.cloned.1.call-update) | async-done | bytes 2097168 | tf_op jit(solution)/shard_map/all_gather | solution.py:72
  131.5 16.9 %fusion.33 = bf16[8,640,1024]{2,1,0:T(8,128)(2,1)} fusion(bf16[8,64,1024]{2,1,0:T(8,128)(2,1)S(1)} %fusion.51, bf16[8,576,1024]{2,1,0:T(8,128)(2,1)} %fusion.7, bf16[1024,1024]{1,0:T(8,128)(2,1)} %all-gather.6.cloned.1.call-done), kind=kOutput, calls=%fused_computation.63 | convolution fusion | flops 10763632640 | bytes 23068672 | tf_op jit(solution)/shard_map/ikd,de->ike/dot_general | solution.py:108
  148.3 8.8 fusion.83
  157.2 7.8 copy.58
  165.0 7.9 copy.57
  172.9 4.6 fusion.40
  177.5 2.7 fusion.14
  180.2 2.6 copy-done
  182.8 1.0 slice-done.7
  183.8 3.9 fusion.65
  188.2 2.0 fusion.85
  190.3 1.3 copy-done.8
  192.0 110.5 %all-gather.12.cloned.1.call-done = bf16[1024,4096]{1,0:T(8,128)(2,1)} async-done(((bf16[64,4096]{1,0:T(8,128)(2,1)}), bf16[1024,4096]{1,0:T(8,128)(2,1)}) %all-gather.12.cloned.1.call-update) | async-done | bytes 8388624 | tf_op jit(solution)/shard_map/all_gather | solution.py:76
  302.5 10.4 fusion.61
  313.0 3.2 copy-done.12
  316.2 19.7 %multiply_convert_fusion.2 = (bf16[8,64,4096]{2,1,0:T(8,128)(2,1)}, f32[8,64,4096]{2,1,0:T(8,128)}) fusion(f32[8,64,4096]{2,1,0:T(8,128)S(1)} %get-tuple-element.61, u8[64,4096]{1,0:T(8,128)(4,1)S(1)} %get-tuple-element.19, u8[64,4096]{1,0:T(8,128)(4,1)S(1)} %get-tuple-element.18), kind=kLoop, calls=%fused_computation.46 | loop fusion | flops 146800640 | bytes 21495808 | tf_op jit(solution)/shard_map/convert_element_type | solution.py:132
  335.9 80.3 %all-gather.14.cloned.1.call-done = bf16[4096,1024]{1,0:T(8,128)(2,1)} async-done(((bf16[256,1024]{1,0:T(8,128)(2,1)}), bf16[4096,1024]{1,0:T(8,128)(2,1)}) %all-gather.14.cloned.1.call-update) | async-done | bytes 8388624 | tf_op jit(solution)/shard_map/all_gather | solution.py:77
  416.2 14.5 %add_convert_fusion = bf16[8,64,4096]{2,1,0:T(8,128)(2,1)} fusion(f32[8,64,4096]{2,1,0:T(8,128)} %get-tuple-element.52, f32[8,64,4096]{2,1,0:T(8,128)} %copy-done.12, bf16[4096,1024]{1,0:T(8,128)(2,1)} %all-gather.14.cloned.1.call-done, f32[8,64,1024]{2,1,0:T(8,128)S(1)} %copy-done.13), kind=kOutput, calls=%fused_computation.45 | convolution fusion | flops 4324851712 | bytes 31457280 | tf_op jit(solution)/shard_map/ild,fd->ilf/dot_general | solution.py:162
  430.7 9.0 multiply_reduce_fusion.1
  440.5 1.3 copy-done.6
  441.8 1.8 bitcast_convert_fusion.3
  443.7 3.5 convolution_convert_fusion
  447.2 2.4 copy.76
  449.6 13.7 %multiply_reduce_fusion = (f32[8,8,64]{2,1,0:T(8,128)S(1)}, f32[8,8,64,640]{3,2,1,0:T(8,128)}) fusion(f32[8,8,64]{2,1,0:T(8,128)S(1)} %log_add_fusion, f32[8,8,64,640]{3,2,1,0:T(8,128)} %copy-done, pred[8,640]{1,0:T(8,128)(4,1)S(1)} %fusion.74, bf16[8,64,8,64]{1,3,2,0:T(8,128)(2,1)} %bitcast.99, bf16[8,640,8,64]{1,3,2,0:T(8,128)(2,1)} %bitcast.93), kind=kOutput, calls=%fused_computation.25 | convolution fusion | flops 348647424 | bytes 26776576 | tf_op jit(solution)/shard_map/iqhe,ikhe->ihqk/dot_general | solution.py:178
  463.3 6.0 multiply_convert_fusion.1
  469.3 2.4 copy-done.2
  471.7 4.4 multiply_convert_fusion.3
  476.1 1.0 copy-done.20
  477.1 2.3 bitcast_convert_fusion.4
  479.5 7.0 fusion.41
  486.5 7.9 copy.65
  494.3 6.3 multiply_convert_fusion
  500.7 8.3 copy.64
  509.0 19.3 %bitcast_convert_fusion.2 = bf16[1024,1024]{1,0:T(8,128)(2,1)} fusion(bf16[8,640,512]{2,1,0:T(8,128)(2,1)} %copy.65, bf16[8,640,512]{2,1,0:T(8,128)(2,1)} %copy.64, bf16[8,64,1024]{2,1,0:T(8,128)(2,1)S(1)} %copy-done.17, bf16[8,576,1024]{2,1,0:T(8,128)(2,1)} %fusion.7), kind=kOutput, calls=%fused_computation.68 | convolution fusion | flops 10780409856 | bytes 23068672 | tf_op jit(solution)/shard_map/ikd,ike->de/dot_general | solution.py:203
  528.4 9.4 bitcast_convert_fusion.1
  537.9 1.5 copy-done.14
  539.4 9.1 bitcast_convert_fusion
  550.2 17.9 %fusion.31 = f32[8,640,1024]{2,1,0:T(8,128)} fusion(bf16[8,640,512]{2,1,0:T(8,128)(2,1)} %copy.65, bf16[8,640,512]{2,1,0:T(8,128)(2,1)} %copy.64, bf16[1024,1024]{1,0:T(8,128)(2,1)S(1)} %copy-done.35), kind=kOutput, calls=%fused_computation.61 | convolution fusion | flops 10758389760 | bytes 33554432 | tf_op jit(solution)/shard_map/ike,de->ikd/dot_general | solution.py:204
  568.2 4.5 fusion.56
  572.7 14.3 %fusion.11 = (bf16[1024]{0:T(1024)(128)(2,1)S(1)}, f32[8,576]{1,0:T(8,128)S(1)}, f32[8,576]{1,0:T(8,128)S(1)}, bf16[1024]{0:T(1024)(128)(2,1)S(1)}) fusion(bf16[8,576,1024]{2,1,0:T(8,128)(2,1)} %param.15, f32[8,640,1024]{2,1,0:T(8,128)} %fusion.31, f32[8,576]{1,0:T(8,128)S(1)} %copy-done.25, f32[8,576]{1,0:T(8,128)S(1)} %copy-done.23, f32[1024]{0:T(1024)S(1)} %copy-done.29), kind=kLoop, calls=%fused_computation.13 | loop fusion | flops 47174656 | bytes 28393472 | tf_op jit(solution)/shard_map/reduce_sum | solution.py:32
  587.1 2.4 copy-done.3
  589.5 7.2 fusion.10
  596.7 78.9 %reduce-scatter.8.cloned.1.call-done = bf16[64,1024]{1,0:T(8,128)(2,1)} async-done(((bf16[1024,1024]{1,0:T(8,128)(2,1)}), bf16[64,1024]{1,0:T(8,128)(2,1)}) %reduce-scatter.8.cloned.1.call-update) | async-done | bytes 131088 | tf_op jit(solution)/shard_map/reduce_scatter | solution.py:230
  675.6 177.3 %reduce-scatter.12.cloned.1.call-done = bf16[64,4096]{1,0:T(8,128)(2,1)} async-done(((bf16[1024,4096]{1,0:T(8,128)(2,1)}), bf16[64,4096]{1,0:T(8,128)(2,1)}) %reduce-scatter.12.cloned.1.call-update) | async-done | bytes 524304 | tf_op jit(solution)/shard_map/reduce_scatter | solution.py:242
  852.9 182.4 %reduce-scatter.14.cloned.1.call-done = bf16[256,1024]{1,0:T(8,128)(2,1)} async-done(((bf16[4096,1024]{1,0:T(8,128)(2,1)}), bf16[256,1024]{1,0:T(8,128)(2,1)}) %reduce-scatter.14.cloned.1.call-update) | async-done | bytes 524304 | tf_op jit(solution)/shard_map/reduce_scatter | solution.py:245
  1035.4 3.6 fusion.55
  1039.0 77.5 %all-reduce.12 = (bf16[1024]{0:T(1024)(128)(2,1)S(1)}, bf16[1024]{0:T(1024)(128)(2,1)S(1)}, bf16[1024]{0:T(1024)(128)(2,1)S(1)}, bf16[1024]{0:T(1024)(128)(2,1)S...) all-reduce(bf16[1024]{0:T(1024)(128)(2,1)S(1)} %get-tuple-element.1, ...), channel_id=2, replica_groups=mesh['dp'=16,'rep'=2] {'dp'}, use_global_device_ids=true, to_apply=%region_16.17.clone | all-reduce | flops 6144 | bytes 24576
  1116.9 2.7 all-reduce.14
  1122.6 11.0 fusion.62
  1133.6 1.5 convert_element_type.209
  1135.1 1.5 convert_element_type.213
  1136.6 1.6 convert_element_type.211
  1138.3 2.1 convert_element_type.219
  1140.3 2.1 convert_element_type.221
  (157 shorter events, 14.5 us)
Async XLA Ops:
  7.2 107.4 %all-gather.8.cloned.1.call-start = ((), (), s32[]{:S(2)}) async-start(), calls=%async_computation.6 | async-start | bytes 1114112 | tf_op jit(solution)/shard_map/all_gather | solution.py:71
  7.9 123.6 %all-gather.6.cloned.1.call-start = ((), (), s32[]{:S(2)}) async-start(), calls=%async_computation.5 | async-start | bytes 2228224 | tf_op jit(solution)/shard_map/all_gather | solution.py:72
  8.7 179.5 %all-gather.10.cloned.1.call-start = ((), (), s32[]{:S(2)}) async-start(), calls=%async_computation.7 | async-start | bytes 1114112 | tf_op jit(solution)/shard_map/all_gather | solution.py:73
  9.4 293.1 %all-gather.12.cloned.1.call-start = ((), (), s32[]{:S(2)}) async-start(), calls=%async_computation.8 | async-start | bytes 8912896 | tf_op jit(solution)/shard_map/all_gather | solution.py:76
  10.0 406.2 %all-gather.14.cloned.1.call-start = ((), (), s32[]{:S(2)}) async-start(), calls=%async_computation.9 | async-start | bytes 8912896 | tf_op jit(solution)/shard_map/all_gather | solution.py:77
  10.6 586.1 %reduce-scatter.10.cloned.1.call-start = ((), (), s32[]{:S(2)}) async-start(), calls=%async_computation.12 | async-start | bytes 1114112 | tf_op jit(solution)/shard_map/reduce_scatter | solution.py:233
  96.3 8.8 copy-start.1
  96.4 11.5 copy-start.30
  98.0 9.9 copy-start.26
  99.9 7.9 copy-start.32
  100.0 7.9 copy-start.4
  100.0 8.4 copy-start.34
  105.1 3.4 copy-start.22
  107.9 6.7 copy-start.24
  108.3 23.2 %copy-start.15 = (bf16[8,64,1024]{2,1,0:T(8,128)(2,1)}, bf16[8,64,1024]{2,1,0:T(8,128)(2,1)S(1)}, u32[]{:S(2)}) copy-start(bf16[8,64,1024]{2,1,0:T(8,128)(2,1)S(1)} %fusion.51) | copy-start | bytes 3145732
  108.4 6.1 copy-start.28
  177.5 5.3 copy-start
  177.5 5.3 slice-start.6
  177.5 6.3 slice-start.7
  187.7 125.3 %copy-start.18 = (bf16[8,8,64,64]{3,2,1,0:T(8,128)(2,1)}, bf16[8,8,64,64]{3,2,1,0:T(8,128)(2,1)S(1)}, u32[]{:S(2)}) copy-start(bf16[8,8,64,64]{3,2,1,0:T(8,128)(2,1)S(1)} %fusion.65) | copy-start | bytes 1572868
  190.2 1.3 copy-start.8
  313.0 3.3 copy-start.12
  316.2 100.0 %copy-start.13 = (f32[8,64,1024]{2,1,0:T(8,128)S(1)}, f32[8,64,1024]{2,1,0:T(8,128)}, u32[]{:S(2)}) copy-start(f32[8,64,1024]{2,1,0:T(8,128)} %param.29) | copy-start | bytes 6291460
  416.2 14.5 %copy-start.9 = (f32[8,64,1024]{2,1,0:T(8,128)S(1)}, f32[8,64,1024]{2,1,0:T(8,128)}, u32[]{:S(2)}) copy-start(f32[8,64,1024]{2,1,0:T(8,128)} %copy-done.8) | copy-start | bytes 6291460
  439.7 2.1 copy-start.19
  440.5 1.3 copy-start.6
  443.6 153.1 %reduce-scatter.6.cloned.1.call-start = ((), (), s32[]{:S(2)}) async-start(), calls=%async_computation.10 | async-start | bytes 1114112 | tf_op jit(solution)/shard_map/reduce_scatter | solution.py:227
  443.7 19.6 %slice-start = ((s8[10485760]{0:T(1024)(128)(4,1)}), s8[2097152]{0:T(1024)(128)(4,1)S(1)}, s32[]{:S(2)}) async-start(s8[10485760]{0:T(1024)(128)(4,1)} %bitcast.85), calls=%async_computation.16 | async-start | bytes 4194304
  449.6 13.7 %slice-start.1 = ((s8[10485760]{0:T(1024)(128)(4,1)}), s8[4194304]{0:T(1024)(128)(4,1)S(1)}, s32[]{:S(2)}) async-start(s8[10485760]{0:T(1024)(128)(4,1)} %bitcast.85), calls=%async_computation.17 | async-start | bytes 8388608
  449.6 13.7 %slice-start.2 = ((s8[10485760]{0:T(1024)(128)(4,1)}), s8[4194304]{0:T(1024)(128)(4,1)S(1)}, s32[]{:S(2)}) async-start(s8[10485760]{0:T(1024)(128)(4,1)} %bitcast.85), calls=%async_computation.18 | async-start | bytes 8388608
  469.3 2.4 copy-start.2
  471.7 5.4 copy-start.16
  471.7 7.8 copy-start.11
  476.1 1.0 copy-start.20
  479.4 196.2 %reduce-scatter.8.cloned.1.call-start = ((), (), s32[]{:S(2)}) async-start(), calls=%async_computation.11 | async-start | bytes 2228224 | tf_op jit(solution)/shard_map/reduce_scatter | solution.py:230
  500.7 8.3 copy-start.17
  509.0 19.4 %copy-start.10 = (f32[8,64,1024]{2,1,0:T(8,128)S(1)}, f32[8,64,1024]{2,1,0:T(8,128)}, u32[]{:S(2)}) copy-start(f32[8,64,1024]{2,1,0:T(8,128)} %copy-done.8) | copy-start | bytes 6291460
  528.3 324.6 %reduce-scatter.12.cloned.1.call-start = ((), (), s32[]{:S(2)}) async-start(), calls=%async_computation.13 | async-start | bytes 8912896 | tf_op jit(solution)/shard_map/reduce_scatter | solution.py:242
  537.9 1.6 copy-start.14
  537.9 497.5 %reduce-scatter.14.cloned.1.call-start = ((), (), s32[]{:S(2)}) async-start(), calls=%async_computation.14 | async-start | bytes 8912896 | tf_op jit(solution)/shard_map/reduce_scatter | solution.py:245
  548.5 1.6 copy-start.35
  548.6 585.1 %all-reduce.18.cloned.1.call-start = ((), (), s32[]{:S(2)}) async-start(), calls=%async_computation.15 | async-start | bytes 2621440 | tf_op jit(solution)/shard_map/psum | solution.py:254
  550.2 17.9 %copy-start.5 = (bf16[8,64,1024]{2,1,0:T(8,128)(2,1)S(1)}, bf16[8,64,1024]{2,1,0:T(8,128)(2,1)}, u32[]{:S(2)}) copy-start(bf16[8,64,1024]{2,1,0:T(8,128)(2,1)} %param.17) | copy-start | bytes 3145732
  550.2 17.9 %copy-start.21 = (bf16[8,8,64,64]{3,2,1,0:T(8,128)(2,1)S(1)}, bf16[8,8,64,64]{3,2,1,0:T(8,128)(2,1)}, u32[]{:S(2)}) copy-start(bf16[8,8,64,64]{3,2,1,0:T(8,128)(2,1)} %copy-done.20) | copy-start | bytes 1572868
  550.2 17.9 %copy-start.27 = (f32[8,64]{1,0:T(8,128)S(1)}, f32[8,64]{1,0:T(8,128)}, u32[]{:S(2)}) copy-start(f32[8,64]{1,0:T(8,128)} %copy-done.26) | copy-start | bytes 6148
  550.2 17.9 %copy-start.31 = (f32[1024]{0:T(1024)S(1)}, f32[1024]{0:T(1024)}, u32[]{:S(2)}) copy-start(f32[1024]{0:T(1024)} %copy-done.30) | copy-start | bytes 12292
  550.2 17.9 %copy-start.33 = (f32[8,64]{1,0:T(8,128)S(1)}, f32[8,64]{1,0:T(8,128)}, u32[]{:S(2)}) copy-start(f32[8,64]{1,0:T(8,128)} %copy-done.32) | copy-start | bytes 6148
  550.2 17.9 %copy-start.36 = (bf16[1024,512]{1,0:T(8,128)(2,1)S(1)}, bf16[1024,512]{1,0:T(8,128)(2,1)}, u32[]{:S(2)}) copy-start(bf16[1024,512]{1,0:T(8,128)(2,1)} %all-gather.8.cloned.1.call-done) | copy-start | bytes 3145732
  568.1 4.6 copy-start.23
  568.1 4.5 copy-start.25
  568.1 4.5 copy-start.29
  568.2 18.9 %slice-start.3 = ((s8[9437184]{0:T(1024)(128)(4,1)}), s8[4194304]{0:T(1024)(128)(4,1)S(1)}, s32[]{:S(2)}) async-start(s8[9437184]{0:T(1024)(128)(4,1)} %bitcast.87), calls=%async_computation.19 | async-start | bytes 8388608
  572.7 14.4 %slice-start.4 = ((s8[9437184]{0:T(1024)(128)(4,1)}), s8[4194304]{0:T(1024)(128)(4,1)S(1)}, s32[]{:S(2)}) async-start(s8[9437184]{0:T(1024)(128)(4,1)} %bitcast.87), calls=%async_computation.20 | async-start | bytes 8388608
  572.7 14.4 %slice-start.5 = ((s8[9437184]{0:T(1024)(128)(4,1)}), s8[1048576]{0:T(1024)(128)(4,1)S(1)}, s32[]{:S(2)}) async-start(s8[9437184]{0:T(1024)(128)(4,1)} %bitcast.87), calls=%async_computation.21 | async-start | bytes 2097152
  572.7 16.8 %copy-start.3 = (f32[8,640,1024]{2,1,0:T(8,128)S(1)}, f32[8,640,1024]{2,1,0:T(8,128)}, u32[]{:S(2)}) copy-start(f32[8,640,1024]{2,1,0:T(8,128)} %fusion.31) | copy-start | bytes 62914564
  589.5 445.9 %copy-start.7 = (f32[8,64,1024]{2,1,0:T(8,128)S(1)}, f32[8,64,1024]{2,1,0:T(8,128)}, u32[]{:S(2)}) copy-start(f32[8,64,1024]{2,1,0:T(8,128)} %copy-done.6) | copy-start | bytes 6291460
Sparse Core Ops, SparseCore 0:
  10.8 58.1 all-gather.7
  71.7 59.7 all-gather.5
  134.2 53.9 all-gather.9
  190.8 111.6 all-gather.11
  305.1 111.0 all-gather.13
  443.7 75.7 reduce-scatter.9
  521.9 74.2 reduce-scatter.5
  598.5 77.0 reduce-scatter.7
  677.9 174.9 reduce-scatter.11
  855.1 180.2 reduce-scatter.13
  1038.0 22.6 all-reduce.17
where the time goes:
time: 1160 us; the launch traced here: 1150 us
  waiting for transfers between devices  646 us (56%)
  matrix products  174 us (15%)
  blocking collectives  159 us (14%)
  other arithmetic  84.5 us (7%)
  local copies, waits for them, and re-layouts  69 us (6%)
  between operations  16.3 us (1%)
    reduce_scatter x1, waiting for transfers between devices, shards(): lax.psum_scatter(grad_ffout.astype(jnp.bfloat16), 'dp', scatter_dimension...  182 us
    reduce_scatter x1, waiting for transfers between devices, shards(): lax.psum_scatter(grad_ffin.astype(jnp.bfloat16), 'dp', scatter_dimension=...  177 us
    unnamed x2, blocking collectives  156 us
    all_gather x1, waiting for transfers between devices, shards(): lax.all_gather(ff_in_weight, 'dp', axis=0, tiled=True)  111 us
    all_gather x1, waiting for transfers between devices, shards(): lax.all_gather(ff_out_weight, 'dp', axis=0, tiled=True)  80.3 us
    reduce_scatter x1, waiting for transfers between devices, shards(): lax.psum_scatter(grad_kvweight.astype(jnp.bfloat16), 'dp', scatter_dimens...  78.9 us
    unnamed x109, local copies, waits for them, and re-layouts  24.4 us
  transfers between devices with their start and end apart: 11, of which 7 were waited for; matrix products, arithmetic and copies ran while one was open for 24% of the time, Pallas kernels for 0%

commit v1 on v0

v1 whole, which is shorter than its diff:
```python
import math

import jax
import jax.numpy as jnp
from jax import lax
from jax.sharding import PartitionSpec as P

HEADS = 8


EPS = 1e-05
F32 = jnp.float32
BF16 = jnp.bfloat16


def norm_parts(values):
    centre = jnp.mean(values, -1, keepdims=True)
    centred = values - centre
    inverse = lax.rsqrt(jnp.mean(centred * centred, -1, keepdims=True) + EPS)
    return centred * inverse, inverse


def norm_grad(grad_normed, unit, inverse, gain):
    scaled = grad_normed * gain
    return inverse * (
        scaled
        - jnp.mean(scaled, -1, keepdims=True)
        - unit * jnp.mean(scaled * unit, -1, keepdims=True)
    )


def row_total(values):
    return jnp.sum(values.reshape(-1, values.shape[-1]), axis=0)


def gelu_exact(values):
    return jax.nn.gelu(values, approximate=False)


def masked_scores(query_heads, key_heads, valid, scale):
    raw = (
        jnp.einsum("iqhe,ikhe->ihqk", query_heads, key_heads, preferred_element_type=F32)
        * scale
    )
    return jnp.where(valid[:, None, None, :], raw, jnp.float32(-1e30))


class Grid:
    def __init__(self, dp, rep):
        self.dp = dp
        self.rep = rep
        self.me = lax.axis_index("dp")
        self.core = lax.axis_index("rep")
        self.column = [1 << b for b in range(2, dp.bit_length() - 1)]

    def swap(self, value, bit):
        return lax.ppermute(value, "dp", [(i, i ^ bit) for i in range(self.dp)])

    def side(self, bit):
        return (self.me & bit) != 0

    def pair(self, own, other, bit, axis):
        return jnp.where(
            self.side(bit), jnp.stack([other, own], axis), jnp.stack([own, other], axis)
        )

    def pick(self, value, bit, axis):
        at = jnp.where(self.side(bit), 1, 0)
        keep = lax.dynamic_index_in_dim(value, at, axis, keepdims=False)
        send = lax.dynamic_index_in_dim(value, 1 - at, axis, keepdims=False)
        return keep, send

    def gather(self, first, second):
        rows = first.shape[0]
        both = jnp.concatenate([first, second], 0)[None]
        for bit in reversed(self.column):
            got = self.swap(both, bit)
            both = self.pair(both, got, bit, 1)
            both = both.reshape((-1,) + both.shape[2:])
        first, second = both[:, :rows], both[:, rows:]
        first_got, second_got = self.swap(first, 2), self.swap(second, 1)
        first = self.pair(first, first_got, 2, 1)
        second = self.pair(second, second_got, 1, 1)
        first_got, second_got = self.swap(first, 1), self.swap(second, 2)
        first = self.pair(first, first_got, 1, 2)
        second = self.pair(second, second_got, 2, 1)
        return (
            first.reshape((self.dp,) + first.shape[3:]),
            second.reshape((self.dp,) + second.shape[3:]),
        )

    def total(self, first, second):
        rows = first.shape[1]
        tail = first.shape[1:]

        def fold(value, bit, axis, last=False):
            keep, send = self.pick(value, bit, axis)
            got = self.swap(send, bit)
            added = keep.astype(F32) + got.astype(F32)
            return added if last else added.astype(BF16)

        first = first.reshape((-1, 2, 2) + tail)
        second = second.reshape((-1, 2, 2) + second.shape[1:])
        first, second = fold(first, 1, 2), fold(second, 2, 1)
        first, second = fold(first, 2, 1), fold(second, 1, 1)
        both = jnp.concatenate([first, second], 1)
        for bit in self.column:
            both = both.reshape((-1, 2) + both.shape[1:])
            both = fold(both, bit, 1, bit == self.column[-1])
        both = both[0]
        return both[:rows], both[rows:]

    def other(self, value):
        return lax.ppermute(value, "rep", [(0, 1), (1, 0)])

    def rep_all(self, value):
        if self.rep != 2:
            return lax.all_gather(value, "rep", axis=0)
        got = self.other(value)
        return jnp.where(self.core == 0, jnp.stack([value, got]), jnp.stack([got, value]))

    def rep_rows(self, value):
        if self.rep != 2:
            return lax.all_gather(value, "rep", axis=0, tiled=True)
        return jnp.concatenate([value, self.other(value)], 0)

    def rep_back(self, value):
        if self.rep != 2:
            return lax.psum_scatter(value, "rep", scatter_dimension=0, tiled=True)
        rows = value.shape[0] // 2
        return value[:rows] + self.other(value[rows:])

    def rep_total(self, value, axis):
        if self.rep != 2:
            value = jnp.moveaxis(value, axis, 0)
            return lax.psum_scatter(value, "rep", scatter_dimension=0).astype(BF16)
        keep = lax.dynamic_index_in_dim(value, self.core, axis, keepdims=False)
        send = lax.dynamic_index_in_dim(value, 1 - self.core, axis, keepdims=False)
        return (keep + self.other(send.astype(BF16)).astype(F32)).astype(BF16)

    def mine(self, value, axis):
        return lax.dynamic_index_in_dim(value, self.core, axis, keepdims=False)


def fold_rows(value):
    half = value.shape[-2] // 2
    return jnp.concatenate([value[..., :half, :], value[..., half:, :]], -1)


def unfold_rows(value):
    half = value.shape[-1] // 2
    return jnp.concatenate([value[..., :half], value[..., half:]], -2)


def shards(
    dp,
    rep,
    media_tokens,
    patch_counts,
    latents,
    media_gain,
    media_bias,
    latent_gain,
    latent_bias,
    query_weight,
    keyval_weight,
    outproj_weight,
    ff_gain,
    ff_bias,
    ff_in_weight,
    ff_out_weight,
    cotangent,
):
    grid = Grid(dp, rep)
    images, media_len, width = media_tokens.shape
    lat_len = latents.shape[1]
    keys_len = media_len + lat_len
    inner_width = query_weight.shape[1]
    head_size = inner_width // HEADS
    hidden = ff_in_weight.shape[1]
    slot = hidden // dp // rep
    part = width // dp
    kv_rows = part // rep
    o_rows = inner_width // dp // rep
    scale = 1.0 / math.sqrt(head_size)

    norms = jnp.stack([media_gain, media_bias, latent_gain, latent_bias, ff_gain, ff_bias])
    norm_row = jnp.pad(norms.reshape(1, -1), ((0, 0), (0, width - norms.size)))
    kv_part = grid.mine(keyval_weight.reshape(rep, kv_rows, width), 0)
    q_part = fold_rows(grid.mine(query_weight.reshape(rep, kv_rows, inner_width), 0))
    q_rows = q_part.shape[0]
    got_kv, got_q = grid.gather(kv_part, jnp.concatenate([q_part, norm_row], 0))
    got_norms = got_q[:, q_rows, : norms.size].reshape(dp, 6, part)
    got_norms = jnp.moveaxis(got_norms, 1, 0).reshape(6, width).astype(F32)
    gain_media, bias_media, gain_latent, bias_latent, gain_ff, bias_ff = got_norms
    w_keyval = jnp.moveaxis(grid.rep_all(got_kv), 0, 1).reshape(width, width)
    w_query = jnp.moveaxis(grid.rep_all(unfold_rows(got_q[:, :q_rows])), 0, 1)
    w_query = w_query.reshape(width, inner_width)

    ffin_part = grid.mine(ff_in_weight.reshape(part, dp, rep, slot), 2).reshape(part, dp * slot)
    cut = ffin_part.shape[1] // 2
    o_part = grid.mine(outproj_weight.reshape(rep, o_rows, width), 0)
    o_part = jnp.pad(o_part, ((0, 0), (0, max(cut - width, 0))))
    got_lo, got_hi = grid.gather(
        ffin_part[:, :cut] if cut >= width else jnp.pad(ffin_part[:, :cut], ((0, 0), (0, width - cut))),
        jnp.concatenate(
            [
                ffin_part[:, cut:] if cut >= width else jnp.pad(ffin_part[:, cut:], ((0, 0), (0, width - cut))),
                o_part,
            ],
            0,
        ),
    )
    w_ffin = jnp.concatenate(
        [
            got_lo[:, :, :cut].reshape(width, cut),
            got_hi[:, :part, :cut].reshape(width, cut),
        ],
        1,
    )
    w_outproj = jnp.moveaxis(grid.rep_all(got_hi[:, part:, :width]), 0, 1).reshape(inner_width, width)
    ffout_part = grid.mine(ff_out_weight.reshape(rep, slot, width), 0)
    w_ffout = lax.all_gather(ffout_part, "dp", axis=0, tiled=True)

    media_unit, media_inv = norm_parts(media_tokens.astype(F32))
    latent_f = latents.astype(F32)
    latent_unit, latent_inv = norm_parts(latent_f)
    grad_out_low = grid.rep_rows(cotangent.astype(BF16).reshape(-1, width))

    media_low = (media_unit * gain_media + bias_media).astype(BF16)
    latent_low = (latent_unit * gain_latent + bias_latent).astype(BF16)
    queries = jnp.einsum("ild,de->ile", latent_low, w_query, preferred_element_type=F32).astype(BF16)
    key_input = jnp.concatenate([media_low, latent_low], axis=1)
    keyvals = jnp.einsum("ikd,de->ike", key_input, w_keyval, preferred_element_type=F32).astype(BF16)
    key_heads = keyvals[:, :, :inner_width].reshape(images, keys_len, HEADS, head_size)
    value_heads = keyvals[:, :, inner_width:].reshape(images, keys_len, HEADS, head_size)
    query_heads = queries.reshape(images, lat_len, HEADS, head_size)
    positions = jnp.arange(keys_len, dtype=jnp.int32)
    valid = (positions[None, :] < patch_counts[:, None]) | (positions[None, :] >= media_len)
    scores = masked_scores(query_heads, key_heads, valid, scale)
    top = jnp.max(scores, -1, keepdims=True)
    expd = jnp.exp(scores - top)
    total = jnp.sum(expd, -1, keepdims=True)
    probs = expd / total
    log_total = top + jnp.log(total)
    mixed = jnp.einsum("ihqk,ikhe->iqhe", probs.astype(BF16), value_heads, preferred_element_type=F32)
    mixed = mixed.reshape(images, lat_len, inner_width).astype(BF16)
    branch = jnp.einsum("ile,ed->ild", mixed, w_outproj, preferred_element_type=F32)
    resid = latent_f + branch
    ff_unit, ff_inv = norm_parts(resid)
    ff_low = grid.rep_rows((ff_unit * gain_ff + bias_ff).astype(BF16).reshape(-1, width))

    pre_act = jnp.dot(ff_low, w_ffin, preferred_element_type=F32)
    activ, gelu_pull = jax.vjp(gelu_exact, pre_act)
    activ_low = activ.astype(BF16)
    grad_ffout = jnp.einsum("rf,rd->fd", activ_low, grad_out_low, preferred_element_type=F32).astype(BF16)
    ff_branch = jnp.dot(activ_low, w_ffout, preferred_element_type=F32)
    grad_activ = jnp.einsum("rd,fd->rf", grad_out_low, w_ffout, preferred_element_type=F32)
    (grad_pre,) = gelu_pull(grad_activ)
    grad_pre_low = grad_pre.astype(BF16)
    grad_ffin = jnp.einsum("rd,rf->df", ff_low, grad_pre_low, preferred_element_type=F32).astype(BF16)
    grad_ffnormed = jnp.einsum("rf,df->rd", grad_pre_low, w_ffin, preferred_element_type=F32)
    grad_ffnormed = grid.rep_back(grad_ffnormed).reshape(resid.shape)
    new_latents = resid + grid.rep_back(ff_branch).reshape(resid.shape)

    grad_ffout = grad_ffout.reshape(dp, slot, width)
    own_lo, own_hi = grid.total(grad_ffout[:, : slot // 2], grad_ffout[:, slot // 2 :])
    own_ffout = grid.rep_all(jnp.concatenate([own_lo, own_hi], 0)).reshape(rep * slot, width)
    grad_ffin = grad_ffin.reshape(dp, part, dp * slot)
    own_lo, own_hi = grid.total(grad_ffin[:, :, :cut], grad_ffin[:, :, cut:])
    own_ffin = grid.rep_all(jnp.concatenate([own_lo, own_hi], 1))
    own_ffin = jnp.moveaxis(own_ffin.reshape(rep, part, dp, slot), 0, 2).reshape(part, hidden)

    grad_gain_ff = row_total(grad_ffnormed * ff_unit)
    grad_bias_ff = row_total(grad_ffnormed)
    grad_resid = cotangent + norm_grad(grad_ffnormed, ff_unit, ff_inv, gain_ff)
    grad_resid_low = grad_resid.astype(BF16)
    grad_outproj = jnp.einsum("ile,ild->ed", mixed, grad_resid_low, preferred_element_type=F32)
    grad_mixed = jnp.einsum("ild,ed->ile", grad_resid_low, w_outproj, preferred_element_type=F32)
    grad_mixed_heads = grad_mixed.astype(BF16).reshape(images, lat_len, HEADS, head_size)
    scores_again = masked_scores(query_heads, key_heads, valid, scale)
    probs_again = jnp.exp(scores_again - log_total)
    grad_probs = jnp.einsum("iqhe,ikhe->ihqk", grad_mixed_heads, value_heads, preferred_element_type=F32)
    grad_scores = probs_again * (grad_probs - jnp.sum(probs_again * grad_probs, -1, keepdims=True))
    grad_scores_low = grad_scores.astype(BF16)
    grad_queries = (
        jnp.einsum("ihqk,ikhe->iqhe", grad_scores_low, key_heads, preferred_element_type=F32) * scale
    )
    grad_queries = grad_queries.reshape(images, lat_len, inner_width).astype(BF16)
    grad_keys = (
        jnp.einsum("ihqk,iqhe->ikhe", grad_scores_low, query_heads, preferred_element_type=F32) * scale
    )
    grad_values = jnp.einsum(
        "ihqk,iqhe->ikhe", probs_again.astype(BF16), grad_mixed_heads, preferred_element_type=F32
    )
    grad_keyvals = jnp.concatenate(
        [
            grad_keys.reshape(images, keys_len, inner_width),
            grad_values.reshape(images, keys_len, inner_width),
        ],
        axis=-1,
    ).astype(BF16)
    grad_qweight = jnp.einsum("ild,ile->de", latent_low, grad_queries, preferred_element_type=F32)
    grad_kvweight = jnp.einsum("ikd,ike->de", key_input, grad_keyvals, preferred_element_type=F32)
    grad_key_input = jnp.einsum("ike,de->ikd", grad_keyvals, w_keyval, preferred_element_type=F32)
    grad_latnormed = jnp.einsum("ile,de->ild", grad_queries, w_query, preferred_element_type=F32)
    grad_latnormed = grad_latnormed + grad_key_input[:, media_len:]
    grad_medianormed = grad_key_input[:, :media_len]
    media_grad = norm_grad(grad_medianormed, media_unit, media_inv, gain_media)
    latent_grad = grad_resid + norm_grad(grad_latnormed, latent_unit, latent_inv, gain_latent)
    vectors = jnp.stack(
        [
            row_total(grad_medianormed * media_unit),
            row_total(grad_medianormed),
            row_total(grad_latnormed * latent_unit),
            row_total(grad_latnormed),
            grad_gain_ff,
            grad_bias_ff,
        ]
    )

    kv_sum = grid.rep_total(grad_kvweight.reshape(dp, rep, kv_rows, width), 1)
    q_sum = fold_rows(grid.rep_total(grad_qweight.reshape(dp, rep, kv_rows, inner_width), 1))
    o_sum = grid.rep_total(grad_outproj.reshape(dp, rep, o_rows, width), 1)
    vec_row = jnp.moveaxis(vectors.reshape(6, dp, part), 1, 0).reshape(dp, 1, 6 * part)
    vec_row = jnp.pad(vec_row, ((0, 0), (0, 0), (0, width - 6 * part))).astype(BF16)
    own_kv, own_rest = grid.total(kv_sum, jnp.concatenate([q_sum, o_sum, vec_row], 1))
    every = grid.rep_all(jnp.concatenate([own_kv, own_rest], 0))
    own_kv = every[:, :kv_rows].reshape(part, width)
    own_q = unfold_rows(every[:, kv_rows : kv_rows + q_rows]).reshape(part, inner_width)
    at = kv_rows + q_rows
    own_o = every[:, at : at + o_rows].reshape(rep * o_rows, width)
    own_vec = jnp.sum(every[:, at + o_rows, : 6 * part], 0).reshape(6, part)
    return (
        new_latents,
        media_grad,
        latent_grad,
        own_vec[0],
        own_vec[1],
        own_vec[2],
        own_vec[3],
        own_q,
        own_kv,
        own_o,
        own_vec[4],
        own_vec[5],
        own_ffin,
        own_ffout,
    )


def solution(mesh):
    dp, rep = mesh.shape["dp"], mesh.shape["rep"]

    def program(*arrays):
        return shards(dp, rep, *arrays)

    return jax.shard_map(
        program,
        mesh=mesh,
        in_specs=(
            P(("dp", "rep"), None, None),
            P(("dp", "rep")),
            P(("dp", "rep"), None, None),
            P("dp"),
            P("dp"),
            P("dp"),
            P("dp"),
            P("dp", None),
            P("dp", None),
            P("dp", None),
            P("dp"),
            P("dp"),
            P("dp", None),
            P("dp", None),
            P(("dp", "rep"), None, None),
        ),
        out_specs=(
            P(("dp", "rep"), None, None),
            P(("dp", "rep"), None, None),
            P(("dp", "rep"), None, None),
            P("dp"),
            P("dp"),
            P("dp"),
            P("dp"),
            P("dp", None),
            P("dp", None),
            P("dp", None),
            P("dp"),
            P("dp"),
            P("dp", None),
            P("dp", None),
        ),
        check_vma=False,
    )
```

time: 1160 us -> 579 us (0.50)
  waiting for transfers between devices: 646 us -> 131 us
  blocking collectives: 159 us -> 0 us
  starting transfers between devices: 0.44 us -> 40.1 us
  other arithmetic: 84.5 us -> 120 us
  local copies, waits for them, and re-layouts: 69 us -> 97.6 us
    reduce_scatter x5 -> x0, waiting for transfers between devices: 439 us -> none  [the longest x1 182 us: shards(): lax.psum_scatter(grad_ffout.astype(jnp.bfloat16), 'dp', scatter_dimension...]
    all_gather x5 -> x1, waiting for transfers between devices: 204 us -> 0.02 us  [shards(): w_ffout = lax.all_gather(ffout_part, 'dp', axis=0, tiled=True)]
    unnamed x2 -> x0, blocking collectives: 156 us -> none
    ppermute x0 -> x43, waiting for transfers between devices: none -> 131 us  [the longest x30 131 us: swap(): return lax.ppermute(value, 'dp', [(i, i ^ bit) for i in range(self.dp)])]
    ppermute x0 -> x43, starting transfers between devices: none -> 40.1 us  [the longest x30 37.7 us: swap(): return lax.ppermute(value, 'dp', [(i, i ^ bit) for i in range(self.dp)])]
    select_n x0 -> x20, other arithmetic: none -> 21.7 us  [the longest x18 19.4 us: pair(): jnp.where(self.side(bit), jnp.stack([other, own], axis), jnp.stack([own,...]
    convert_element_type x21 -> x24, other arithmetic: 44.1 us -> 32.4 us  [the longest x1 10.8 us: shards(): media_low = (media_unit * gain_media + bias_media).astype(BF16)]
    unnamed x109 -> x202, local copies, waits for them, and re-layouts: 24.4 us -> 13.5 us
  transfers between devices with their start and end apart: 11 -> 44, of which waited for: 7 -> 18; matrix products, arithmetic and copies ran while one was open for 24% -> 63% of each run, Pallas kernels for 0% -> 0%
where the time goes in v1:
time: 579 us; the launch traced here: 570 us
  matrix products  165 us (28%)
  waiting for transfers between devices  131 us (23%)
  other arithmetic  120 us (21%)
  local copies, waits for them, and re-layouts  97.6 us (17%)
  starting transfers between devices  40.1 us (7%)
  between operations  16.1 us (3%)
    ppermute x30, waiting for transfers between devices, swap(): return lax.ppermute(value, 'dp', [(i, i ^ bit) for i in range(self.dp)])  131 us
    ppermute x30, starting transfers between devices, swap(): return lax.ppermute(value, 'dp', [(i, i ^ bit) for i in range(self.dp)])  37.7 us
    dot_general x1, matrix products, shards(): pre_act = jnp.dot(ff_low, w_ffin, preferred_element_type=F32)  27.6 us
    dot_general x1, matrix products, shards(): jnp.einsum('ikd,ike->de', key_input, grad_keyvals, preferred_element_type...  19.9 us
    select_n x18, other arithmetic, pair(): jnp.where(self.side(bit), jnp.stack([other, own], axis), jnp.stack([own,...  19.4 us
    dot_general x1, matrix products, shards(): jnp.einsum('ike,de->ikd', grad_keyvals, w_keyval, preferred_element_type=...  19 us
    mul x1, other arithmetic, norm_grad(): inverse * (scaled - jnp.mean(scaled, -1, keepdims=True) - unit * jnp.mean...  17.6 us
    dot_general x1, matrix products, shards(): jnp.einsum('ikd,de->ike', key_input, w_keyval, preferred_element_type=F32)  17.4 us
  transfers between devices with their start and end apart: 44, of which 18 were waited for; matrix products, arithmetic and copies ran while one was open for 63% of the time, Pallas kernels for 0%

profile of v1, /device:TPU:0, one launch (start us, length us, event | category | flops | bytes accessed | tf_op | source)
XLA Modules:
  0.0 569.6 jit_solution(9769790356219920538)
XLA Ops:
  11.2 4.1 collective-permute-start.8
  18.6 5.1 convert_reduce_fusion
  24.9 2.7 fusion.12
  27.7 5.9 %collective-permute-done = bf16[1,49,1024]{2,1,0:T(8,128)(2,1)S(1)} collective-permute-done((bf16[1,49,1024]{2,1,0:T(8,128)(2,1)S(1)}, bf16[1,49,1024]{2,1,0:T(8,128)(2,1)S(1)}, u32[]{:S(2)}, u32[]{:S(2)}) %collective-permute-start) | collective-permute-done | bytes 100384 | tf_op jit(solution)/shard_map/ppermute | solution.py:57
  36.7 5.6 collective-permute-done.1
  49.6 2.5 collective-permute-done.4
  57.7 10.8 %fusion.7 = bf16[8,576,1024]{2,1,0:T(8,128)(2,1)} fusion(bf16[8,576,1024]{2,1,0:T(8,128)(2,1)} %param.15, f32[1024]{0:T(1024)S(1)} %add.239, f32[1024]{0:T(1024)S(1)} %mul.203, f32[8,576]{1,0:T(8,128)S(1)} %add_rsqrt_fusion, f32[8,576]{1,0:T(8,128)S(1)} %broadcast_multiply_fusion.2), kind=kLoop, calls=%fused_computation.9 | loop fusion | flops 28311552 | bytes 18919424 | tf_op jit(solution)/shard_map/convert_element_type | solution.py:230
  76.7 2.3 maximum_select_fusion.6
  86.7 1.8 collective-permute-done.14
  88.4 2.7 maximum_select_fusion.9
  91.8 3.0 maximum_select_fusion.3
  96.4 2.5 maximum_select_fusion.4
  98.9 2.7 fusion.57
  103.2 17.4 %fusion.25 = bf16[8,640,1024]{2,1,0:T(8,128)(2,1)} fusion(bf16[1024,1024,1]{1,0,2:T(8,128)(2,1)S(1)} %bitcast.383, bf16[8,64,1024]{2,1,0:T(8,128)(2,1)S(1)} %copy-done.46, bf16[8,576,1024]{2,1,0:T(8,128)(2,1)} %fusion.7), kind=kOutput, calls=%fused_computation.49 | convolution fusion | flops 10763632640 | bytes 23068672 | tf_op jit(solution)/shard_map/ikd,de->ike/dot_general | solution.py:234
  120.5 9.0 %fusion.116 = (bf16[8,640,512]{2,1,0:T(8,128)(2,1)}, bf16[8,640,512]{2,1,0:T(8,128)(2,1)}) fusion(bf16[8,640,1024]{2,1,0:T(8,128)(2,1)} %fusion.25), kind=kLoop, calls=%fused_computation.294 | loop fusion | bytes 20971520 | tf_op jit(solution)/shard_map/slice | solution.py:235
  129.5 7.8 %copy.240 = bf16[8,640,512]{1,2,0:T(8,128)(2,1)} copy(bf16[8,640,512]{2,1,0:T(8,128)(2,1)} %get-tuple-element.35) | data formatting | bytes 10485760 | tf_op jit(solution)/shard_map/slice | solution.py:235
  137.4 8.1 %copy.238 = bf16[8,640,512]{1,2,0:T(8,128)(2,1)} copy(bf16[8,640,512]{2,1,0:T(8,128)(2,1)} %get-tuple-element.36) | data formatting | bytes 10485760 | tf_op jit(solution)/shard_map/slice | solution.py:236
  145.4 4.5 fusion.30
  150.0 2.7 fusion.14
  152.7 4.1 copy.321
  157.5 3.9 fusion.68
  168.4 2.0 maximum_select_fusion.2
  171.0 27.6 %multiply_convert_fusion.2 = (bf16[1024,2048]{1,0:T(8,128)(2,1)S(1)}, f32[1024,2048]{1,0:T(8,128)}, f32[1024,2048]{1,0:T(8,128)}) fusion(bf16[1024,1024]{1,0:T(8,128)(2,1)S(1)} %bitcast.387, bf16[1024,1024]{1,0:T(8,128)(2,1)S(1)} %bitcast.385, bf16[512,1024]{1,0:T(8,128)(2,1)} %collective-permute-done.13, bf16[512,1024]{1,0:T(8,128)(2,1)S(1)} %bitcast.393), kind=kOutput, calls=%fused_computation.31 | convolution fusion | flops 4443865088 | bytes 27262976 | tf_op jit(solution)/shard_map/dot_general | solution.py:253
  198.7 7.9 %convolution_convert_fusion = bf16[2048,1024]{1,0:T(8,128)(2,1)S(1)} fusion(bf16[1024,2048]{1,0:T(8,128)(2,1)S(1)} %get-tuple-element.33, bf16[512,1024]{1,0:T(8,128)(2,1)} %collective-permute-done.17, bf16[512,1024]{1,0:T(8,128)(2,1)} %bitcast.71), kind=kOutput, calls=%fused_computation.59 | convolution fusion | flops 4301258752 | bytes 10485760 | tf_op jit(solution)/shard_map/rf,rd->fd/dot_general | solution.py:256
  206.6 1.9 fusion.117
  211.3 1.9 constant_dynamic-slice_fusion.2
  213.9 36.6 %collective-permute-done.36 = bf16[4,2,64,1024]{3,2,1,0:T(8,128)(2,1)} collective-permute-done((bf16[4,2,64,1024]{3,2,1,0:T(8,128)(2,1)S(1)}, bf16[4,2,64,1024]{3,2,1,0:T(8,128)(2,1)}, u32[]{:S(2)}, u32[]{:S(2)}) %collective-permute-start.36) | collective-permute-done | bytes 1048608 | tf_op jit(solution)/shard_map/ppermute | solution.py:57
  255.4 10.2 %collective-permute-done.37 = bf16[4,64,1024]{2,1,0:T(8,128)(2,1)S(1)} collective-permute-done((bf16[4,64,1024]{2,1,0:T(8,128)(2,1)S(1)}, bf16[4,64,1024]{2,1,0:T(8,128)(2,1)S(1)}, u32[]{:S(2)}, u32[]{:S(2)}) %collective-permute-start.37) | collective-permute-done | bytes 524320 | tf_op jit(solution)/shard_map/ppermute | solution.py:57
  269.5 1.7 collective-permute-start.40
  271.2 10.8 %collective-permute-done.40 = bf16[2,128,1024]{2,1,0:T(8,128)(2,1)S(1)} collective-permute-done((bf16[2,128,1024]{2,1,0:T(8,128)(2,1)S(1)}, bf16[2,128,1024]{2,1,0:T(8,128)(2,1)S(1)}, u32[]{:S(2)}, u32[]{:S(2)}) %collective-permute-start.40) | collective-permute-done | bytes 524320 | tf_op jit(solution)/shard_map/ppermute | solution.py:57
  282.2 3.6 collective-permute-start.41
  286.3 2.5 copy.255
  288.9 6.8 %collective-permute-done.41 = bf16[1,128,1024]{2,1,0:T(8,128)(2,1)S(1)} collective-permute-done((bf16[1,128,1024]{2,1,0:T(8,128)(2,1)S(1)}, bf16[1,128,1024]{2,1,0:T(8,128)(2,1)S(1)}, u32[]{:S(2)}, u32[]{:S(2)}) %collective-permute-start.41) | collective-permute-done | bytes 262176 | tf_op jit(solution)/shard_map/ppermute | solution.py:57
  296.1 11.6 %add_convert_fusion = bf16[1024,2048]{1,0:T(8,128)(2,1)S(1)} fusion(f32[1024,2048]{1,0:T(8,128)} %get-tuple-element.34, f32[1024,2048]{1,0:T(8,128)} %get-tuple-element.96, bf16[1,2048,1024]{2,1,0:T(8,128)(2,1)} %all-gather.3.cloned.1.call-done, bf16[512,1024]{1,0:T(8,128)(2,1)} %collective-permute-done.17, bf16[512,1024]{1,0:T(8,128)(2,1)} %bitcast.71), kind=kOutput, calls=%fused_computation.30 | convolution fusion | flops 4328521728 | bytes 27262976 | tf_op jit(solution)/shard_map/rd,fd->rf/dot_general | solution.py:258
  307.7 6.3 %convolution_convert_fusion.1 = bf16[1024,2048]{1,0:T(8,128)(2,1)S(1)} fusion(bf16[1024,2048]{1,0:T(8,128)(2,1)S(1)} %add_convert_fusion, bf16[512,1024]{1,0:T(8,128)(2,1)} %collective-permute-done.13, bf16[512,1024]{1,0:T(8,128)(2,1)S(1)} %bitcast.394), kind=kOutput, calls=%fused_computation.60 | convolution fusion | flops 4301258752 | bytes 10485760 | tf_op jit(solution)/shard_map/rd,rf->df/dot_general | solution.py:261
  316.7 4.5 fusion.40
  321.9 18.5 %collective-permute-done.29 = bf16[4,2,64,1024]{3,2,0,1:T(8,128)(2,1)S(1)} collective-permute-done((bf16[4,2,64,1024]{3,2,0,1:T(8,128)(2,1)S(1)}, bf16[4,2,64,1024]{3,2,0,1:T(8,128)(2,1)S(1)}, u32[]{:S(2)}, u32[]{:S(2)}) %collective-permute-start.29) | collective-permute-done | bytes 1048608 | tf_op jit(solution)/shard_map/ppermute | solution.py:57
  343.8 4.5 fusion.33
  348.4 1.8 slice.240
  351.3 3.1 collective-permute-done.30
  357.5 1.7 fusion.114
  359.4 3.6 multiply_reduce_fusion.1
  363.1 2.2 slice_add_fusion.2
  365.9 2.4 multiply_add_fusion
  371.8 13.8 %multiply_reduce_fusion = (f32[8,8,64]{2,1,0:T(8,128)S(1)}, f32[8,8,64,640]{3,2,1,0:T(8,128)}) fusion(f32[8,8,64]{2,1,0:T(8,128)S(1)} %log_add_fusion, f32[8,8,64,640]{3,2,1,0:T(8,128)} %copy-done.2, pred[8,640]{1,0:T(8,128)(4,1)S(1)} %copy-done.54, bf16[8,64,8,64]{1,3,2,0:T(8,128)(2,1)} %bitcast.356, bf16[8,640,8,64]{1,3,2,0:T(8,128)(2,1)} %bitcast.348), kind=kOutput, calls=%fused_computation.23 | convolution fusion | flops 348647424 | bytes 26776576 | tf_op jit(solution)/shard_map/iqhe,ikhe->ihqk/dot_general | solution.py:283
  385.6 4.4 fusion.37
  390.0 6.0 %multiply_convert_fusion.1 = bf16[8,8,64,640]{3,2,1,0:T(8,128)(2,1)S(1)} fusion(f32[8,8,64,640]{3,2,1,0:T(8,128)} %get-tuple-element.98, f32[8,8,64]{2,1,0:T(8,128)S(1)} %get-tuple-element.97, f32[8,8,64]{2,1,0:T(8,128)S(1)} %log_add_fusion, f32[8,8,64,640]{3,2,1,0:T(8,128)S(1)} %bitcast.338, pred[8,640]{1,0:T(8,128)(4,1)S(1)} %copy-done.54), kind=kLoop, calls=%fused_computation.22 | loop fusion | flops 15728640 | bytes 26252288 | tf_op jit(solution)/shard_map/convert_element_type | solution.py:285
  396.0 4.0 multiply_convert_fusion
  400.0 7.9 %copy.250 = bf16[8,640,512]{2,1,0:T(8,128)(2,1)} copy(bf16[8,640,512]{1,2,0:T(8,128)(2,1)} %bitcast.345) | data formatting | bytes 10485760 | tf_op jit(solution)/shard_map/reshape | solution.py:298
  407.9 8.2 %copy.251 = bf16[8,640,512]{2,1,0:T(8,128)(2,1)} copy(bf16[8,640,512]{1,2,0:T(8,128)(2,1)} %bitcast.347) | data formatting | bytes 10485760 | tf_op jit(solution)/shard_map/reshape | solution.py:299
  416.1 19.9 %fusion.22 = f32[1024,1024,1]{1,0,2:T(8,128)} fusion(bf16[8,640,512]{2,1,0:T(8,128)(2,1)} %copy.251, bf16[8,640,512]{2,1,0:T(8,128)(2,1)} %copy.250, bf16[8,64,1024]{2,1,0:T(8,128)(2,1)S(1)} %copy-done.47, bf16[8,576,1024]{2,1,0:T(8,128)(2,1)} %fusion.7), kind=kOutput, calls=%fused_computation.46 | convolution fusion | flops 10779361280 | bytes 25165824 | tf_op jit(solution)/shard_map/ikd,ike->de/dot_general | solution.py:304
  436.0 19.0 %fusion.23 = f32[8,640,1024]{2,1,0:T(8,128)} fusion(bf16[1024,1024,1]{1,0,2:T(8,128)(2,1)} %bitcast.384, bf16[8,640,512]{2,1,0:T(8,128)(2,1)} %copy.251, bf16[8,640,512]{2,1,0:T(8,128)(2,1)} %copy.250), kind=kOutput, calls=%fused_computation.47 | convolution fusion | flops 10758389760 | bytes 33554432 | tf_op jit(solution)/shard_map/ike,de->ikd/dot_general | solution.py:305
  455.1 4.4 multiply_convert_fusion.3
  461.2 3.5 collective-permute-start.34
  464.6 2.7 fusion.71
  472.9 11.6 %fusion.11 = (bf16[1024]{0:T(1024)(128)(2,1)S(1)}, f32[8,576]{1,0:T(8,128)S(1)}, f32[8,576]{1,0:T(8,128)S(1)}, bf16[1024]{0:T(1024)(128)(2,1)S(1)}) fusion(bf16[8,576,1024]{2,1,0:T(8,128)(2,1)S(1)} %bitcast.340, f32[8,640,1024]{2,1,0:T(8,128)} %fusion.23, f32[8,576]{1,0:T(8,128)S(1)} %copy-done.56, f32[8,576]{1,0:T(8,128)S(1)} %copy-done.52, ...), kind=kLoop, calls=%fused_computation.13 | loop fusion | flops 47174656 | bytes 28393472 | tf_op jit(solution)/shard_map/reduce_sum | solution.py:33
  484.7 5.9 %fusion.55 = (bf16[1024]{0:T(1024)(128)(2,1)S(1)}, f32[8,64]{1,0:T(8,128)}, f32[8,64]{1,0:T(8,128)}, bf16[1024]{0:T(1024)(128)(2,1)S(1)}, f32[8,64,1024]{2,1,0:T(8,128)}) fusion(bf16[8,64,1024]{2,1,0:T(8,128)(2,1)S(1)} %copy-done.8, f32[8,64]{1,0:T(8,128)S(1)} %copy-done.70, f32[8,64]{1,0:T(8,128)S(1)} %copy-done.59, f32[1024]{0:T(1024)S(1)} %copy-done.67, ...), kind=kOutput, calls=%fused_computation.82 | convolution fusion | flops 542635008 | bytes 6832128 | tf_op jit(solution)/shard_map/ile,de->ild/dot_general | solution.py:306
  495.2 1.7 fusion.83
  500.5 17.6 %fusion.10 = f32[8,576,1024]{2,1,0:T(8,128)} fusion(bf16[8,576,1024]{2,1,0:T(8,128)(2,1)} %param.15, f32[8,640,1024]{2,1,0:T(8,128)} %fusion.23, f32[8,576]{1,0:T(8,128)S(1)} %get-tuple-element.100, f32[8,576]{1,0:T(8,128)S(1)} %copy-done.64, f32[1024]{0:T(1024)S(1)} %copy-done.74, f32[8,576]{1,0:T(8,128)S(1)} %copy-done.56, f32[8,576]{1,0:T(8,128)S(1)} %copy-done.52), kind=kLoop, calls=%fused_computation.12 | loop fusion | flops 37748736 | bytes 47263744 | tf_op jit(solution)/shard_map/mul | solution.py:25
  521.0 6.2 %collective-permute-done.25 = bf16[4,33,1024]{2,0,1:T(4,128)(2,1)S(1)} collective-permute-done((bf16[4,33,1024]{2,0,1:T(4,128)(2,1)S(1)}, bf16[4,33,1024]{2,0,1:T(4,128)(2,1)S(1)}, u32[]{:S(2)}, u32[]{:S(2)}) %collective-permute-start.25) | collective-permute-done | bytes 270368 | tf_op jit(solution)/shard_map/ppermute | solution.py:57
  531.5 5.8 %collective-permute-done.26 = bf16[2,65,1024]{2,0,1:T(2,128)(2,1)S(1)} collective-permute-done((bf16[2,65,1024]{2,0,1:T(2,128)(2,1)S(1)}, bf16[2,65,1024]{2,0,1:T(2,128)(2,1)S(1)}, u32[]{:S(2)}, u32[]{:S(2)}) %collective-permute-start.26) | collective-permute-done | bytes 266272 | tf_op jit(solution)/shard_map/ppermute | solution.py:57
  538.4 12.5 %collective-permute-done.27 = bf16[1,65,1024]{2,0,1:T(2,128)(2,1)S(1)} collective-permute-done((bf16[1,65,1024]{2,0,1:T(2,128)(2,1)S(1)}, bf16[1,65,1024]{2,0,1:T(2,128)(2,1)S(1)}, u32[]{:S(2)}, u32[]{:S(2)}) %collective-permute-start.27) | collective-permute-done | bytes 133152 | tf_op jit(solution)/shard_map/ppermute | solution.py:57
  552.2 2.1 fusion.54
  557.0 1.8 reshape.881
  (434 shorter events, 111.8 us)
Async XLA Ops:
  7.2 159.1 %copy-start = (bf16[256,1024]{1,0:T(8,128)(2,1)S(1)}, bf16[256,1024]{1,0:T(8,128)(2,1)}, u32[]{:S(2)}) copy-start(bf16[256,1024]{1,0:T(8,128)(2,1)} %param.28) | copy-start | bytes 1572868
  7.2 288.8 %all-gather.3.cloned.1.call-start = ((), (), s32[]{:S(2)}) async-start(), calls=%async_computation | async-start | bytes 4456448 | tf_op jit(solution)/shard_map/all_gather | solution.py:223
  11.2 23.2 %collective-permute-start.8 = (bf16[1,144,1024]{2,1,0:T(8,128)(2,1)S(1)}, bf16[1,144,1024]{2,1,0:T(8,128)(2,1)S(1)}, u32[]{:S(2)}, u32[]{:S(2)}) collective-permute-start(bf16[1,144,1024]{2,1,0:T(8,128)(2,1)S(1)} %get-tuple-element.78), channel_id=1, source_target_pairs={{0,16},{2,18},{4,20},{6,22},{8,24},{10,26},{12,28},{14,30},{16,0},... | collective-permute-start | bytes 884744 | tf_op jit(solution)/shard_map/ppermute | solution.py:57
  17.8 15.8 %collective-permute-start = (bf16[1,49,1024]{2,1,0:T(8,128)(2,1)S(1)}, bf16[1,49,1024]{2,1,0:T(8,128)(2,1)S(1)}, u32[]{:S(2)}, u32[]{:S(2)}) collective-permute-start(bf16[1,49,1024]{2,1,0:T(8,128)(2,1)S(1)} %get-tuple-element.82), channel_id=1, source_target_pairs={{0,16},{2,18},{4,20},{6,22},{8,24},{10,26},{12,28},{14,30},{16,0},... | collective-permute-start | bytes 301064 | tf_op jit(solution)/shard_map/ppermute | solution.py:57
  18.1 60.9 %copy-start.57 = (f32[8,64]{1,0:T(8,128)}, f32[8,64]{1,0:T(8,128)S(1)}, u32[]{:S(2)}) copy-start(f32[8,64]{1,0:T(8,128)S(1)} %broadcast_multiply_fusion.7) | copy-start | bytes 6148
  18.6 60.5 %copy-start.68 = (f32[8,64]{1,0:T(8,128)}, f32[8,64]{1,0:T(8,128)S(1)}, u32[]{:S(2)}) copy-start(f32[8,64]{1,0:T(8,128)S(1)} %add_rsqrt_fusion.2) | copy-start | bytes 6148
  24.9 32.8 %copy-start.51 = (f32[8,576]{1,0:T(8,128)}, f32[8,576]{1,0:T(8,128)S(1)}, u32[]{:S(2)}) copy-start(f32[8,576]{1,0:T(8,128)S(1)} %broadcast_multiply_fusion.2) | copy-start | bytes 55300
  27.6 30.1 %copy-start.55 = (f32[8,576]{1,0:T(8,128)}, f32[8,576]{1,0:T(8,128)S(1)}, u32[]{:S(2)}) copy-start(f32[8,576]{1,0:T(8,128)S(1)} %add_rsqrt_fusion) | copy-start | bytes 55300
  27.7 129.7 %copy-start.53 = (pred[8,640]{1,0:T(8,128)(4,1)}, pred[8,640]{1,0:T(8,128)(4,1)S(1)}, u32[]{:S(2)}) copy-start(pred[8,640]{1,0:T(8,128)(4,1)S(1)} %fusion.96) | copy-start | bytes 15364
  33.6 8.6 %collective-permute-start.1 = (bf16[2,49,1024]{2,1,0:T(8,128)(2,1)S(1)}, bf16[2,49,1024]{2,1,0:T(8,128)(2,1)S(1)}, u32[]{:S(2)}, u32[]{:S(2)}) collective-permute-start(bf16[2,49,1024]{2,1,0:T(8,128)(2,1)S(1)} %maximum_select_fusion.22), channel_id=1, source_target_pairs={{0,8},{2,10},{4,12},{6,14},{8,0},{10,2},{12,4},{14,6},{16,24},{18,... | collective-permute-start | bytes 602120 | tf_op jit(solution)/shard_map/ppermute | solution.py:57
  35.4 33.3 %collective-permute-start.9 = (bf16[2,144,1024]{2,1,0:T(8,128)(2,1)}, bf16[2,144,1024]{2,1,0:T(8,128)(2,1)}, u32[]{:S(2)}, u32[]{:S(2)}) collective-permute-start(bf16[2,144,1024]{2,1,0:T(8,128)(2,1)} %maximum_select_fusion.13), channel_id=1, source_target_pairs={{0,8},{2,10},{4,12},{6,14},{8,0},{10,2},{12,4},{14,6},{16,24},{18,... | collective-permute-start | bytes 1769480 | tf_op jit(solution)/shard_map/ppermute | solution.py:57
  42.4 5.1 collective-permute-start.2
  44.1 8.0 %collective-permute-start.4 = (bf16[4,32,1024]{2,1,0:T(8,128)(2,1)S(1)}, bf16[4,32,1024]{2,1,0:T(8,128)(2,1)S(1)}, u32[]{:S(2)}, u32[]{:S(2)}) collective-permute-start(bf16[4,32,1024]{2,1,0:T(8,128)(2,1)S(1)} %get-tuple-element.75), channel_id=1, source_target_pairs={{0,4},{2,6},{4,0},{6,2},{8,12},{10,14},{12,8},{14,10},{16,20},{18,... | collective-permute-start | bytes 786440 | tf_op jit(solution)/shard_map/ppermute | solution.py:57
  47.8 7.3 %collective-permute-start.3 = (bf16[4,2,17,1024]{3,0,2,1:T(4,128)(2,1)S(1)}, bf16[4,2,17,1024]{3,0,2,1:T(4,128)(2,1)S(1)}, u32[]{:S(2)}, u32[]{:S(2)}) collective-permute-start(bf16[4,2,17,1024]{3,0,2,1:T(4,128)(2,1)S(1)} %maximum_select_fusion.20), channel_id=1, source_target_pairs={{0,4},{2,6},{4,0},{6,2},{8,12},{10,14},{12,8},{14,10},{16,20},{18,... | collective-permute-start | bytes 835592 | tf_op jit(solution)/shard_map/ppermute | solution.py:57
  53.0 22.6 %collective-permute-start.5 = (bf16[4,2,32,1024]{3,2,0,1:T(8,128)(2,1)}, bf16[4,2,32,1024]{3,2,0,1:T(8,128)(2,1)}, u32[]{:S(2)}, u32[]{:S(2)}) collective-permute-start(bf16[4,2,32,1024]{3,2,0,1:T(8,128)(2,1)} %maximum_select_fusion.17), channel_id=1, source_target_pairs={{0,2},{2,0},{4,6},{6,4},{8,10},{10,8},{12,14},{14,12},{16,18},{18,... | collective-permute-start | bytes 1572872 | tf_op jit(solution)/shard_map/ppermute | solution.py:57
  57.4 23.2 %collective-permute-start.7 = (bf16[16,32,512]{2,0,1:T(8,128)(2,1)}, bf16[16,32,512]{2,0,1:T(8,128)(2,1)}, u32[]{:S(2)}, u32[]{:S(2)}) collective-permute-start(bf16[16,32,512]{2,0,1:T(8,128)(2,1)} %get-tuple-element.72), channel_id=1, source_target_pairs={{0,1},{1,0},{2,3},{3,2},{4,5},{5,4},{6,7},{7,6},{8,9},{9,8},{10,11... | collective-permute-start | bytes 1572872 | tf_op jit(solution)/shard_map/ppermute | solution.py:114
  72.8 19.1 %collective-permute-start.10 = (bf16[4,80,1024]{2,1,0:T(8,128)(2,1)}, bf16[4,80,1024]{2,1,0:T(8,128)(2,1)}, u32[]{:S(2)}, u32[]{:S(2)}) collective-permute-start(bf16[4,80,1024]{2,1,0:T(8,128)(2,1)} %get-tuple-element.56), channel_id=1, source_target_pairs={{0,2},{2,0},{4,6},{6,4},{8,10},{10,8},{12,14},{14,12},{16,18},{18,... | collective-permute-start | bytes 1966088 | tf_op jit(solution)/shard_map/ppermute | solution.py:57
  74.1 14.4 %collective-permute-start.14 = (bf16[4,64,1024]{2,1,0:T(8,128)(2,1)}, bf16[4,64,1024]{2,1,0:T(8,128)(2,1)}, u32[]{:S(2)}, u32[]{:S(2)}) collective-permute-start(bf16[4,64,1024]{2,1,0:T(8,128)(2,1)} %get-tuple-element.53), channel_id=1, source_target_pairs={{0,4},{2,6},{4,0},{6,2},{8,12},{10,14},{12,8},{14,10},{16,20},{18,... | collective-permute-start | bytes 1572872 | tf_op jit(solution)/shard_map/ppermute | solution.py:57
  79.0 19.9 %collective-permute-start.6 = (bf16[16,32,1024]{2,1,0:T(8,128)(2,1)}, bf16[16,32,1024]{2,1,0:T(8,128)(2,1)}, u32[]{:S(2)}, u32[]{:S(2)}) collective-permute-start(bf16[16,32,1024]{2,1,0:T(8,128)(2,1)} %bitcast.28), channel_id=1, source_target_pairs={{0,1},{1,0},{2,3},{3,2},{4,5},{5,4},{6,7},{7,6},{8,9},{9,8},{10,11... | collective-permute-start | bytes 3145736 | tf_op jit(solution)/shard_map/ppermute | solution.py:114
  80.6 83.4 %copy-start.60 = (f32[1024]{0:T(1024)}, f32[1024]{0:T(1024)S(1)}, u32[]{:S(2)}) copy-start(f32[1024]{0:T(1024)S(1)} %mul.216) | copy-start | bytes 12292
  86.7 58.8 %copy-start.10 = (bf16[8,64,512]{1,2,0:T(8,128)(2,1)}, bf16[8,64,512]{1,2,0:T(8,128)(2,1)S(1)}, u32[]{:S(2)}) copy-start(bf16[8,64,512]{1,2,0:T(8,128)(2,1)S(1)} %copy.293) | copy-start | bytes 1572868
  91.1 77.3 %collective-permute-start.15 = (bf16[4,2,64,1024]{3,2,0,1:T(8,128)(2,1)}, bf16[4,2,64,1024]{3,2,0,1:T(8,128)(2,1)}, u32[]{:S(2)}, u32[]{:S(2)}) collective-permute-start(bf16[4,2,64,1024]{3,2,0,1:T(8,128)(2,1)} %maximum_select_fusion.9), channel_id=1, source_target_pairs={{0,2},{2,0},{4,6},{6,4},{8,10},{10,8},{12,14},{14,12},{16,18},{18,... | collective-permute-start | bytes 3145736 | tf_op jit(solution)/shard_map/ppermute | solution.py:57
  94.9 57.8 %collective-permute-start.11 = (bf16[4,2,80,1024]{3,2,0,1:T(8,128)(2,1)}, bf16[4,2,80,1024]{3,2,0,1:T(8,128)(2,1)}, u32[]{:S(2)}, u32[]{:S(2)}) collective-permute-start(bf16[4,2,80,1024]{3,2,0,1:T(8,128)(2,1)} %maximum_select_fusion.3), channel_id=1, source_target_pairs={{0,4},{2,6},{4,0},{6,2},{8,12},{10,14},{12,8},{14,10},{16,20},{18,... | collective-permute-start | bytes 3932168 | tf_op jit(solution)/shard_map/ppermute | solution.py:57
  157.4 4.1 collective-permute-start.12
  164.5 6.5 %collective-permute-start.13 = (bf16[512,1024]{1,0:T(8,128)(2,1)S(1)}, bf16[512,1024]{1,0:T(8,128)(2,1)}, u32[]{:S(2)}, u32[]{:S(2)}) collective-permute-start(bf16[512,1024]{1,0:T(8,128)(2,1)S(1)} %bitcast.392), channel_id=1, source_target_pairs={{0,1},{1,0},{2,3},{3,2},{4,5},{5,4},{6,7},{7,6},{8,9},{9,8},{10,11... | collective-permute-start | bytes 3145736 | tf_op jit(solution)/shard_map/ppermute | solution.py:114
  166.2 32.5 %collective-permute-start.17 = (bf16[512,1024]{1,0:T(8,128)(2,1)}, bf16[512,1024]{1,0:T(8,128)(2,1)}, u32[]{:S(2)}, u32[]{:S(2)}) collective-permute-start(bf16[512,1024]{1,0:T(8,128)(2,1)} %bitcast.71), channel_id=1, source_target_pairs={{0,1},{1,0},{2,3},{3,2},{4,5},{5,4},{6,7},{7,6},{8,9},{9,8},{10,11... | collective-permute-start | bytes 3145736 | tf_op jit(solution)/shard_map/ppermute | solution.py:114
  170.8 27.9 %copy-start.35 = (bf16[4,2,2,64,1024]{4,3,2,1,0:T(8,128)(2,1)}, bf16[4,2,2,64,1024]{4,3,2,1,0:T(8,128)(2,1)S(1)}, u32[]{:S(2)}) copy-start(bf16[4,2,2,64,1024]{4,3,2,1,0:T(8,128)(2,1)S(1)} %copy.246) | copy-start | bytes 6291460
  171.0 27.7 %copy-start.37 = (bf16[16,64,1024]{2,1,0:T(8,128)(2,1)}, bf16[16,64,1024]{2,1,0:T(8,128)(2,1)S(1)}, u32[]{:S(2)}) copy-start(bf16[16,64,1024]{2,1,0:T(8,128)(2,1)S(1)} %slice.238) | copy-start | bytes 6291460
  210.0 40.5 %collective-permute-start.36 = (bf16[4,2,64,1024]{3,2,1,0:T(8,128)(2,1)S(1)}, bf16[4,2,64,1024]{3,2,1,0:T(8,128)(2,1)}, u32[]{:S(2)}, u32[]{:S(2)}) collective-permute-start(bf16[4,2,64,1024]{3,2,1,0:T(8,128)(2,1)S(1)} %dynamic-slice_bitcast_fusion), channel_id=1, source_target_pairs={{0,2},{2,0},{4,6},{6,4},{8,10},{10,8},{12,14},{14,12},{16,18},{18,... | collective-permute-start | bytes 3145736 | tf_op jit(solution)/shard_map/ppermute | solution.py:57
  211.3 39.2 %copy-start.23 = (bf16[16,64,1024]{2,1,0:T(8,128)(2,1)S(1)}, bf16[16,64,1024]{2,1,0:T(8,128)(2,1)}, u32[]{:S(2)}) copy-start(bf16[16,64,1024]{2,1,0:T(8,128)(2,1)} %copy-done.22) | copy-start | bytes 6291460
  213.3 40.1 %collective-permute-start.38 = (bf16[4,2,64,1024]{3,2,0,1:T(8,128)(2,1)S(1)}, bf16[4,2,64,1024]{3,2,0,1:T(8,128)(2,1)S(1)}, u32[]{:S(2)}, u32[]{:S(2)}) collective-permute-start(bf16[4,2,64,1024]{3,2,0,1:T(8,128)(2,1)S(1)} %bitcast.399), channel_id=1, source_target_pairs={{0,4},{2,6},{4,0},{6,2},{8,12},{10,14},{12,8},{14,10},{16,20},{18,... | collective-permute-start | bytes 3145736 | tf_op jit(solution)/shard_map/ppermute | solution.py:57
  252.2 13.5 %collective-permute-start.37 = (bf16[4,64,1024]{2,1,0:T(8,128)(2,1)S(1)}, bf16[4,64,1024]{2,1,0:T(8,128)(2,1)S(1)}, u32[]{:S(2)}, u32[]{:S(2)}) collective-permute-start(bf16[4,64,1024]{2,1,0:T(8,128)(2,1)S(1)} %dynamic-slice_bitcast_fusion.4), channel_id=1, source_target_pairs={{0,4},{2,6},{4,0},{6,2},{8,12},{10,14},{12,8},{14,10},{16,20},{18,... | collective-permute-start | bytes 1572872 | tf_op jit(solution)/shard_map/ppermute | solution.py:57
  254.7 13.5 %collective-permute-start.39 = (bf16[4,64,1024]{2,1,0:T(8,128)(2,1)}, bf16[4,64,1024]{2,1,0:T(8,128)(2,1)}, u32[]{:S(2)}, u32[]{:S(2)}) collective-permute-start(bf16[4,64,1024]{2,1,0:T(8,128)(2,1)} %dynamic-slice_bitcast_fusion.3), channel_id=1, source_target_pairs={{0,2},{2,0},{4,6},{6,4},{8,10},{10,8},{12,14},{14,12},{16,18},{18,... | collective-permute-start | bytes 1572872 | tf_op jit(solution)/shard_map/ppermute | solution.py:57
  255.4 30.4 %copy-start.58 = (f32[8,64]{1,0:T(8,128)S(1)}, f32[8,64]{1,0:T(8,128)}, u32[]{:S(2)}) copy-start(f32[8,64]{1,0:T(8,128)} %copy-done.57) | copy-start | bytes 6148
  255.4 30.4 %copy-start.66 = (f32[1024]{0:T(1024)S(1)}, f32[1024]{0:T(1024)}, u32[]{:S(2)}) copy-start(f32[1024]{0:T(1024)} %copy-done.65) | copy-start | bytes 12292
  255.4 30.4 %copy-start.69 = (f32[8,64]{1,0:T(8,128)S(1)}, f32[8,64]{1,0:T(8,128)}, u32[]{:S(2)}) copy-start(f32[8,64]{1,0:T(8,128)} %copy-done.68) | copy-start | bytes 6148
  255.4 30.4 %copy-start.76 = (f32[1024]{0:T(1024)S(1)}, f32[1024]{0:T(1024)}, u32[]{:S(2)}) copy-start(f32[1024]{0:T(1024)} %copy-done.75) | copy-start | bytes 12292
  269.5 12.5 %collective-permute-start.40 = (bf16[2,128,1024]{2,1,0:T(8,128)(2,1)S(1)}, bf16[2,128,1024]{2,1,0:T(8,128)(2,1)S(1)}, u32[]{:S(2)}, u32[]{:S(2)}) collective-permute-start(bf16[2,128,1024]{2,1,0:T(8,128)(2,1)S(1)} %dynamic-slice_bitcast_fusion.2), channel_id=1, source_target_pairs={{0,8},{2,10},{4,12},{6,14},{8,0},{10,2},{12,4},{14,6},{16,24},{18,... | collective-permute-start | bytes 1572872 | tf_op jit(solution)/shard_map/ppermute | solution.py:57
  282.2 13.5 %collective-permute-start.41 = (bf16[1,128,1024]{2,1,0:T(8,128)(2,1)S(1)}, bf16[1,128,1024]{2,1,0:T(8,128)(2,1)S(1)}, u32[]{:S(2)}, u32[]{:S(2)}) collective-permute-start(bf16[1,128,1024]{2,1,0:T(8,128)(2,1)S(1)} %constant_dynamic-slice_fusion), channel_id=1, source_target_pairs={{0,16},{2,18},{4,20},{6,22},{8,24},{10,26},{12,28},{14,30},{16,0},... | collective-permute-start | bytes 786440 | tf_op jit(solution)/shard_map/ppermute | solution.py:57
  295.9 54.2 %collective-permute-start.42 = (f32[128,1024]{1,0:T(8,128)S(1)}, f32[128,1024]{1,0:T(8,128)S(1)}, u32[]{:S(2)}, u32[]{:S(2)}) collective-permute-start(f32[128,1024]{1,0:T(8,128)S(1)} %get-tuple-element.64), channel_id=1, source_target_pairs={{0,1},{1,0},{2,3},{3,2},{4,5},{5,4},{6,7},{7,6},{8,9},{9,8},{10,11... | collective-permute-start | bytes 1572872 | tf_op jit(solution)/shard_map/ppermute | solution.py:114
  314.8 25.6 %collective-permute-start.29 = (bf16[4,2,64,1024]{3,2,0,1:T(8,128)(2,1)S(1)}, bf16[4,2,64,1024]{3,2,0,1:T(8,128)(2,1)S(1)}, u32[]{:S(2)}, u32[]{:S(2)}) collective-permute-start(bf16[4,2,64,1024]{3,2,0,1:T(8,128)(2,1)S(1)} %bitcast.398), channel_id=1, source_target_pairs={{0,2},{2,0},{4,6},{6,4},{8,10},{10,8},{12,14},{14,12},{16,18},{18,... | collective-permute-start | bytes 3145736 | tf_op jit(solution)/shard_map/ppermute | solution.py:57
  315.8 25.9 %collective-permute-start.31 = (bf16[4,2,64,1024]{3,2,1,0:T(8,128)(2,1)S(1)}, bf16[4,2,64,1024]{3,2,1,0:T(8,128)(2,1)S(1)}, u32[]{:S(2)}, u32[]{:S(2)}) collective-permute-start(bf16[4,2,64,1024]{3,2,1,0:T(8,128)(2,1)S(1)} %dynamic-slice_bitcast_fusion.1), channel_id=1, source_target_pairs={{0,4},{2,6},{4,0},{6,2},{8,12},{10,14},{12,8},{14,10},{16,20},{18,... | collective-permute-start | bytes 3145736 | tf_op jit(solution)/shard_map/ppermute | solution.py:57
  321.4 36.2 %collective-permute-start.18 = (f32[512,1024]{1,0:T(8,128)S(1)}, f32[512,1024]{1,0:T(8,128)S(1)}, u32[]{:S(2)}, u32[]{:S(2)}) collective-permute-start(f32[512,1024]{1,0:T(8,128)S(1)} %slice.242), channel_id=1, source_target_pairs={{0,1},{1,0},{2,3},{3,2},{4,5},{5,4},{6,7},{7,6},{8,9},{9,8},{10,11... | collective-permute-start | bytes 6291464 | tf_op jit(solution)/shard_map/ppermute | solution.py:114
  340.9 13.5 %collective-permute-start.30 = (bf16[4,64,1024]{2,1,0:T(8,128)(2,1)S(1)}, bf16[4,64,1024]{2,1,0:T(8,128)(2,1)S(1)}, u32[]{:S(2)}, u32[]{:S(2)}) collective-permute-start(bf16[4,64,1024]{2,1,0:T(8,128)(2,1)S(1)} %dynamic-slice_bitcast_fusion.7), channel_id=1, source_target_pairs={{0,4},{2,6},{4,0},{6,2},{8,12},{10,14},{12,8},{14,10},{16,20},{18,... | collective-permute-start | bytes 1572872 | tf_op jit(solution)/shard_map/ppermute | solution.py:57
  342.3 13.3 %collective-permute-start.32 = (bf16[4,64,1024]{2,1,0:T(8,128)(2,1)S(1)}, bf16[4,64,1024]{2,1,0:T(8,128)(2,1)S(1)}, u32[]{:S(2)}, u32[]{:S(2)}) collective-permute-start(bf16[4,64,1024]{2,1,0:T(8,128)(2,1)S(1)} %dynamic-slice_bitcast_fusion.6), channel_id=1, source_target_pairs={{0,2},{2,0},{4,6},{6,4},{8,10},{10,8},{12,14},{14,12},{16,18},{18,... | collective-permute-start | bytes 1572872 | tf_op jit(solution)/shard_map/ppermute | solution.py:57
  350.1 12.9 %collective-permute-start.16 = (f32[512,1024]{1,0:T(8,128)}, f32[512,1024]{1,0:T(8,128)}, u32[]{:S(2)}, u32[]{:S(2)}) collective-permute-start(f32[512,1024]{1,0:T(8,128)} %slice.240), channel_id=1, source_target_pairs={{0,1},{1,0},{2,3},{3,2},{4,5},{5,4},{6,7},{7,6},{8,9},{9,8},{10,11... | collective-permute-start | bytes 6291464 | tf_op jit(solution)/shard_map/ppermute | solution.py:114
  356.9 102.6 %collective-permute-start.33 = (bf16[2,128,1024]{2,1,0:T(8,128)(2,1)S(1)}, bf16[2,128,1024]{2,1,0:T(8,128)(2,1)}, u32[]{:S(2)}, u32[]{:S(2)}) collective-permute-start(bf16[2,128,1024]{2,1,0:T(8,128)(2,1)S(1)} %dynamic-slice_bitcast_fusion.5), channel_id=1, source_target_pairs={{0,8},{2,10},{4,12},{6,14},{8,0},{10,2},{12,4},{14,6},{16,24},{18,... | collective-permute-start | bytes 1572872 | tf_op jit(solution)/shard_map/ppermute | solution.py:57
  369.7 15.9 %slice-start = ((s8[10485760]{0:T(1024)(128)(4,1)}), s8[2097152]{0:T(1024)(128)(4,1)S(1)}, s32[]{:S(2)}) async-start(s8[10485760]{0:T(1024)(128)(4,1)} %bitcast.337), calls=%async_computation.1 | async-start | bytes 4194304
  416.1 38.9 %slice-start.6 = ((s8[5242880]{0:T(1024)(128)(4,1)}), s8[1048576]{0:T(1024)(128)(4,1)S(1)}, s32[]{:S(2)}) async-start(s8[5242880]{0:T(1024)(128)(4,1)} %bitcast.341), calls=%async_computation.7 | async-start | bytes 2097152
  436.0 19.0 %slice-start.7 = ((s8[5242880]{0:T(1024)(128)(4,1)}), s8[4194304]{0:T(1024)(128)(4,1)S(1)}, s32[]{:S(2)}) async-start(s8[5242880]{0:T(1024)(128)(4,1)} %bitcast.341), calls=%async_computation.8 | async-start | bytes 8388608
  461.2 69.0 %collective-permute-start.34 = (bf16[1,128,1024]{2,1,0:T(8,128)(2,1)S(1)}, bf16[1,128,1024]{2,1,0:T(8,128)(2,1)}, u32[]{:S(2)}, u32[]{:S(2)}) collective-permute-start(bf16[1,128,1024]{2,1,0:T(8,128)(2,1)S(1)} %constant_dynamic-slice_fusion.3), channel_id=1, source_target_pairs={{0,16},{2,18},{4,20},{6,22},{8,24},{10,26},{12,28},{14,30},{16,0},... | collective-permute-start | bytes 786440 | tf_op jit(solution)/shard_map/ppermute | solution.py:57
  467.4 31.4 %collective-permute-start.19 = (bf16[16,32,1024]{2,1,0:T(8,128)(2,1)}, bf16[16,32,1024]{2,1,0:T(8,128)(2,1)S(1)}, u32[]{:S(2)}, u32[]{:S(2)}) collective-permute-start(bf16[16,32,1024]{2,1,0:T(8,128)(2,1)} %fusion.71), channel_id=1, source_target_pairs={{0,1},{1,0},{2,3},{3,2},{4,5},{5,4},{6,7},{7,6},{8,9},{9,8},{10,11... | collective-permute-start | bytes 3145736 | tf_op jit(solution)/shard_map/ppermute | solution.py:114
  468.8 24.8 %collective-permute-start.22 = (bf16[16,32,512]{2,1,0:T(8,128)(2,1)S(1)}, bf16[16,32,512]{2,1,0:T(8,128)(2,1)}, u32[]{:S(2)}, u32[]{:S(2)}) collective-permute-start(bf16[16,32,512]{2,1,0:T(8,128)(2,1)S(1)} %fusion.87), channel_id=1, source_target_pairs={{0,1},{1,0},{2,3},{3,2},{4,5},{5,4},{6,7},{7,6},{8,9},{9,8},{10,11... | collective-permute-start | bytes 1572872 | tf_op jit(solution)/shard_map/ppermute | solution.py:114
  472.4 22.8 %collective-permute-start.23 = (bf16[16,16,1024]{2,1,0:T(8,128)(2,1)}, bf16[16,16,1024]{2,1,0:T(8,128)(2,1)}, u32[]{:S(2)}, u32[]{:S(2)}) collective-permute-start(bf16[16,16,1024]{2,1,0:T(8,128)(2,1)} %fusion.88), channel_id=1, source_target_pairs={{0,1},{1,0},{2,3},{3,2},{4,5},{5,4},{6,7},{7,6},{8,9},{9,8},{10,11... | collective-permute-start | bytes 1572872 | tf_op jit(solution)/shard_map/ppermute | solution.py:114
  497.7 20.5 %collective-permute-start.24 = (bf16[4,2,33,1024]{3,0,2,1:T(4,128)(2,1)S(1)}, bf16[4,2,33,1024]{3,0,2,1:T(4,128)(2,1)S(1)}, u32[]{:S(2)}, u32[]{:S(2)}) collective-permute-start(bf16[4,2,33,1024]{3,0,2,1:T(4,128)(2,1)S(1)} %bitcast.413), channel_id=1, source_target_pairs={{0,4},{2,6},{4,0},{6,2},{8,12},{10,14},{12,8},{14,10},{16,20},{18,... | collective-permute-start | bytes 1622024 | tf_op jit(solution)/shard_map/ppermute | solution.py:57
  499.3 20.5 %collective-permute-start.20 = (bf16[4,2,32,1024]{3,2,1,0:T(8,128)(2,1)S(1)}, bf16[4,2,32,1024]{3,2,1,0:T(8,128)(2,1)S(1)}, u32[]{:S(2)}, u32[]{:S(2)}) collective-permute-start(bf16[4,2,32,1024]{3,2,1,0:T(8,128)(2,1)S(1)} %dynamic-slice_bitcast_fusion.8), channel_id=1, source_target_pairs={{0,2},{2,0},{4,6},{6,4},{8,10},{10,8},{12,14},{14,12},{16,18},{18,... | collective-permute-start | bytes 1572872 | tf_op jit(solution)/shard_map/ppermute | solution.py:57
  518.8 8.4 %collective-permute-start.25 = (bf16[4,33,1024]{2,0,1:T(4,128)(2,1)S(1)}, bf16[4,33,1024]{2,0,1:T(4,128)(2,1)S(1)}, u32[]{:S(2)}, u32[]{:S(2)}) collective-permute-start(bf16[4,33,1024]{2,0,1:T(4,128)(2,1)S(1)} %dynamic-slice_bitcast_fusion.9), channel_id=1, source_target_pairs={{0,2},{2,0},{4,6},{6,4},{8,10},{10,8},{12,14},{14,12},{16,18},{18,... | collective-permute-start | bytes 811016 | tf_op jit(solution)/shard_map/ppermute | solution.py:57
  520.0 8.0 %collective-permute-start.21 = (bf16[4,32,1024]{2,1,0:T(8,128)(2,1)S(1)}, bf16[4,32,1024]{2,1,0:T(8,128)(2,1)S(1)}, u32[]{:S(2)}, u32[]{:S(2)}) collective-permute-start(bf16[4,32,1024]{2,1,0:T(8,128)(2,1)S(1)} %dynamic-slice_bitcast_fusion.10), channel_id=1, source_target_pairs={{0,4},{2,6},{4,0},{6,2},{8,12},{10,14},{12,8},{14,10},{16,20},{18,... | collective-permute-start | bytes 786440 | tf_op jit(solution)/shard_map/ppermute | solution.py:57
  529.8 22.4 %copy-start.14 = (f32[8,64,1024]{2,1,0:T(8,128)S(1)}, f32[8,64,1024]{2,1,0:T(8,128)}, u32[]{:S(2)}) copy-start(f32[8,64,1024]{2,1,0:T(8,128)} %copy-done.12) | copy-start | bytes 6291460
  529.8 22.4 %copy-start.31 = (f32[8,64,1024]{2,1,0:T(8,128)S(1)}, f32[8,64,1024]{2,1,0:T(8,128)}, u32[]{:S(2)}) copy-start(f32[8,64,1024]{2,1,0:T(8,128)} %get-tuple-element.99) | copy-start | bytes 6291460
  530.1 7.2 %collective-permute-start.26 = (bf16[2,65,1024]{2,0,1:T(2,128)(2,1)S(1)}, bf16[2,65,1024]{2,0,1:T(2,128)(2,1)S(1)}, u32[]{:S(2)}, u32[]{:S(2)}) collective-permute-start(bf16[2,65,1024]{2,0,1:T(2,128)(2,1)S(1)} %bitcast.419), channel_id=1, source_target_pairs={{0,8},{2,10},{4,12},{6,14},{8,0},{10,2},{12,4},{14,6},{16,24},{18,... | collective-permute-start | bytes 798728 | tf_op jit(solution)/shard_map/ppermute | solution.py:57
  538.0 12.8 %collective-permute-start.27 = (bf16[1,65,1024]{2,0,1:T(2,128)(2,1)S(1)}, bf16[1,65,1024]{2,0,1:T(2,128)(2,1)S(1)}, u32[]{:S(2)}, u32[]{:S(2)}) collective-permute-start(bf16[1,65,1024]{2,0,1:T(2,128)(2,1)S(1)} %constant_dynamic-slice_fusion.6), channel_id=1, source_target_pairs={{0,16},{2,18},{4,20},{6,22},{8,24},{10,26},{12,28},{14,30},{16,0},... | collective-permute-start | bytes 399368 | tf_op jit(solution)/shard_map/ppermute | solution.py:57
  538.3 16.6 %collective-permute-start.35 = (f32[64,2048]{1,0:T(8,128)S(1)}, f32[64,2048]{1,0:T(8,128)S(1)}, u32[]{:S(2)}, u32[]{:S(2)}) collective-permute-start(f32[64,2048]{1,0:T(8,128)S(1)} %pad_maximum_fusion.21), channel_id=1, source_target_pairs={{0,1},{1,0},{2,3},{3,2},{4,5},{5,4},{6,7},{7,6},{8,9},{9,8},{10,11... | collective-permute-start | bytes 1572872 | tf_op jit(solution)/shard_map/ppermute | solution.py:114
  552.2 6.6 %collective-permute-start.28 = (f32[65,1024]{1,0:T(8,128)}, f32[65,1024]{1,0:T(8,128)}, u32[]{:S(2)}, u32[]{:S(2)}) collective-permute-start(f32[65,1024]{1,0:T(8,128)} %get-tuple-element.77), channel_id=1, source_target_pairs={{0,1},{1,0},{2,3},{3,2},{4,5},{5,4},{6,7},{7,6},{8,9},{9,8},{10,11... | collective-permute-start | bytes 798728 | tf_op jit(solution)/shard_map/ppermute | solution.py:114
  (75 other events, 411.3 us)
Sparse Core Ops, SparseCore 0:
  167.1 92.1 all-gather.2

commit v2 on v1

v2 whole, which is shorter than its diff:
```python
import functools
import math

import jax
import jax.numpy as jnp
from jax import lax
from jax.experimental import pallas as pl
from jax.experimental.pallas import tpu as pltpu
from jax.sharding import PartitionSpec as P

HEADS = 8
GROUP = 4
EPS = 1e-05
NEG = -1e30
ROWS = 64
FF_TILE = 512
FF_ROWS = 1024
F32 = jnp.float32
BF16 = jnp.bfloat16


def contract(a, b, over):
    return lax.dot_general(a, b, ((over[:1], over[1:]), ((), ())), preferred_element_type=F32)


def norm_rows(values):
    centred = values - jnp.mean(values, -1, keepdims=True)
    inverse = lax.rsqrt(jnp.mean(centred * centred, -1, keepdims=True) + EPS)
    return centred * inverse, inverse


def norm_back(grad, unit, inverse, gain):
    scaled = grad * gain
    return inverse * (
        scaled
        - jnp.mean(scaled, -1, keepdims=True)
        - unit * jnp.mean(scaled * unit, -1, keepdims=True)
    )


def spread(value, size):
    lane = lax.broadcasted_iota(jnp.int32, value.shape, 1) // size
    value = value.astype(F32)
    return jnp.concatenate([jnp.where(lane == h, value, 0.0) for h in range(GROUP)], 0)


def gathered(value, size):
    rows = value.shape[0] // GROUP
    lane = lax.broadcasted_iota(jnp.int32, (rows, value.shape[1]), 1) // size
    out = jnp.zeros((rows, value.shape[1]), F32)
    for h in range(GROUP):
        out = jnp.where(lane == h, value[h * rows : (h + 1) * rows], out)
    return out


def params(mib):
    return pltpu.CompilerParams(vmem_limit_bytes=mib << 20)


def image_at(i, c):
    return (i, 0, 0)


def fixed_at(*_):
    return (0, 0)


def attend_kernel(counts, media, latent, norms, w_kv, w_q, key_input, keyvals, queries, mixed):
    media_len, lat_len = media.shape[1], latent.shape[1]
    keys_len = media_len + lat_len
    inner = w_q.shape[1]
    size = inner // HEADS
    wide = size * GROUP
    for at in range(0, media_len, ROWS):
        unit, _ = norm_rows(media[0, at : at + ROWS, :].astype(F32))
        key_input[0, at : at + ROWS, :] = (unit * norms[0:1, :] + norms[1:2, :]).astype(BF16)
    unit, _ = norm_rows(latent[0].astype(F32))
    low = (unit * norms[2:3, :] + norms[3:4, :]).astype(BF16)
    key_input[0, media_len:, :] = low
    query = contract(low, w_q[...], (1, 0)).astype(BF16)
    queries[0] = query
    keyvals[0] = contract(key_input[0], w_kv[...], (1, 0)).astype(BF16)
    key_at = lax.broadcasted_iota(jnp.int32, (1, keys_len), 1)
    valid = (key_at < counts[pl.program_id(0)]) | (key_at >= media_len)
    for at in range(0, inner, wide):
        own = spread(query[:, at : at + wide].astype(F32) * (1.0 / math.sqrt(size)), size)
        scores = contract(own.astype(BF16), keyvals[0, :, at : at + wide], (1, 1))
        scores = jnp.where(valid, scores, NEG)
        expd = jnp.exp(scores - jnp.max(scores, -1, keepdims=True))
        probs = (expd * (1.0 / jnp.sum(expd, -1, keepdims=True))).astype(BF16)
        out = contract(probs, keyvals[0, :, inner + at : inner + at + wide], (1, 0))
        mixed[0, :, at : at + wide] = gathered(out, size).astype(BF16)


def attend(counts, media, latent, norms, w_kv, w_q):
    images, media_len, width = media.shape
    lat_len, inner = latent.shape[1], w_q.shape[1]
    keys_len = media_len + lat_len
    flops = 2 * images * (keys_len * width * 2 * inner + lat_len * width * inner)
    return pl.pallas_call(
        attend_kernel,
        grid_spec=pltpu.PrefetchScalarGridSpec(
            num_scalar_prefetch=1,
            grid=(images,),
            in_specs=[
                pl.BlockSpec((1, media_len, width), image_at),
                pl.BlockSpec((1, lat_len, width), image_at),
                pl.BlockSpec(norms.shape, fixed_at),
                pl.BlockSpec(w_kv.shape, fixed_at),
                pl.BlockSpec(w_q.shape, fixed_at),
            ],
            out_specs=[
                pl.BlockSpec((1, keys_len, width), image_at),
                pl.BlockSpec((1, keys_len, 2 * inner), image_at),
                pl.BlockSpec((1, lat_len, inner), image_at),
                pl.BlockSpec((1, lat_len, inner), image_at),
            ],
        ),
        out_shape=[
            jax.ShapeDtypeStruct((images, keys_len, width), BF16),
            jax.ShapeDtypeStruct((images, keys_len, 2 * inner), BF16),
            jax.ShapeDtypeStruct((images, lat_len, inner), BF16),
            jax.ShapeDtypeStruct((images, lat_len, inner), BF16),
        ],
        compiler_params=params(32),
        cost_estimate=pl.CostEstimate(
            flops=2 * flops, bytes_accessed=images * keys_len * width * 6, transcendentals=0
        ),
        name="attend",
    )(counts, media, latent, norms, w_kv, w_q)


def resid_kernel(mixed, latent, w_o, norms, resid, low):
    value = latent[...].astype(F32) + contract(mixed[...], w_o[...], (1, 0))
    resid[...] = value
    unit, _ = norm_rows(value)
    low[...] = (unit * norms[4:5, :] + norms[5:6, :]).astype(BF16)


def add_branch(mixed, latent, w_o, norms):
    rows, width = latent.shape
    inner = mixed.shape[1]
    block = rows // 4
    row_at = lambda i: (i, 0)
    return pl.pallas_call(
        resid_kernel,
        grid=(rows // block,),
        in_specs=[
            pl.BlockSpec((block, inner), row_at),
            pl.BlockSpec((block, width), row_at),
            pl.BlockSpec(w_o.shape, fixed_at),
            pl.BlockSpec(norms.shape, fixed_at),
        ],
        out_specs=[pl.BlockSpec((block, width), row_at), pl.BlockSpec((block, width), row_at)],
        out_shape=[
            jax.ShapeDtypeStruct((rows, width), F32),
            jax.ShapeDtypeStruct((rows, width), BF16),
        ],
        compiler_params=params(16),
        cost_estimate=pl.CostEstimate(
            flops=4 * rows * inner * width, bytes_accessed=rows * width * 9, transcendentals=0
        ),
        name="add_branch",
    )(mixed, latent, w_o, norms)


def ff_kernel(low, dout, w_in, w_out, kept, sent, slope, grad_out, branch):
    step = pl.program_id(0)
    pre = contract(low[...], w_in[...], (1, 0))
    cdf = 0.5 * (1.0 + lax.erf(pre * math.sqrt(0.5)))
    slope[...] = cdf + pre * (jnp.exp(pre * pre * -0.5) * (1.0 / math.sqrt(2.0 * math.pi)))
    activ = (pre * cdf).astype(BF16)
    grad_out[...] = contract(activ, dout[...], (0, 0)).astype(BF16)

    @pl.when(step == 0)
    def _():
        branch[...] = jnp.zeros_like(branch)

    branch[...] += contract(activ, w_out[...], (1, 0))

    @pl.when(step == pl.num_programs(0) - 1)
    def _():
        kept[...] = branch[: kept.shape[0], :]
        sent[...] = branch[kept.shape[0] :, :].astype(BF16)


def feed_forward(low, dout, w_in, w_out):
    rows, width = low.shape
    hidden = w_in.shape[1]
    tile = min(FF_TILE, hidden)
    half = rows // 2
    in_at, out_at = (lambda t: (0, t)), (lambda t: (t, 0))
    return pl.pallas_call(
        ff_kernel,
        grid=(hidden // tile,),
        in_specs=[
            pl.BlockSpec((rows, width), fixed_at),
            pl.BlockSpec((rows, width), fixed_at),
            pl.BlockSpec((width, tile), in_at),
            pl.BlockSpec((tile, width), out_at),
        ],
        out_specs=[
            pl.BlockSpec((half, width), fixed_at),
            pl.BlockSpec((rows - half, width), fixed_at),
            pl.BlockSpec((rows, tile), in_at),
            pl.BlockSpec((tile, width), out_at),
        ],
        out_shape=[
            jax.ShapeDtypeStruct((half, width), F32),
            jax.ShapeDtypeStruct((rows - half, width), BF16),
            jax.ShapeDtypeStruct((rows, hidden), F32),
            jax.ShapeDtypeStruct((hidden, width), BF16),
        ],
        scratch_shapes=[pltpu.VMEM((rows, width), F32)],
        compiler_params=params(48),
        cost_estimate=pl.CostEstimate(
            flops=10 * rows * width * hidden, bytes_accessed=28 << 20, transcendentals=0
        ),
        name="feed_forward",
    )(low, dout, w_in, w_out)


def ff_back_kernel(low, dout, w_in, w_out, slope, grad_in, kept, sent, low_t, grad_low):
    step = pl.program_id(0)

    @pl.when(step == 0)
    def _():
        low_t[...] = low[...].T
        grad_low[...] = jnp.zeros_like(grad_low)

    grad = (contract(dout[...], w_out[...], (1, 1)) * slope[...]).astype(BF16)
    grad_in[...] = contract(low_t[...], grad, (1, 0)).astype(BF16)
    grad_low[...] += contract(grad, w_in[...], (1, 1))

    @pl.when(step == pl.num_programs(0) - 1)
    def _():
        kept[...] = grad_low[: kept.shape[0], :]
        sent[...] = grad_low[kept.shape[0] :, :].astype(BF16)


def feed_back(low, dout, w_in, w_out, slope):
    rows, width = low.shape
    hidden = w_in.shape[1]
    tile = min(FF_TILE, hidden)
    half = rows // 2
    in_at, out_at = (lambda t: (0, t)), (lambda t: (t, 0))
    return pl.pallas_call(
        ff_back_kernel,
        grid=(hidden // tile,),
        in_specs=[
            pl.BlockSpec((rows, width), fixed_at),
            pl.BlockSpec((rows, width), fixed_at),
            pl.BlockSpec((width, tile), in_at),
            pl.BlockSpec((tile, width), out_at),
            pl.BlockSpec((rows, tile), in_at),
        ],
        out_specs=[
            pl.BlockSpec((width, tile), in_at),
            pl.BlockSpec((half, width), fixed_at),
            pl.BlockSpec((rows - half, width), fixed_at),
        ],
        out_shape=[
            jax.ShapeDtypeStruct((width, hidden), BF16),
            jax.ShapeDtypeStruct((half, width), F32),
            jax.ShapeDtypeStruct((rows - half, width), BF16),
        ],
        scratch_shapes=[pltpu.VMEM((width, rows), BF16), pltpu.VMEM((rows, width), F32)],
        compiler_params=params(48),
        cost_estimate=pl.CostEstimate(
            flops=10 * rows * width * hidden, bytes_accessed=28 << 20, transcendentals=0
        ),
        name="feed_back",
    )(low, dout, w_in, w_out, slope)


def resid_back_kernel(
    kept, got, resid, cotangent, mixed, w_o, norms, grad_resid, grad_mixed, grad_o, vectors, total
):
    step = pl.program_id(0)

    @pl.when(step == 0)
    def _():
        vectors[...] = jnp.zeros_like(vectors)
        total[...] = jnp.zeros_like(total)

    grad = kept[...] + got[...].astype(F32)
    unit, inverse = norm_rows(resid[...])
    vectors[0:1, :] += jnp.sum(grad * unit, 0, keepdims=True)
    vectors[1:2, :] += jnp.sum(grad, 0, keepdims=True)
    value = cotangent[...] + norm_back(grad, unit, inverse, norms[4:5, :])
    grad_resid[...] = value
    low = value.astype(BF16)
    grad_mixed[...] = contract(low, w_o[...], (1, 1)).astype(BF16)
    total[...] += contract(mixed[...], low, (0, 0))
    grad_o[...] = total[...].astype(BF16)


def resid_back(kept, got, resid, cotangent, mixed, w_o, norms):
    rows, width = resid.shape
    inner = mixed.shape[1]
    block = rows // 4
    row_at = lambda i: (i, 0)
    wide = pl.BlockSpec((block, width), row_at)
    return pl.pallas_call(
        resid_back_kernel,
        grid=(rows // block,),
        in_specs=[
            wide,
            wide,
            wide,
            wide,
            pl.BlockSpec((block, inner), row_at),
            pl.BlockSpec(w_o.shape, fixed_at),
            pl.BlockSpec(norms.shape, fixed_at),
        ],
        out_specs=[
            wide,
            pl.BlockSpec((block, inner), row_at),
            pl.BlockSpec(w_o.shape, fixed_at),
            pl.BlockSpec((8, width), fixed_at),
        ],
        out_shape=[
            jax.ShapeDtypeStruct((rows, width), F32),
            jax.ShapeDtypeStruct((rows, inner), BF16),
            jax.ShapeDtypeStruct(w_o.shape, BF16),
            jax.ShapeDtypeStruct((8, width), F32),
        ],
        scratch_shapes=[pltpu.VMEM(w_o.shape, F32)],
        compiler_params=params(24),
        cost_estimate=pl.CostEstimate(
            flops=8 * rows * inner * width, bytes_accessed=rows * width * 20, transcendentals=0
        ),
        name="resid_back",
    )(kept, got, resid, cotangent, mixed, w_o, norms)


def attend_back_kernel(
    counts, keyvals, queries, key_input, grad_mixed, grad_kv, grad_q, grad_w, sums
):
    step = pl.program_id(0)
    keys_len = keyvals.shape[1]
    lat_len, inner = queries.shape[1:]
    media_len = keys_len - lat_len
    size = inner // HEADS
    wide = size * GROUP
    scale = 1.0 / math.sqrt(size)
    key_at = lax.broadcasted_iota(jnp.int32, (keys_len, 1), 0)
    valid = (key_at < counts[step]) | (key_at >= media_len)
    for at in range(0, inner, wide):
        keys = keyvals[0, :, at : at + wide]
        values = keyvals[0, :, inner + at : inner + at + wide]
        own = spread(queries[0, :, at : at + wide].astype(F32) * scale, size).astype(BF16)
        grad = spread(grad_mixed[0, :, at : at + wide], size).astype(BF16)
        scores = jnp.where(valid, contract(keys, own, (1, 1)), NEG)
        expd = jnp.exp(scores - jnp.max(scores, 0, keepdims=True))
        probs = expd * (1.0 / jnp.sum(expd, 0, keepdims=True))
        grad_v = contract(probs.astype(BF16), grad, (1, 0)).astype(BF16)
        grad_kv[0, :, inner + at : inner + at + wide] = grad_v
        grad_probs = contract(values, grad, (1, 1))
        held = jnp.sum(probs * grad_probs, 0, keepdims=True)
        low = (probs * (grad_probs - held)).astype(BF16)
        grad_kv[0, :, at : at + wide] = contract(low, own, (1, 0)).astype(BF16)
        back = contract(low, keys, (0, 0))
        grad_q[0, :, at : at + wide] = (gathered(back, size) * scale).astype(BF16)

    @pl.when(step == 0)
    def _():
        grad_w[...] = jnp.zeros_like(grad_w)
        sums[...] = jnp.zeros_like(sums)

    sums[...] += jnp.sum(grad_kv[0, :media_len, :].astype(F32), 0, keepdims=True)
    grad_w[...] += contract(key_input[0], grad_kv[0, :media_len, :], (0, 0))


def attend_back(counts, keyvals, queries, key_input, grad_mixed):
    images, keys_len, width = key_input.shape
    lat_len, inner = queries.shape[1:]
    media_len = keys_len - lat_len
    flops = 2 * images * (media_len * width * 2 * inner + 5 * lat_len * keys_len * inner * GROUP)
    return pl.pallas_call(
        attend_back_kernel,
        grid_spec=pltpu.PrefetchScalarGridSpec(
            num_scalar_prefetch=1,
            grid=(images,),
            in_specs=[
                pl.BlockSpec((1, keys_len, 2 * inner), image_at),
                pl.BlockSpec((1, lat_len, inner), image_at),
                pl.BlockSpec((1, media_len, width), image_at),
                pl.BlockSpec((1, lat_len, inner), image_at),
            ],
            out_specs=[
                pl.BlockSpec((1, keys_len, 2 * inner), image_at),
                pl.BlockSpec((1, lat_len, inner), image_at),
                pl.BlockSpec((width, 2 * inner), fixed_at),
                pl.BlockSpec((8, 2 * inner), fixed_at),
            ],
        ),
        out_shape=[
            jax.ShapeDtypeStruct((images, keys_len, 2 * inner), BF16),
            jax.ShapeDtypeStruct((images, lat_len, inner), BF16),
            jax.ShapeDtypeStruct((width, 2 * inner), F32),
            jax.ShapeDtypeStruct((8, 2 * inner), F32),
        ],
        compiler_params=params(40),
        cost_estimate=pl.CostEstimate(
            flops=2 * flops, bytes_accessed=images * keys_len * width * 8, transcendentals=0
        ),
        name="attend_back",
    )(counts, keyvals, queries, key_input, grad_mixed)


def as_row(column):
    out = []
    size = 128
    same = lax.broadcasted_iota(jnp.int32, (size, size), 0) == lax.broadcasted_iota(
        jnp.int32, (size, size), 1
    )
    for at in range(0, column.shape[0], size):
        out.append(jnp.sum(jnp.where(same, column[at : at + size, :], 0.0), 0, keepdims=True))
    return jnp.concatenate(out, 1)


def latent_back_kernel(
    grad_kv,
    grad_q,
    key_input,
    latent,
    grad_resid,
    w_kv,
    w_q,
    norms,
    media_w,
    media_sums,
    latent_grad,
    grad_wkv,
    grad_wq,
    vectors,
):
    images, lat_len, width = latent.shape
    rows = images * lat_len
    flat_kv = grad_kv[...].reshape(rows, grad_kv.shape[2])
    flat_q = grad_q[...].reshape(rows, grad_q.shape[2])
    low = key_input[...].reshape(rows, width)
    grad = contract(flat_kv, w_kv[...], (1, 1)) + contract(flat_q, w_q[...], (1, 1))
    unit, inverse = norm_rows(latent[...].reshape(rows, width).astype(F32))
    back = norm_back(grad, unit, inverse, norms[2:3, :])
    latent_grad[...] = grad_resid[...] + back.reshape(images, lat_len, width)
    grad_wq[...] = contract(low, flat_q, (0, 0)).astype(BF16)
    grad_wkv[...] = (media_w[...] + contract(low, flat_kv, (0, 0))).astype(BF16)
    parts, left = [], media_sums[0:1, :]
    for _ in range(3):
        parts.append(left.astype(BF16))
        left = left - parts[-1].astype(F32)
    parts.append(jnp.zeros((5, left.shape[1]), BF16))
    bias = jnp.sum(contract(jnp.concatenate(parts, 0), w_kv[...], (1, 1)), 0, keepdims=True)
    both = as_row(jnp.sum(media_w[...] * w_kv[...].astype(F32), 1, keepdims=True))
    vectors[...] = jnp.zeros_like(vectors)
    vectors[0:1, :] = (both - norms[1:2, :] * bias) / norms[0:1, :]
    vectors[1:2, :] = bias
    vectors[2:3, :] = jnp.sum(grad * unit, 0, keepdims=True)
    vectors[3:4, :] = jnp.sum(grad, 0, keepdims=True)


def latent_back(grad_kv, grad_q, key_input, latent, grad_resid, w_kv, w_q, norms, media_w, media_sums):
    images, lat_len, width = latent.shape
    inner = w_q.shape[1]
    tail = grad_kv.shape[1] // lat_len - 1
    tail_at = lambda i: (0, tail, 0)
    whole3 = lambda i: (0, 0, 0)
    return pl.pallas_call(
        latent_back_kernel,
        grid=(1,),
        in_specs=[
            pl.BlockSpec((images, lat_len, 2 * inner), tail_at),
            pl.BlockSpec((images, lat_len, inner), whole3),
            pl.BlockSpec((images, lat_len, width), tail_at),
            pl.BlockSpec((images, lat_len, width), whole3),
            pl.BlockSpec((images, lat_len, width), whole3),
            pl.BlockSpec(w_kv.shape, fixed_at),
            pl.BlockSpec(w_q.shape, fixed_at),
            pl.BlockSpec(norms.shape, fixed_at),
            pl.BlockSpec(media_w.shape, fixed_at),
            pl.BlockSpec(media_sums.shape, fixed_at),
        ],
        out_specs=[
            pl.BlockSpec((images, lat_len, width), whole3),
            pl.BlockSpec(w_kv.shape, fixed_at),
            pl.BlockSpec(w_q.shape, fixed_at),
            pl.BlockSpec((8, width), fixed_at),
        ],
        out_shape=[
            jax.ShapeDtypeStruct((images, lat_len, width), F32),
            jax.ShapeDtypeStruct(w_kv.shape, BF16),
            jax.ShapeDtypeStruct(w_q.shape, BF16),
            jax.ShapeDtypeStruct((8, width), F32),
        ],
        compiler_params=params(48),
        cost_estimate=pl.CostEstimate(
            flops=14 * images * lat_len * inner * width, bytes_accessed=20 << 20, transcendentals=0
        ),
        name="latent_back",
    )(grad_kv, grad_q, key_input, latent, grad_resid, w_kv, w_q, norms, media_w, media_sums)


def media_back_kernel(media, grad_kv, norms, w_kv, out, grad):
    grad[...] = contract(grad_kv[0], w_kv[...], (1, 1))
    for at in range(0, media.shape[1], ROWS):
        unit, inverse = norm_rows(media[0, at : at + ROWS, :].astype(F32))
        out[0, at : at + ROWS, :] = norm_back(grad[at : at + ROWS, :], unit, inverse, norms[0:1, :])


def media_back(media, grad_kv, norms, w_kv):
    images, media_len, width = media.shape
    inner2 = w_kv.shape[1]
    at = lambda i: (i, 0, 0)
    return pl.pallas_call(
        media_back_kernel,
        grid=(images,),
        in_specs=[
            pl.BlockSpec((1, media_len, width), at),
            pl.BlockSpec((1, media_len, inner2), at),
            pl.BlockSpec(norms.shape, fixed_at),
            pl.BlockSpec(w_kv.shape, fixed_at),
        ],
        out_specs=pl.BlockSpec((1, media_len, width), at),
        out_shape=jax.ShapeDtypeStruct((images, media_len, width), F32),
        scratch_shapes=[pltpu.VMEM((media_len, width), F32)],
        compiler_params=params(32),
        cost_estimate=pl.CostEstimate(
            flops=4 * images * media_len * width * inner2,
            bytes_accessed=images * media_len * width * 8,
            transcendentals=0,
        ),
        name="media_back",
    )(media, grad_kv, norms, w_kv)


class Grid:
    def __init__(self, dp, rep):
        self.dp = dp
        self.rep = rep
        self.me = lax.axis_index("dp")
        self.core = lax.axis_index("rep")
        self.column = [1 << b for b in range(2, dp.bit_length() - 1)]

    def swap(self, value, bit):
        return lax.ppermute(value, "dp", [(i, i ^ bit) for i in range(self.dp)])

    def side(self, bit):
        return (self.me & bit) != 0

    def pair(self, own, other, bit, axis):
        return jnp.where(
            self.side(bit), jnp.stack([other, own], axis), jnp.stack([own, other], axis)
        )

    def pick(self, value, bit, axis):
        at = jnp.where(self.side(bit), 1, 0)
        keep = lax.dynamic_index_in_dim(value, at, axis, keepdims=False)
        send = lax.dynamic_index_in_dim(value, 1 - at, axis, keepdims=False)
        return keep, send

    def gather(self, first, second):
        rows = first.shape[0]
        both = jnp.concatenate([first, second], 0)[None]
        for bit in reversed(self.column):
            got = self.swap(both, bit)
            both = self.pair(both, got, bit, 1)
            both = both.reshape((-1,) + both.shape[2:])
        first, second = both[:, :rows], both[:, rows:]
        first_got, second_got = self.swap(first, 2), self.swap(second, 1)
        first = self.pair(first, first_got, 2, 1)
        second = self.pair(second, second_got, 1, 1)
        first_got, second_got = self.swap(first, 1), self.swap(second, 2)
        first = self.pair(first, first_got, 1, 2)
        second = self.pair(second, second_got, 2, 1)
        return (
            first.reshape((self.dp,) + first.shape[3:]),
            second.reshape((self.dp,) + second.shape[3:]),
        )

    def total(self, first, second):
        rows = first.shape[1]
        tail = first.shape[1:]

        def fold(value, bit, axis, last=False):
            keep, send = self.pick(value, bit, axis)
            got = self.swap(send, bit)
            added = keep.astype(F32) + got.astype(F32)
            return added if last else added.astype(BF16)

        first = first.reshape((-1, 2, 2) + tail)
        second = second.reshape((-1, 2, 2) + second.shape[1:])
        first, second = fold(first, 1, 2), fold(second, 2, 1)
        first, second = fold(first, 2, 1), fold(second, 1, 1)
        both = jnp.concatenate([first, second], 1)
        for bit in self.column:
            both = both.reshape((-1, 2) + both.shape[1:])
            both = fold(both, bit, 1, bit == self.column[-1])
        both = both[0]
        return both[:rows], both[rows:]

    def other(self, value):
        return lax.ppermute(value, "rep", [(0, 1), (1, 0)])

    def rep_all(self, value):
        if self.rep != 2:
            return lax.all_gather(value, "rep", axis=0)
        got = self.other(value)
        return jnp.where(self.core == 0, jnp.stack([value, got]), jnp.stack([got, value]))

    def rep_rows(self, value):
        if self.rep != 2:
            return lax.all_gather(value, "rep", axis=0, tiled=True)
        return jnp.concatenate([value, self.other(value)], 0)

    def rep_back(self, pieces):
        if self.rep != 2:
            value = jnp.concatenate([piece.astype(F32) for pair in pieces for piece in pair], 0)
            value = lax.psum_scatter(value, "rep", scatter_dimension=0, tiled=True)
            return value, jnp.zeros(value.shape, BF16)
        ((kept, sent),) = pieces
        return kept, self.other(sent)

    def rep_total(self, value, axis):
        if self.rep != 2:
            value = jnp.moveaxis(value, axis, 0).astype(F32)
            return lax.psum_scatter(value, "rep", scatter_dimension=0).astype(BF16)
        keep = lax.dynamic_index_in_dim(value, self.core, axis, keepdims=False)
        send = lax.dynamic_index_in_dim(value, 1 - self.core, axis, keepdims=False)
        return (keep.astype(F32) + self.other(send).astype(F32)).astype(BF16)

    def mine(self, value, axis):
        return lax.dynamic_index_in_dim(value, self.core, axis, keepdims=False)


def fold_rows(value):
    half = value.shape[-2] // 2
    return jnp.concatenate([value[..., :half, :], value[..., half:, :]], -1)


def unfold_rows(value):
    half = value.shape[-1] // 2
    return jnp.concatenate([value[..., :half], value[..., half:]], -2)


def shards(
    dp,
    rep,
    media_tokens,
    patch_counts,
    latents,
    media_gain,
    media_bias,
    latent_gain,
    latent_bias,
    query_weight,
    keyval_weight,
    outproj_weight,
    ff_gain,
    ff_bias,
    ff_in_weight,
    ff_out_weight,
    cotangent,
):
    grid = Grid(dp, rep)
    images, media_len, width = media_tokens.shape
    lat_len = latents.shape[1]
    inner_width = query_weight.shape[1]
    hidden = ff_in_weight.shape[1]
    slot = hidden // dp // rep
    part = width // dp
    kv_rows = part // rep
    o_rows = inner_width // dp // rep

    norms = jnp.stack([media_gain, media_bias, latent_gain, latent_bias, ff_gain, ff_bias])
    norm_row = jnp.pad(norms.reshape(1, -1), ((0, 0), (0, width - norms.size)))
    kv_part = grid.mine(keyval_weight.reshape(rep, kv_rows, width), 0)
    q_part = fold_rows(grid.mine(query_weight.reshape(rep, kv_rows, inner_width), 0))
    q_rows = q_part.shape[0]
    got_kv, got_q = grid.gather(kv_part, jnp.concatenate([q_part, norm_row], 0))
    got_norms = got_q[:, q_rows, : norms.size].reshape(dp, 6, part)
    got_norms = jnp.moveaxis(got_norms, 1, 0).reshape(6, width).astype(F32)
    norms_all = jnp.concatenate([got_norms, jnp.zeros((2, width), F32)], 0)
    w_keyval = jnp.moveaxis(grid.rep_all(got_kv), 0, 1).reshape(width, width)
    w_query = jnp.moveaxis(grid.rep_all(unfold_rows(got_q[:, :q_rows])), 0, 1)
    w_query = w_query.reshape(width, inner_width)

    ffin_part = grid.mine(ff_in_weight.reshape(part, dp, rep, slot), 2).reshape(part, dp * slot)
    cut = ffin_part.shape[1] // 2
    o_part = grid.mine(outproj_weight.reshape(rep, o_rows, width), 0)
    o_part = jnp.pad(o_part, ((0, 0), (0, max(cut - width, 0))))
    got_lo, got_hi = grid.gather(
        ffin_part[:, :cut] if cut >= width else jnp.pad(ffin_part[:, :cut], ((0, 0), (0, width - cut))),
        jnp.concatenate(
            [
                ffin_part[:, cut:] if cut >= width else jnp.pad(ffin_part[:, cut:], ((0, 0), (0, width - cut))),
                o_part,
            ],
            0,
        ),
    )
    w_ffin = jnp.concatenate(
        [
            got_lo[:, :, :cut].reshape(width, cut),
            got_hi[:, :part, :cut].reshape(width, cut),
        ],
        1,
    )
    w_outproj = jnp.moveaxis(grid.rep_all(got_hi[:, part:, :width]), 0, 1).reshape(inner_width, width)
    ffout_part = grid.mine(ff_out_weight.reshape(rep, slot, width), 0)
    w_ffout = lax.all_gather(ffout_part, "dp", axis=0, tiled=True)

    flat = (images * lat_len, width)
    dout = grid.rep_rows(cotangent.astype(BF16).reshape(flat))
    key_input, keyvals, queries, mixed = attend(
        patch_counts, media_tokens, latents, norms_all, w_keyval, w_query
    )
    mixed = mixed.reshape(-1, inner_width)
    resid, low = add_branch(mixed, latents.reshape(flat), w_outproj, norms_all)

    low = grid.rep_rows(low)
    cuts = [slice(at, at + FF_ROWS) for at in range(0, low.shape[0], FF_ROWS)]
    ahead = [feed_forward(low[cut], dout[cut], w_ffin, w_ffout) for cut in cuts]
    grad_ffout = functools.reduce(jnp.add, [part[3] for part in ahead])
    back = [
        feed_back(low[cut], dout[cut], w_ffin, w_ffout, part[2])
        for cut, part in zip(cuts, ahead, strict=True)
    ]
    grad_ffin = functools.reduce(jnp.add, [part[0] for part in back])
    kept, got = grid.rep_back([part[1:] for part in back])
    share, other_share = grid.rep_back([part[:2] for part in ahead])
    new_latents = (resid + share + other_share.astype(F32)).reshape(latents.shape)

    grad_ffout = grad_ffout.reshape(dp, slot, width)
    own_lo, own_hi = grid.total(grad_ffout[:, : slot // 2], grad_ffout[:, slot // 2 :])
    own_ffout = grid.rep_all(jnp.concatenate([own_lo, own_hi], 0)).reshape(rep * slot, width)
    grad_ffin = grad_ffin.reshape(dp, part, dp * slot)
    own_lo, own_hi = grid.total(grad_ffin[:, :, :cut], grad_ffin[:, :, cut:])
    own_ffin = grid.rep_all(jnp.concatenate([own_lo, own_hi], 1))
    own_ffin = jnp.moveaxis(own_ffin.reshape(rep, part, dp, slot), 0, 2).reshape(part, hidden)

    grad_resid, grad_mixed, grad_outproj, ff_vectors = resid_back(
        kept, got, resid, cotangent.reshape(flat), mixed, w_outproj, norms_all
    )
    grad_kv, grad_q, media_w, media_sums = attend_back(
        patch_counts, keyvals, queries, key_input, grad_mixed.reshape(images, lat_len, inner_width)
    )
    latent_grad, grad_kvweight, grad_qweight, vectors = latent_back(
        grad_kv,
        grad_q,
        key_input,
        latents,
        grad_resid.reshape(latents.shape),
        w_keyval,
        w_query,
        norms_all,
        media_w,
        media_sums,
    )
    media_grad = media_back(media_tokens, grad_kv, norms_all, w_keyval)
    vectors = jnp.concatenate([vectors[:4], ff_vectors[:2]], 0)

    kv_sum = grid.rep_total(grad_kvweight.reshape(dp, rep, kv_rows, width), 1)
    q_sum = fold_rows(grid.rep_total(grad_qweight.reshape(dp, rep, kv_rows, inner_width), 1))
    o_sum = grid.rep_total(grad_outproj.reshape(dp, rep, o_rows, width), 1)
    vec_row = jnp.moveaxis(vectors.reshape(6, dp, part), 1, 0).reshape(dp, 1, 6 * part)
    vec_row = jnp.pad(vec_row, ((0, 0), (0, 0), (0, width - 6 * part))).astype(BF16)
    own_kv, own_rest = grid.total(kv_sum, jnp.concatenate([q_sum, o_sum, vec_row], 1))
    every = grid.rep_all(jnp.concatenate([own_kv, own_rest], 0))
    own_kv = every[:, :kv_rows].reshape(part, width)
    own_q = unfold_rows(every[:, kv_rows : kv_rows + q_rows]).reshape(part, inner_width)
    at = kv_rows + q_rows
    own_o = every[:, at : at + o_rows].reshape(rep * o_rows, width)
    own_vec = jnp.sum(every[:, at + o_rows, : 6 * part], 0).reshape(6, part)
    return (
        new_latents,
        media_grad,
        latent_grad,
        own_vec[0],
        own_vec[1],
        own_vec[2],
        own_vec[3],
        own_q,
        own_kv,
        own_o,
        own_vec[4],
        own_vec[5],
        own_ffin,
        own_ffout,
    )


def solution(mesh):
    dp, rep = mesh.shape["dp"], mesh.shape["rep"]

    def program(*arrays):
        return shards(dp, rep, *arrays)

    return jax.shard_map(
        program,
        mesh=mesh,
        in_specs=(
            P(("dp", "rep"), None, None),
            P(("dp", "rep")),
            P(("dp", "rep"), None, None),
            P("dp"),
            P("dp"),
            P("dp"),
            P("dp"),
            P("dp", None),
            P("dp", None),
            P("dp", None),
            P("dp"),
            P("dp"),
            P("dp", None),
            P("dp", None),
            P(("dp", "rep"), None, None),
        ),
        out_specs=(
            P(("dp", "rep"), None, None),
            P(("dp", "rep"), None, None),
            P(("dp", "rep"), None, None),
            P("dp"),
            P("dp"),
            P("dp"),
            P("dp"),
            P("dp", None),
            P("dp", None),
            P("dp", None),
            P("dp"),
            P("dp"),
            P("dp", None),
            P("dp", None),
        ),
        check_vma=False,
    )
```

time: 579 us -> 477 us (0.82)
  matrix products: 165 us -> 0 us
  Pallas kernels: 0 us -> 140 us
  other arithmetic: 120 us -> 54.9 us
  local copies, waits for them, and re-layouts: 97.6 us -> 75.3 us
  waiting for transfers between devices: 131 us -> 141 us
    dot_general x21 -> x0, matrix products: 165 us -> none  [the longest x1 27.6 us: shards(): pre_act = jnp.dot(ff_low, w_ffin, preferred_element_type=F32)]
    pallas_call x0 -> x8, Pallas kernels: none -> 140 us  [the longest x1 35.4 us: attend_back(): pl.pallas_call(attend_back_kernel, grid_spec=pltpu.PrefetchScalarGridSpec...]
    reduce_sum x9 -> x0, other arithmetic: 28.5 us -> none  [the longest x3 17 us: row_total(): return jnp.sum(values.reshape(-1, values.shape[-1]), axis=0)]
    slice x5 -> x3, local copies, waits for them, and re-layouts: 26.8 us -> 0.72 us  [the longest x1 0.71 us: shards(): got_norms = got_q[:, q_rows, :norms.size].reshape(dp, 6, part)]
    convert_element_type x9 -> x4, other arithmetic: 23.4 us -> 3.47 us  [the longest x3 2.35 us: rep_total(): return (keep.astype(F32) + self.other(send).astype(F32)).astype(BF16)]
    mul x1 -> x0, other arithmetic: 17.6 us -> none  [norm_grad(): inverse * (scaled - jnp.mean(scaled, -1, keepdims=True) - unit * jnp.mean...]
    reshape x4 -> x3, local copies, waits for them, and re-layouts: 18.9 us -> 3.05 us  [the longest x1 2.95 us: total(): second = second.reshape((-1, 2, 2) + second.shape[1:])]
    ppermute x30, waiting for transfers between devices: 131 us -> 141 us  [swap(): return lax.ppermute(value, 'dp', [(i, i ^ bit) for i in range(self.dp)])]
  transfers between devices with their start and end apart: 44 -> 44, of which waited for: 18 -> 13; matrix products, arithmetic and copies ran while one was open for 63% -> 21% of each run, Pallas kernels for 0% -> 25%
where the time goes in v2:
time: 477 us; the launch traced here: 470 us
  waiting for transfers between devices  141 us (30%)
  Pallas kernels  140 us (29%)
  local copies, waits for them, and re-layouts  75.3 us (16%)
  other arithmetic  54.9 us (12%)
  starting transfers between devices  44.1 us (9%)
  between operations  15.7 us (3%)
    ppermute x30, waiting for transfers between devices, swap(): return lax.ppermute(value, 'dp', [(i, i ^ bit) for i in range(self.dp)])  141 us
    ppermute x30, starting transfers between devices, swap(): return lax.ppermute(value, 'dp', [(i, i ^ bit) for i in range(self.dp)])  42.5 us
    pallas_call x1, Pallas kernels, attend_back(): pl.pallas_call(attend_back_kernel, grid_spec=pltpu.PrefetchScalarGridSpec...  35.4 us
    pallas_call x1, Pallas kernels, attend(): pl.pallas_call(attend_kernel, grid_spec=pltpu.PrefetchScalarGridSpec(num_...  26.8 us
    unnamed x149, local copies, waits for them, and re-layouts  22.6 us
    pallas_call x1, Pallas kernels, feed_forward(): pl.pallas_call(ff_kernel, grid=(hidden // tile,), in_specs=[pl.BlockSpec(...  21.7 us
    pallas_call x1, Pallas kernels, feed_back(): pl.pallas_call(ff_back_kernel, grid=(hidden // tile,), in_specs=[pl.Block...  19.3 us
    pallas_call x1, Pallas kernels, media_back(): pl.pallas_call(media_back_kernel, grid=(images,), in_specs=[pl.BlockSpec(...  18.8 us
  transfers between devices with their start and end apart: 44, of which 13 were waited for; matrix products, arithmetic and copies ran while one was open for 21% of the time, Pallas kernels for 25%

profile of v2, /device:TPU:0, one launch (start us, length us, event | category | flops | bytes accessed | tf_op | source)
XLA Modules:
  0.0 470.5 jit_solution(779620799054003809)
XLA Ops:
  7.3 1.5 reshape.695
  8.9 1.5 dynamic-slice_reduce_fusion
  10.6 4.1 collective-permute-start.8
  15.8 20.8 %collective-permute-done = bf16[1,49,1024]{2,1,0:T(8,128)(2,1)S(1)} collective-permute-done((bf16[1,49,1024]{2,1,0:T(8,128)(2,1)S(1)}, bf16[1,49,1024]{2,1,0:T(8,128)(2,1)S(1)}, u32[]{:S(2)}, u32[]{:S(2)}) %collective-permute-start) | collective-permute-done | bytes 100384 | tf_op jit(solution)/shard_map/ppermute | solution.py:547
  36.6 2.4 collective-permute-start.1
  39.3 6.6 %collective-permute-done.1 = bf16[2,49,1024]{2,1,0:T(8,128)(2,1)S(1)} collective-permute-done((bf16[2,49,1024]{2,1,0:T(8,128)(2,1)S(1)}, bf16[2,49,1024]{2,1,0:T(8,128)(2,1)S(1)}, u32[]{:S(2)}, u32[]{:S(2)}) %collective-permute-start.1) | collective-permute-done | bytes 200736 | tf_op jit(solution)/shard_map/ppermute | solution.py:547
  46.3 1.6 collective-permute-start.2
  48.0 1.4 collective-permute-start.4
  49.4 5.2 %collective-permute-done.2 = bf16[4,17,1024]{2,0,1:T(4,128)(2,1)S(1)} collective-permute-done((bf16[4,17,1024]{2,0,1:T(4,128)(2,1)S(1)}, bf16[4,17,1024]{2,0,1:T(4,128)(2,1)S(1)}, u32[]{:S(2)}, u32[]{:S(2)}) %collective-permute-start.2) | collective-permute-done | bytes 139296 | tf_op jit(solution)/shard_map/ppermute | solution.py:547
  54.8 1.4 collective-permute-start.3
  56.4 12.3 %collective-permute-done.9 = bf16[2,144,1024]{2,1,0:T(8,128)(2,1)S(1)} collective-permute-done((bf16[2,144,1024]{2,1,0:T(8,128)(2,1)S(1)}, bf16[2,144,1024]{2,1,0:T(8,128)(2,1)S(1)}, u32[]{:S(2)}, u32[]{:S(2)}) %collective-permute-start.9) | collective-permute-done | bytes 589856 | tf_op jit(solution)/shard_map/ppermute | solution.py:547
  75.5 2.9 select_n.374
  80.6 17.4 %collective-permute-done.10 = bf16[4,80,1024]{2,1,0:T(8,128)(2,1)S(1)} collective-permute-done((bf16[4,80,1024]{2,1,0:T(8,128)(2,1)}, bf16[4,80,1024]{2,1,0:T(8,128)(2,1)S(1)}, u32[]{:S(2)}, u32[]{:S(2)}) %collective-permute-start.10) | collective-permute-done | bytes 655392 | tf_op jit(solution)/shard_map/ppermute | solution.py:547
  99.2 1.4 collective-permute-start.11
  100.6 11.7 %collective-permute-done.5 = bf16[4,2,32,1024]{3,2,0,1:T(8,128)(2,1)} collective-permute-done((bf16[4,2,32,1024]{3,2,0,1:T(8,128)(2,1)}, bf16[4,2,32,1024]{3,2,0,1:T(8,128)(2,1)}, u32[]{:S(2)}, u32[]{:S(2)}) %collective-permute-start.5) | collective-permute-done | bytes 524320 | tf_op jit(solution)/shard_map/ppermute | solution.py:547
  118.9 1.4 fusion.8
  120.9 13.1 %collective-permute-done.15 = bf16[4,64,1024]{2,1,0:T(8,128)(2,1)S(1)} collective-permute-done((bf16[4,64,1024]{2,1,0:T(8,128)(2,1)}, bf16[4,64,1024]{2,1,0:T(8,128)(2,1)S(1)}, u32[]{:S(2)}, u32[]{:S(2)}) %collective-permute-start.15) | collective-permute-done | bytes 524320 | tf_op jit(solution)/shard_map/ppermute | solution.py:547
  135.2 2.4 collective-permute-start.16
  137.8 1.9 maximum_select_fusion.1
  139.8 2.7 maximum_select_fusion
  144.4 26.8 %attend.1 = (bf16[8,640,1024]{2,1,0:T(8,128)(2,1)}, bf16[8,640,1024]{2,1,0:T(8,128)(2,1)}, bf16[8,64,512]{2,1,0:T(8,128)(2,1)S(1)}, bf16[8,64,512]{2,1,0:T(8,128)(2,1)S(1)}) custom-call(s32[8]{0:T(128)S(1)} %copy-done.27, bf16[8,576,1024]{2,1,0:T(8,128)(2,1)S(1)} %bitcast.275, bf16[8,64,1024]{2,1,0:T(8,128)(2,1)S(1)} %copy-done.18, ...), custom_call_target="tpu_custom_call" | custom-call | flops 22548578304 | bytes 31457280 | tf_op jit(solution)/shard_map/attend/pallas_call | solution.py:100
  171.3 3.1 add_branch.1
  174.4 3.1 pad_maximum_fusion.1.dout
  179.2 1.5 copy-done.31
  181.0 2.4 pad_maximum_fusion.w_in
  187.3 1.6 copy-done.23
  188.9 21.7 %feed_forward.1 = (f32[512,1024]{1,0:T(8,128)S(1)}, bf16[512,1024]{1,0:T(8,128)(2,1)}, f32[1024,2048]{1,0:T(8,128)}, bf16[2048,1024]{1,0:T(8,128)(2,1)}) custom-call(bf16[1024,1024]{1,0:T(8,128)(2,1)S(1)} %copy-done.23, bf16[1024,1024]{1,0:T(8,128)(2,1)} %pad_maximum_fusion.1.dout, bf16[1024,2048]{1,0:T(8,128)(2,1)} %pad_maximum_fusion.w_in, ...), custom_call_target="tpu_custom_call" | custom-call | flops 21474836480 | bytes 29360128 | tf_op jit(solution)/shard_map/feed_forward/pallas_call | solution.py:193
  210.6 3.7 fusion.31
  218.1 1.7 collective-permute-start.38
  219.9 19.3 %feed_back.1 = (bf16[1024,2048]{1,0:T(8,128)(2,1)}, f32[512,1024]{1,0:T(8,128)S(1)}, bf16[512,1024]{1,0:T(8,128)(2,1)S(1)}) custom-call(bf16[1024,1024]{1,0:T(8,128)(2,1)S(1)} %copy-done.23, bf16[1024,1024]{1,0:T(8,128)(2,1)} %pad_maximum_fusion.1.dout, bf16[1024,2048]{1,0:T(8,128)(2,1)} %pad_maximum_fusion.w_in, bf16[2048,1024]{1,0:T(8,128)(2,1)} %bitcast.343, ...), custom_call_target="tpu_custom_call" | custom-call | flops 21474836480 | bytes 29360128 | tf_op jit(solution)/shard_map/feed_back/pallas_call | solution.py:247
  239.2 5.4 %fusion.32 = (bf16[16,64,1024]{2,1,0:T(8,128)(2,1)S(1)}, bf16[16,64,1024]{2,1,0:T(8,128)(2,1)}) fusion(bf16[16,64,2048]{2,1,0:T(8,128)(2,1)} %bitcast.292), kind=kLoop, calls=%fused_computation.157 | loop fusion | bytes 8388608 | tf_op jit(solution)/shard_map/slice | solution.py:739
  246.9 1.8 collective-permute-start.29
  251.0 1.9 fusion.2
  253.8 1.7 collective-permute-start.37
  255.6 1.7 fusion.1
  258.2 14.0 %collective-permute-done.29 = bf16[4,2,64,1024]{3,2,0,1:T(8,128)(2,1)} collective-permute-done((bf16[4,2,64,1024]{3,2,0,1:T(8,128)(2,1)}, bf16[4,2,64,1024]{3,2,0,1:T(8,128)(2,1)}, u32[]{:S(2)}, u32[]{:S(2)}) %collective-permute-start.29) | collective-permute-done | bytes 1048608 | tf_op jit(solution)/shard_map/ppermute | solution.py:547
  272.2 1.7 collective-permute-start.39
  274.0 1.8 fusion.4
  279.5 4.9 %resid_back.1 = (f32[512,1024]{1,0:T(8,128)S(1)}, bf16[512,512]{1,0:T(8,128)(2,1)S(1)}, bf16[512,1024]{1,0:T(8,128)(2,1)S(1)}, f32[8,1024]{1,0:T(8,128)S(1)}) custom-call(f32[512,1024]{1,0:T(8,128)S(1)} %copy-done.13, bf16[512,1024]{1,0:T(8,128)(2,1)S(1)} %collective-permute-done.18.got, f32[512,1024]{1,0:T(8,128)S(1)} %get-tuple-element.40.resid, ...), custom_call_target="tpu_custom_call" | custom-call | flops 2147483648 | bytes 10485760 | tf_op jit(solution)/shard_map/resid_back/pallas_call | solution.py:304
  285.7 35.4 %attend_back.1 = (bf16[8,640,1024]{2,1,0:T(8,128)(2,1)}, bf16[8,64,512]{2,1,0:T(8,128)(2,1)S(1)}, f32[1024,1024]{1,0:T(8,128)S(1)}, f32[8,1024]{1,0:T(8,128)S(1)}) custom-call(s32[8]{0:T(128)S(1)} %copy-done.27, bf16[8,640,1024]{2,1,0:T(8,128)(2,1)} %get-tuple-element.44.keyvals, bf16[8,64,512]{2,1,0:T(8,128)(2,1)S(1)} %copy-done.29, ...), custom_call_target="tpu_custom_call" | custom-call | flops 32749125632 | bytes 41943040 | tf_op jit(solution)/shard_map/attend_back/pallas_call | solution.py:380
  321.1 2.0 copy-done.7
  323.2 9.8 %latent_back.1 = (f32[8,64,1024]{2,1,0:T(8,128)}, bf16[1024,1024]{1,0:T(8,128)(2,1)S(1)}, bf16[1024,512]{1,0:T(8,128)(2,1)S(1)}, f32[8,1024]{1,0:T(8,128)S(1)}) custom-call(bf16[8,640,1024]{2,1,0:T(8,128)(2,1)} %get-tuple-element.51.grad_kv, bf16[8,64,512]{2,1,0:T(8,128)(2,1)S(1)} %get-tuple-element.52.grad_q, ...), custom_call_target="tpu_custom_call" | custom-call | flops 3758096384 | bytes 20971520 | tf_op jit(solution)/shard_map/latent_back/pallas_call | solution.py:470
  335.9 4.0 copy-done.2
  339.9 1.6 copy-done.6
  341.5 3.7 copy-done.24
  345.2 18.8 %media_back.1 = f32[8,576,1024]{2,1,0:T(8,128)} custom-call(bf16[8,576,1024]{2,1,0:T(8,128)(2,1)S(1)} %copy-done.24, bf16[8,640,1024]{2,1,0:T(8,128)(2,1)S(1)} %copy-done.2, f32[8,1024]{1,0:T(8,128)S(1)} %pad_convert_fusion.norms, bf16[1024,1024]{1,0:T(8,128)(2,1)S(1)} %bitcast.261), custom_call_target="tpu_custom_call" | custom-call | flops 19327352832 | bytes 37748736 | tf_op jit(solution)/shard_map/media_back/pallas_call | solution.py:516
  366.0 3.3 convert_add_fusion.5
  376.8 2.0 collective-permute-start.33
  380.7 3.0 reshape.712
  385.2 1.6 fusion.5
  386.8 1.8 collective-permute-start.20
  389.9 4.4 collective-permute-start.41
  394.3 10.1 %collective-permute-done.33 = bf16[2,128,1024]{2,1,0:T(8,128)(2,1)} collective-permute-done((bf16[2,128,1024]{2,1,0:T(8,128)(2,1)}, bf16[2,128,1024]{2,1,0:T(8,128)(2,1)}, u32[]{:S(2)}, u32[]{:S(2)}) %collective-permute-start.33) | collective-permute-done | bytes 524320 | tf_op jit(solution)/shard_map/ppermute | solution.py:547
  405.7 4.2 collective-permute-start.34
  410.7 1.4 constant_dynamic-slice_fusion.8
  412.3 1.8 collective-permute-start.25
  414.1 5.7 %collective-permute-done.34 = bf16[1,128,1024]{2,1,0:T(8,128)(2,1)S(1)} collective-permute-done((bf16[1,128,1024]{2,1,0:T(8,128)(2,1)S(1)}, bf16[1,128,1024]{2,1,0:T(8,128)(2,1)S(1)}, u32[]{:S(2)}, u32[]{:S(2)}) %collective-permute-start.34) | collective-permute-done | bytes 262176 | tf_op jit(solution)/shard_map/ppermute | solution.py:547
  421.3 7.0 %collective-permute-done.21 = bf16[4,32,1024]{2,1,0:T(8,128)(2,1)S(1)} collective-permute-done((bf16[4,32,1024]{2,1,0:T(8,128)(2,1)S(1)}, bf16[4,32,1024]{2,1,0:T(8,128)(2,1)S(1)}, u32[]{:S(2)}, u32[]{:S(2)}) %collective-permute-start.21) | collective-permute-done | bytes 262176 | tf_op jit(solution)/shard_map/ppermute | solution.py:547
  431.7 6.1 %collective-permute-done.26 = bf16[2,65,1024]{2,0,1:T(2,128)(2,1)S(1)} collective-permute-done((bf16[2,65,1024]{2,0,1:T(2,128)(2,1)S(1)}, bf16[2,65,1024]{2,0,1:T(2,128)(2,1)S(1)}, u32[]{:S(2)}, u32[]{:S(2)}) %collective-permute-start.26) | collective-permute-done | bytes 266272 | tf_op jit(solution)/shard_map/ppermute | solution.py:547
  439.5 1.7 stack.374
  441.1 10.5 %collective-permute-done.27 = bf16[1,65,1024]{2,0,1:T(2,128)(2,1)} collective-permute-done((bf16[1,65,1024]{2,0,1:T(2,128)(2,1)S(1)}, bf16[1,65,1024]{2,0,1:T(2,128)(2,1)}, u32[]{:S(2)}, u32[]{:S(2)}) %collective-permute-start.27) | collective-permute-done | bytes 133152 | tf_op jit(solution)/shard_map/ppermute | solution.py:547
  453.9 1.5 fusion.9
  455.4 1.8 reshape.721
  457.2 2.3 maximum_select_fusion.12
  (320 shorter events, 75.6 us)
Async XLA Ops:
  7.2 7.9 %copy-start = (bf16[256,1024]{1,0:T(8,128)(2,1)S(1)}, bf16[256,1024]{1,0:T(8,128)(2,1)}, u32[]{:S(2)}) copy-start(bf16[256,1024]{1,0:T(8,128)(2,1)} %param.28) | copy-start | bytes 1572868
  7.2 7.5 %copy-start.66 = (bf16[64]{0:T(256)(128)(2,1)S(1)}, bf16[64]{0:T(256)(128)(2,1)}, u32[]{:S(2)}) copy-start(bf16[64]{0:T(256)(128)(2,1)} %param.26) | copy-start | bytes 388
  7.2 7.5 %copy-start.61 = (bf16[64]{0:T(256)(128)(2,1)S(1)}, bf16[64]{0:T(256)(128)(2,1)}, u32[]{:S(2)}) copy-start(bf16[64]{0:T(256)(128)(2,1)} %param.18) | copy-start | bytes 388
  7.2 7.5 %copy-start.62 = (bf16[64]{0:T(256)(128)(2,1)S(1)}, bf16[64]{0:T(256)(128)(2,1)}, u32[]{:S(2)}) copy-start(bf16[64]{0:T(256)(128)(2,1)} %param.19) | copy-start | bytes 388
  7.3 7.5 %copy-start.63 = (bf16[64]{0:T(256)(128)(2,1)S(1)}, bf16[64]{0:T(256)(128)(2,1)}, u32[]{:S(2)}) copy-start(bf16[64]{0:T(256)(128)(2,1)} %param.20) | copy-start | bytes 388
  7.3 7.5 %copy-start.64 = (bf16[64]{0:T(256)(128)(2,1)S(1)}, bf16[64]{0:T(256)(128)(2,1)}, u32[]{:S(2)}) copy-start(bf16[64]{0:T(256)(128)(2,1)} %param.21) | copy-start | bytes 388
  7.3 7.6 %copy-start.60 = (bf16[64,512]{1,0:T(8,128)(2,1)S(1)}, bf16[64,512]{1,0:T(8,128)(2,1)}, u32[]{:S(2)}) copy-start(bf16[64,512]{1,0:T(8,128)(2,1)} %param.22) | copy-start | bytes 196612
  7.3 180.0 %all-gather.3.cloned.1.call-start = ((), (), s32[]{:S(2)}) async-start(), calls=%async_computation | async-start | bytes 4456448 | tf_op jit(solution)/shard_map/all_gather | solution.py:712
  10.6 28.4 %collective-permute-start.8 = (bf16[1,144,1024]{2,1,0:T(8,128)(2,1)S(1)}, bf16[1,144,1024]{2,1,0:T(8,128)(2,1)S(1)}, u32[]{:S(2)}, u32[]{:S(2)}) collective-permute-start(bf16[1,144,1024]{2,1,0:T(8,128)(2,1)S(1)} %get-tuple-element.107), channel_id=1, source_target_pairs={{0,16},{2,18},{4,20},{6,22},{8,24},{10,26},{12,28},{14,30},{16,0},... | collective-permute-start | bytes 884744 | tf_op jit(solution)/shard_map/ppermute | solution.py:547
  14.9 21.6 %collective-permute-start = (bf16[1,49,1024]{2,1,0:T(8,128)(2,1)S(1)}, bf16[1,49,1024]{2,1,0:T(8,128)(2,1)S(1)}, u32[]{:S(2)}, u32[]{:S(2)}) collective-permute-start(bf16[1,49,1024]{2,1,0:T(8,128)(2,1)S(1)} %get-tuple-element.111), channel_id=1, source_target_pairs={{0,16},{2,18},{4,20},{6,22},{8,24},{10,26},{12,28},{14,30},{16,0},... | collective-permute-start | bytes 301064 | tf_op jit(solution)/shard_map/ppermute | solution.py:547
  36.6 9.3 %collective-permute-start.1 = (bf16[2,49,1024]{2,1,0:T(8,128)(2,1)S(1)}, bf16[2,49,1024]{2,1,0:T(8,128)(2,1)S(1)}, u32[]{:S(2)}, u32[]{:S(2)}) collective-permute-start(bf16[2,49,1024]{2,1,0:T(8,128)(2,1)S(1)} %maximum_select_fusion.22), channel_id=1, source_target_pairs={{0,8},{2,10},{4,12},{6,14},{8,0},{10,2},{12,4},{14,6},{16,24},{18,... | collective-permute-start | bytes 602120 | tf_op jit(solution)/shard_map/ppermute | solution.py:547
  39.1 29.6 %collective-permute-start.9 = (bf16[2,144,1024]{2,1,0:T(8,128)(2,1)S(1)}, bf16[2,144,1024]{2,1,0:T(8,128)(2,1)S(1)}, u32[]{:S(2)}, u32[]{:S(2)}) collective-permute-start(bf16[2,144,1024]{2,1,0:T(8,128)(2,1)S(1)} %maximum_select_fusion.13), channel_id=1, source_target_pairs={{0,8},{2,10},{4,12},{6,14},{8,0},{10,2},{12,4},{14,6},{16,24},{18,... | collective-permute-start | bytes 1769480 | tf_op jit(solution)/shard_map/ppermute | solution.py:547
  46.3 8.3 %collective-permute-start.2 = (bf16[4,17,1024]{2,0,1:T(4,128)(2,1)S(1)}, bf16[4,17,1024]{2,0,1:T(4,128)(2,1)S(1)}, u32[]{:S(2)}, u32[]{:S(2)}) collective-permute-start(bf16[4,17,1024]{2,0,1:T(4,128)(2,1)S(1)} %copy.111), channel_id=1, source_target_pairs={{0,2},{2,0},{4,6},{6,4},{8,10},{10,8},{12,14},{14,12},{16,18},{18,... | collective-permute-start | bytes 417800 | tf_op jit(solution)/shard_map/ppermute | solution.py:547
  48.0 23.4 %collective-permute-start.4 = (bf16[4,32,1024]{2,1,0:T(8,128)(2,1)S(1)}, bf16[4,32,1024]{2,1,0:T(8,128)(2,1)S(1)}, u32[]{:S(2)}, u32[]{:S(2)}) collective-permute-start(bf16[4,32,1024]{2,1,0:T(8,128)(2,1)S(1)} %get-tuple-element.104), channel_id=1, source_target_pairs={{0,4},{2,6},{4,0},{6,2},{8,12},{10,14},{12,8},{14,10},{16,20},{18,... | collective-permute-start | bytes 786440 | tf_op jit(solution)/shard_map/ppermute | solution.py:547
  54.8 19.0 %collective-permute-start.3 = (bf16[4,2,17,1024]{3,0,2,1:T(4,128)(2,1)S(1)}, bf16[4,2,17,1024]{3,0,2,1:T(4,128)(2,1)S(1)}, u32[]{:S(2)}, u32[]{:S(2)}) collective-permute-start(bf16[4,2,17,1024]{3,0,2,1:T(4,128)(2,1)S(1)} %maximum_select_fusion.20), channel_id=1, source_target_pairs={{0,4},{2,6},{4,0},{6,2},{8,12},{10,14},{12,8},{14,10},{16,20},{18,... | collective-permute-start | bytes 835592 | tf_op jit(solution)/shard_map/ppermute | solution.py:547
  70.0 27.9 %collective-permute-start.10 = (bf16[4,80,1024]{2,1,0:T(8,128)(2,1)}, bf16[4,80,1024]{2,1,0:T(8,128)(2,1)S(1)}, u32[]{:S(2)}, u32[]{:S(2)}) collective-permute-start(bf16[4,80,1024]{2,1,0:T(8,128)(2,1)} %get-tuple-element.79), channel_id=1, source_target_pairs={{0,2},{2,0},{4,6},{6,4},{8,10},{10,8},{12,14},{14,12},{16,18},{18,... | collective-permute-start | bytes 1966088 | tf_op jit(solution)/shard_map/ppermute | solution.py:547
  72.3 40.0 %collective-permute-start.5 = (bf16[4,2,32,1024]{3,2,0,1:T(8,128)(2,1)}, bf16[4,2,32,1024]{3,2,0,1:T(8,128)(2,1)}, u32[]{:S(2)}, u32[]{:S(2)}) collective-permute-start(bf16[4,2,32,1024]{3,2,0,1:T(8,128)(2,1)} %maximum_select_fusion.17), channel_id=1, source_target_pairs={{0,2},{2,0},{4,6},{6,4},{8,10},{10,8},{12,14},{14,12},{16,18},{18,... | collective-permute-start | bytes 1572872 | tf_op jit(solution)/shard_map/ppermute | solution.py:547
  79.5 32.8 %copy-start.53 = (bf16[4,2,1,32,1024]{4,3,0,2,1:T(8,128)(2,1)S(1)}, bf16[4,2,1,32,1024]{4,3,0,2,1:T(8,128)(2,1)}, u32[]{:S(2)}) copy-start(bf16[4,2,1,32,1024]{4,3,0,2,1:T(8,128)(2,1)} %maximum_select_fusion.18) | copy-start | bytes 1572868
  80.5 38.3 %collective-permute-start.7 = (bf16[16,32,512]{2,0,1:T(8,128)(2,1)}, bf16[16,32,512]{2,0,1:T(8,128)(2,1)}, u32[]{:S(2)}, u32[]{:S(2)}) collective-permute-start(bf16[16,32,512]{2,0,1:T(8,128)(2,1)} %get-tuple-element.101), channel_id=1, source_target_pairs={{0,1},{1,0},{2,3},{3,2},{4,5},{5,4},{6,7},{7,6},{8,9},{9,8},{10,11... | collective-permute-start | bytes 1572872 | tf_op jit(solution)/shard_map/ppermute | solution.py:604
  97.9 15.7 %copy-start.48 = (bf16[4,80,1024]{2,1,0:T(8,128)(2,1)}, bf16[4,80,1024]{2,1,0:T(8,128)(2,1)S(1)}, u32[]{:S(2)}) copy-start(bf16[4,80,1024]{2,1,0:T(8,128)(2,1)S(1)} %collective-permute-done.10) | copy-start | bytes 1966084
  99.2 40.6 %collective-permute-start.11 = (bf16[4,2,80,1024]{3,2,0,1:T(8,128)(2,1)}, bf16[4,2,80,1024]{3,2,0,1:T(8,128)(2,1)}, u32[]{:S(2)}, u32[]{:S(2)}) collective-permute-start(bf16[4,2,80,1024]{3,2,0,1:T(8,128)(2,1)} %maximum_select_fusion.3), channel_id=1, source_target_pairs={{0,4},{2,6},{4,0},{6,2},{8,12},{10,14},{12,8},{14,10},{16,20},{18,... | collective-permute-start | bytes 3932168 | tf_op jit(solution)/shard_map/ppermute | solution.py:547
  113.8 24.0 %collective-permute-start.6 = (bf16[16,32,1024]{2,1,0:T(8,128)(2,1)S(1)}, bf16[16,32,1024]{2,1,0:T(8,128)(2,1)}, u32[]{:S(2)}, u32[]{:S(2)}) collective-permute-start(bf16[16,32,1024]{2,1,0:T(8,128)(2,1)S(1)} %bitcast.289), channel_id=1, source_target_pairs={{0,1},{1,0},{2,3},{3,2},{4,5},{5,4},{6,7},{7,6},{8,9},{9,8},{10,11... | collective-permute-start | bytes 3145736 | tf_op jit(solution)/shard_map/ppermute | solution.py:604
  115.2 18.8 %collective-permute-start.15 = (bf16[4,64,1024]{2,1,0:T(8,128)(2,1)}, bf16[4,64,1024]{2,1,0:T(8,128)(2,1)S(1)}, u32[]{:S(2)}, u32[]{:S(2)}) collective-permute-start(bf16[4,64,1024]{2,1,0:T(8,128)(2,1)} %get-tuple-element.76), channel_id=1, source_target_pairs={{0,4},{2,6},{4,0},{6,2},{8,12},{10,14},{12,8},{14,10},{16,20},{18,... | collective-permute-start | bytes 1572872 | tf_op jit(solution)/shard_map/ppermute | solution.py:547
  117.7 56.7 %collective-permute-start.14 = (bf16[512,1024]{1,0:T(8,128)(2,1)}, bf16[512,1024]{1,0:T(8,128)(2,1)}, u32[]{:S(2)}, u32[]{:S(2)}) collective-permute-start(bf16[512,1024]{1,0:T(8,128)(2,1)} %bitcast.55), channel_id=1, source_target_pairs={{0,1},{1,0},{2,3},{3,2},{4,5},{5,4},{6,7},{7,6},{8,9},{9,8},{10,11... | collective-permute-start | bytes 3145736 | tf_op jit(solution)/shard_map/ppermute | solution.py:604
  118.9 15.1 %copy-start.55 = (bf16[4,1,64,1024]{3,2,0,1:T(8,128)(2,1)S(1)}, bf16[4,1,64,1024]{3,2,0,1:T(8,128)(2,1)}, u32[]{:S(2)}) copy-start(bf16[4,1,64,1024]{3,2,0,1:T(8,128)(2,1)} %get-tuple-element.74) | copy-start | bytes 1572868
  120.3 17.3 %copy-start.49 = (bf16[4,80,1024]{2,1,0:T(8,128)(2,1)S(1)}, bf16[4,80,1024]{2,1,0:T(8,128)(2,1)}, u32[]{:S(2)}) copy-start(bf16[4,80,1024]{2,1,0:T(8,128)(2,1)} %copy-done.48) | copy-start | bytes 1966084
  120.9 23.4 %copy-start.8 = (bf16[16,2,32,512]{3,2,1,0:T(8,128)(2,1)}, bf16[16,2,32,512]{3,2,1,0:T(8,128)(2,1)S(1)}, u32[]{:S(2)}) copy-start(bf16[16,2,32,512]{3,2,1,0:T(8,128)(2,1)S(1)} %copy.89) | copy-start | bytes 3145732
  134.0 10.3 %slice-start = ((s8[9437184]{0:T(1024)(128)(4,1)}), s8[4194304]{0:T(1024)(128)(4,1)S(1)}, s32[]{:S(2)}) async-start(s8[9437184]{0:T(1024)(128)(4,1)} %bitcast.274), calls=%async_computation.1 | async-start | bytes 8388608
  135.2 42.4 %collective-permute-start.16 = (bf16[4,2,64,1024]{3,2,0,1:T(8,128)(2,1)}, bf16[4,2,64,1024]{3,2,0,1:T(8,128)(2,1)}, u32[]{:S(2)}, u32[]{:S(2)}) collective-permute-start(bf16[4,2,64,1024]{3,2,0,1:T(8,128)(2,1)} %maximum_select_fusion.9), channel_id=1, source_target_pairs={{0,2},{2,0},{4,6},{6,4},{8,10},{10,8},{12,14},{14,12},{16,18},{18,... | collective-permute-start | bytes 3145736 | tf_op jit(solution)/shard_map/ppermute | solution.py:547
  143.0 28.2 %collective-permute-start.12 = (bf16[16,16,1024]{2,1,0:T(8,128)(2,1)S(1)}, bf16[16,16,1024]{2,1,0:T(8,128)(2,1)S(1)}, u32[]{:S(2)}, u32[]{:S(2)}) collective-permute-start(bf16[16,16,1024]{2,1,0:T(8,128)(2,1)S(1)} %get-tuple-element.69), channel_id=1, source_target_pairs={{0,1},{1,0},{2,3},{3,2},{4,5},{5,4},{6,7},{7,6},{8,9},{9,8},{10,11... | collective-permute-start | bytes 1572872 | tf_op jit(solution)/shard_map/ppermute | solution.py:604
  174.3 10.3 %collective-permute-start.13 = (bf16[512,1024]{1,0:T(8,128)(2,1)}, bf16[512,1024]{1,0:T(8,128)(2,1)}, u32[]{:S(2)}, u32[]{:S(2)}) collective-permute-start(bf16[512,1024]{1,0:T(8,128)(2,1)} %get-tuple-element.41), channel_id=1, source_target_pairs={{0,1},{1,0},{2,3},{3,2},{4,5},{5,4},{6,7},{7,6},{8,9},{9,8},{10,11... | collective-permute-start | bytes 3145736 | tf_op jit(solution)/shard_map/ppermute | solution.py:604
  214.3 24.8 %copy-start.33 = (bf16[16,64,1024]{2,1,0:T(8,128)(2,1)}, bf16[16,64,1024]{2,1,0:T(8,128)(2,1)S(1)}, u32[]{:S(2)}) copy-start(bf16[16,64,1024]{2,1,0:T(8,128)(2,1)S(1)} %get-tuple-element.64) | copy-start | bytes 6291460
  215.5 35.0 %collective-permute-start.36 = (bf16[4,2,64,1024]{3,2,1,0:T(8,128)(2,1)}, bf16[4,2,64,1024]{3,2,1,0:T(8,128)(2,1)}, u32[]{:S(2)}, u32[]{:S(2)}) collective-permute-start(bf16[4,2,64,1024]{3,2,1,0:T(8,128)(2,1)} %dynamic-slice_bitcast_fusion), channel_id=1, source_target_pairs={{0,2},{2,0},{4,6},{6,4},{8,10},{10,8},{12,14},{14,12},{16,18},{18,... | collective-permute-start | bytes 3145736 | tf_op jit(solution)/shard_map/ppermute | solution.py:547
  218.1 35.7 %collective-permute-start.38 = (bf16[4,2,64,1024]{3,2,0,1:T(8,128)(2,1)}, bf16[4,2,64,1024]{3,2,0,1:T(8,128)(2,1)}, u32[]{:S(2)}, u32[]{:S(2)}) collective-permute-start(bf16[4,2,64,1024]{3,2,0,1:T(8,128)(2,1)} %bitcast.244), channel_id=1, source_target_pairs={{0,4},{2,6},{4,0},{6,2},{8,12},{10,14},{12,8},{14,10},{16,20},{18,... | collective-permute-start | bytes 3145736 | tf_op jit(solution)/shard_map/ppermute | solution.py:547
  246.9 25.3 %collective-permute-start.29 = (bf16[4,2,64,1024]{3,2,0,1:T(8,128)(2,1)}, bf16[4,2,64,1024]{3,2,0,1:T(8,128)(2,1)}, u32[]{:S(2)}, u32[]{:S(2)}) collective-permute-start(bf16[4,2,64,1024]{3,2,0,1:T(8,128)(2,1)} %bitcast.245), channel_id=1, source_target_pairs={{0,2},{2,0},{4,6},{6,4},{8,10},{10,8},{12,14},{14,12},{16,18},{18,... | collective-permute-start | bytes 3145736 | tf_op jit(solution)/shard_map/ppermute | solution.py:547
  250.1 26.6 %collective-permute-start.31 = (bf16[4,2,64,1024]{3,2,1,0:T(8,128)(2,1)S(1)}, bf16[4,2,64,1024]{3,2,1,0:T(8,128)(2,1)S(1)}, u32[]{:S(2)}, u32[]{:S(2)}) collective-permute-start(bf16[4,2,64,1024]{3,2,1,0:T(8,128)(2,1)S(1)} %dynamic-slice_bitcast_fusion.1), channel_id=1, source_target_pairs={{0,4},{2,6},{4,0},{6,2},{8,12},{10,14},{12,8},{14,10},{16,20},{18,... | collective-permute-start | bytes 3145736 | tf_op jit(solution)/shard_map/ppermute | solution.py:547
  250.4 27.8 %collective-permute-start.18 = (bf16[512,1024]{1,0:T(8,128)(2,1)S(1)}, bf16[512,1024]{1,0:T(8,128)(2,1)S(1)}, u32[]{:S(2)}, u32[]{:S(2)}) collective-permute-start(bf16[512,1024]{1,0:T(8,128)(2,1)S(1)} %copy-done.26), channel_id=1, source_target_pairs={{0,1},{1,0},{2,3},{3,2},{4,5},{5,4},{6,7},{7,6},{8,9},{9,8},{10,11... | collective-permute-start | bytes 3145736 | tf_op jit(solution)/shard_map/ppermute | solution.py:604
  250.5 114.6 %collective-permute-start.17 = (bf16[512,1024]{1,0:T(8,128)(2,1)}, bf16[512,1024]{1,0:T(8,128)(2,1)}, u32[]{:S(2)}, u32[]{:S(2)}) collective-permute-start(bf16[512,1024]{1,0:T(8,128)(2,1)} %get-tuple-element.43), channel_id=1, source_target_pairs={{0,1},{1,0},{2,3},{3,2},{4,5},{5,4},{6,7},{7,6},{8,9},{9,8},{10,11... | collective-permute-start | bytes 3145736 | tf_op jit(solution)/shard_map/ppermute | solution.py:604
  253.8 115.4 %collective-permute-start.37 = (bf16[4,64,1024]{2,1,0:T(8,128)(2,1)}, bf16[4,64,1024]{2,1,0:T(8,128)(2,1)}, u32[]{:S(2)}, u32[]{:S(2)}) collective-permute-start(bf16[4,64,1024]{2,1,0:T(8,128)(2,1)} %dynamic-slice_bitcast_fusion.6), channel_id=1, source_target_pairs={{0,4},{2,6},{4,0},{6,2},{8,12},{10,14},{12,8},{14,10},{16,20},{18,... | collective-permute-start | bytes 1572872 | tf_op jit(solution)/shard_map/ppermute | solution.py:547
  255.6 18.4 %copy-start.35 = (bf16[4,2,1,64,1024]{4,3,2,1,0:T(8,128)(2,1)S(1)}, bf16[4,2,1,64,1024]{4,3,2,1,0:T(8,128)(2,1)}, u32[]{:S(2)}) copy-start(bf16[4,2,1,64,1024]{4,3,2,1,0:T(8,128)(2,1)} %get-tuple-element.72) | copy-start | bytes 3145732
  257.3 16.7 %copy-start.38 = (bf16[4,2,64,1024]{3,2,0,1:T(8,128)(2,1)}, bf16[4,2,64,1024]{3,2,0,1:T(8,128)(2,1)S(1)}, u32[]{:S(2)}) copy-start(bf16[4,2,64,1024]{3,2,0,1:T(8,128)(2,1)S(1)} %fusion.1) | copy-start | bytes 3145732
  272.2 98.3 %collective-permute-start.39 = (bf16[4,64,1024]{2,1,0:T(8,128)(2,1)}, bf16[4,64,1024]{2,1,0:T(8,128)(2,1)}, u32[]{:S(2)}, u32[]{:S(2)}) collective-permute-start(bf16[4,64,1024]{2,1,0:T(8,128)(2,1)} %dynamic-slice_bitcast_fusion.5), channel_id=1, source_target_pairs={{0,2},{2,0},{4,6},{6,4},{8,10},{10,8},{12,14},{14,12},{16,18},{18,... | collective-permute-start | bytes 1572872 | tf_op jit(solution)/shard_map/ppermute | solution.py:547
  276.6 96.7 %collective-permute-start.30 = (bf16[4,64,1024]{2,1,0:T(8,128)(2,1)}, bf16[4,64,1024]{2,1,0:T(8,128)(2,1)}, u32[]{:S(2)}, u32[]{:S(2)}) collective-permute-start(bf16[4,64,1024]{2,1,0:T(8,128)(2,1)} %dynamic-slice_bitcast_fusion.9), channel_id=1, source_target_pairs={{0,4},{2,6},{4,0},{6,2},{8,12},{10,14},{12,8},{14,10},{16,20},{18,... | collective-permute-start | bytes 1572872 | tf_op jit(solution)/shard_map/ppermute | solution.py:547
  278.3 96.3 %collective-permute-start.32 = (bf16[4,64,1024]{2,1,0:T(8,128)(2,1)}, bf16[4,64,1024]{2,1,0:T(8,128)(2,1)}, u32[]{:S(2)}, u32[]{:S(2)}) collective-permute-start(bf16[4,64,1024]{2,1,0:T(8,128)(2,1)} %dynamic-slice_bitcast_fusion.8), channel_id=1, source_target_pairs={{0,2},{2,0},{4,6},{6,4},{8,10},{10,8},{12,14},{14,12},{16,18},{18,... | collective-permute-start | bytes 1572872 | tf_op jit(solution)/shard_map/ppermute | solution.py:547
  285.7 37.5 %copy-start.9 = (bf16[16,2,32,512]{3,2,1,0:T(8,128)(2,1)S(1)}, bf16[16,2,32,512]{3,2,1,0:T(8,128)(2,1)}, u32[]{:S(2)}) copy-start(bf16[16,2,32,512]{3,2,1,0:T(8,128)(2,1)} %copy-done.8) | copy-start | bytes 3145732
  285.7 37.5 %copy-start.19 = (bf16[8,64,1024]{2,1,0:T(8,128)(2,1)S(1)}, bf16[8,64,1024]{2,1,0:T(8,128)(2,1)}, u32[]{:S(2)}) copy-start(bf16[8,64,1024]{2,1,0:T(8,128)(2,1)} %latent.3) | copy-start | bytes 3145732
  345.2 18.8 %copy-start.15 = (bf16[1024,1024]{1,0:T(8,128)(2,1)S(1)}, bf16[1024,1024]{1,0:T(8,128)(2,1)}, u32[]{:S(2)}) copy-start(bf16[1024,1024]{1,0:T(8,128)(2,1)} %copy-done.14) | copy-start | bytes 6291460
  365.1 20.1 %collective-permute-start.19 = (bf16[16,32,1024]{2,1,0:T(8,128)(2,1)}, bf16[16,32,1024]{2,1,0:T(8,128)(2,1)}, u32[]{:S(2)}, u32[]{:S(2)}) collective-permute-start(bf16[16,32,1024]{2,1,0:T(8,128)(2,1)} %dynamic-slice_bitcast_fusion.2), channel_id=1, source_target_pairs={{0,1},{1,0},{2,3},{3,2},{4,5},{5,4},{6,7},{7,6},{8,9},{9,8},{10,11... | collective-permute-start | bytes 3145736 | tf_op jit(solution)/shard_map/ppermute | solution.py:604
  369.3 9.6 %collective-permute-start.22 = (bf16[16,32,512]{2,0,1:T(8,128)(2,1)S(1)}, bf16[16,32,512]{2,0,1:T(8,128)(2,1)S(1)}, u32[]{:S(2)}, u32[]{:S(2)}) collective-permute-start(bf16[16,32,512]{2,0,1:T(8,128)(2,1)S(1)} %bitcast.322), channel_id=1, source_target_pairs={{0,1},{1,0},{2,3},{3,2},{4,5},{5,4},{6,7},{7,6},{8,9},{9,8},{10,11... | collective-permute-start | bytes 1572872 | tf_op jit(solution)/shard_map/ppermute | solution.py:604
  370.6 8.7 %collective-permute-start.23 = (bf16[16,16,1024]{2,0,1:T(8,128)(2,1)S(1)}, bf16[16,16,1024]{2,0,1:T(8,128)(2,1)S(1)}, u32[]{:S(2)}, u32[]{:S(2)}) collective-permute-start(bf16[16,16,1024]{2,0,1:T(8,128)(2,1)S(1)} %bitcast.321), channel_id=1, source_target_pairs={{0,1},{1,0},{2,3},{3,2},{4,5},{5,4},{6,7},{7,6},{8,9},{9,8},{10,11... | collective-permute-start | bytes 1572872 | tf_op jit(solution)/shard_map/ppermute | solution.py:604
  373.3 15.3 %collective-permute-start.40 = (bf16[2,128,1024]{2,1,0:T(8,128)(2,1)}, bf16[2,128,1024]{2,1,0:T(8,128)(2,1)}, u32[]{:S(2)}, u32[]{:S(2)}) collective-permute-start(bf16[2,128,1024]{2,1,0:T(8,128)(2,1)} %dynamic-slice_bitcast_fusion.4), channel_id=1, source_target_pairs={{0,8},{2,10},{4,12},{6,14},{8,0},{10,2},{12,4},{14,6},{16,24},{18,... | collective-permute-start | bytes 1572872 | tf_op jit(solution)/shard_map/ppermute | solution.py:547
  376.8 27.6 %collective-permute-start.33 = (bf16[2,128,1024]{2,1,0:T(8,128)(2,1)}, bf16[2,128,1024]{2,1,0:T(8,128)(2,1)}, u32[]{:S(2)}, u32[]{:S(2)}) collective-permute-start(bf16[2,128,1024]{2,1,0:T(8,128)(2,1)} %dynamic-slice_bitcast_fusion.7), channel_id=1, source_target_pairs={{0,8},{2,10},{4,12},{6,14},{8,0},{10,2},{12,4},{14,6},{16,24},{18,... | collective-permute-start | bytes 1572872 | tf_op jit(solution)/shard_map/ppermute | solution.py:547
  384.3 25.6 %collective-permute-start.24 = (bf16[4,2,33,1024]{3,1,0,2:T(2,128)(2,1)S(1)}, bf16[4,2,33,1024]{3,1,0,2:T(2,128)(2,1)S(1)}, u32[]{:S(2)}, u32[]{:S(2)}) collective-permute-start(bf16[4,2,33,1024]{3,1,0,2:T(2,128)(2,1)S(1)} %dynamic-slice_bitcast_fusion.3), channel_id=1, source_target_pairs={{0,4},{2,6},{4,0},{6,2},{8,12},{10,14},{12,8},{14,10},{16,20},{18,... | collective-permute-start | bytes 1622024 | tf_op jit(solution)/shard_map/ppermute | solution.py:547
  386.8 17.6 %copy-start.47 = (bf16[4,128,1024]{2,1,0:T(8,128)(2,1)S(1)}, bf16[4,128,1024]{2,1,0:T(8,128)(2,1)}, u32[]{:S(2)}) copy-start(bf16[4,128,1024]{2,1,0:T(8,128)(2,1)} %copy-done.46) | copy-start | bytes 3145732
  386.8 33.1 %collective-permute-start.20 = (bf16[4,2,32,1024]{3,2,1,0:T(8,128)(2,1)S(1)}, bf16[4,2,32,1024]{3,2,1,0:T(8,128)(2,1)S(1)}, u32[]{:S(2)}, u32[]{:S(2)}) collective-permute-start(bf16[4,2,32,1024]{3,2,1,0:T(8,128)(2,1)S(1)} %dynamic-slice_bitcast_fusion.10), channel_id=1, source_target_pairs={{0,2},{2,0},{4,6},{6,4},{8,10},{10,8},{12,14},{14,12},{16,18},{18,... | collective-permute-start | bytes 1572872 | tf_op jit(solution)/shard_map/ppermute | solution.py:547
  389.9 40.7 %collective-permute-start.41 = (bf16[1,128,1024]{2,1,0:T(8,128)(2,1)S(1)}, bf16[1,128,1024]{2,1,0:T(8,128)(2,1)}, u32[]{:S(2)}, u32[]{:S(2)}) collective-permute-start(bf16[1,128,1024]{2,1,0:T(8,128)(2,1)S(1)} %constant_dynamic-slice_fusion), channel_id=1, source_target_pairs={{0,16},{2,18},{4,20},{6,22},{8,24},{10,26},{12,28},{14,30},{16,0},... | collective-permute-start | bytes 786440 | tf_op jit(solution)/shard_map/ppermute | solution.py:547
  405.7 14.2 %collective-permute-start.34 = (bf16[1,128,1024]{2,1,0:T(8,128)(2,1)S(1)}, bf16[1,128,1024]{2,1,0:T(8,128)(2,1)S(1)}, u32[]{:S(2)}, u32[]{:S(2)}) collective-permute-start(bf16[1,128,1024]{2,1,0:T(8,128)(2,1)S(1)} %constant_dynamic-slice_fusion.3), channel_id=1, source_target_pairs={{0,16},{2,18},{4,20},{6,22},{8,24},{10,26},{12,28},{14,30},{16,0},... | collective-permute-start | bytes 786440 | tf_op jit(solution)/shard_map/ppermute | solution.py:547
  412.3 8.8 %collective-permute-start.25 = (bf16[4,33,1024]{2,0,1:T(4,128)(2,1)S(1)}, bf16[4,33,1024]{2,0,1:T(4,128)(2,1)S(1)}, u32[]{:S(2)}, u32[]{:S(2)}) collective-permute-start(bf16[4,33,1024]{2,0,1:T(4,128)(2,1)S(1)} %bitcast.325), channel_id=1, source_target_pairs={{0,2},{2,0},{4,6},{6,4},{8,10},{10,8},{12,14},{14,12},{16,18},{18,... | collective-permute-start | bytes 811016 | tf_op jit(solution)/shard_map/ppermute | solution.py:547
  420.2 8.1 %collective-permute-start.21 = (bf16[4,32,1024]{2,1,0:T(8,128)(2,1)S(1)}, bf16[4,32,1024]{2,1,0:T(8,128)(2,1)S(1)}, u32[]{:S(2)}, u32[]{:S(2)}) collective-permute-start(bf16[4,32,1024]{2,1,0:T(8,128)(2,1)S(1)} %dynamic-slice_bitcast_fusion.11), channel_id=1, source_target_pairs={{0,4},{2,6},{4,0},{6,2},{8,12},{10,14},{12,8},{14,10},{16,20},{18,... | collective-permute-start | bytes 786440 | tf_op jit(solution)/shard_map/ppermute | solution.py:547
  430.4 7.4 %collective-permute-start.26 = (bf16[2,65,1024]{2,0,1:T(2,128)(2,1)S(1)}, bf16[2,65,1024]{2,0,1:T(2,128)(2,1)S(1)}, u32[]{:S(2)}, u32[]{:S(2)}) collective-permute-start(bf16[2,65,1024]{2,0,1:T(2,128)(2,1)S(1)} %bitcast.326), channel_id=1, source_target_pairs={{0,8},{2,10},{4,12},{6,14},{8,0},{10,2},{12,4},{14,6},{16,24},{18,... | collective-permute-start | bytes 798728 | tf_op jit(solution)/shard_map/ppermute | solution.py:547
  430.5 8.9 %collective-permute-start.35 = (f32[64,2048]{1,0:T(8,128)S(1)}, f32[64,2048]{1,0:T(8,128)}, u32[]{:S(2)}, u32[]{:S(2)}) collective-permute-start(f32[64,2048]{1,0:T(8,128)S(1)} %pad_maximum_fusion.6), channel_id=1, source_target_pairs={{0,1},{1,0},{2,3},{3,2},{4,5},{5,4},{6,7},{7,6},{8,9},{9,8},{10,11... | collective-permute-start | bytes 1572872 | tf_op jit(solution)/shard_map/ppermute | solution.py:604
  438.5 13.2 %collective-permute-start.27 = (bf16[1,65,1024]{2,0,1:T(2,128)(2,1)S(1)}, bf16[1,65,1024]{2,0,1:T(2,128)(2,1)}, u32[]{:S(2)}, u32[]{:S(2)}) collective-permute-start(bf16[1,65,1024]{2,0,1:T(2,128)(2,1)S(1)} %constant_dynamic-slice_fusion.6), channel_id=1, source_target_pairs={{0,16},{2,18},{4,20},{6,22},{8,24},{10,26},{12,28},{14,30},{16,0},... | collective-permute-start | bytes 399368 | tf_op jit(solution)/shard_map/ppermute | solution.py:547
  439.4 17.9 %collective-permute-start.42 = (f32[128,1024]{1,0:T(8,128)S(1)}, f32[128,1024]{1,0:T(8,128)}, u32[]{:S(2)}, u32[]{:S(2)}) collective-permute-start(f32[128,1024]{1,0:T(8,128)S(1)} %get-tuple-element.93), channel_id=1, source_target_pairs={{0,1},{1,0},{2,3},{3,2},{4,5},{5,4},{6,7},{7,6},{8,9},{9,8},{10,11... | collective-permute-start | bytes 1572872 | tf_op jit(solution)/shard_map/ppermute | solution.py:604
  453.9 5.7 %collective-permute-start.28 = (f32[65,1024]{1,0:T(8,128)}, f32[65,1024]{1,0:T(8,128)}, u32[]{:S(2)}, u32[]{:S(2)}) collective-permute-start(f32[65,1024]{1,0:T(8,128)} %get-tuple-element.106), channel_id=1, source_target_pairs={{0,1},{1,0},{2,3},{3,2},{4,5},{5,4},{6,7},{7,6},{8,9},{9,8},{10,11... | collective-permute-start | bytes 798728 | tf_op jit(solution)/shard_map/ppermute | solution.py:604
  (50 other events, 169.9 us)
Sparse Core Ops, SparseCore 0:
  15.9 103.4 all-gather.2
